TPU v7x, 128 devices: a whole 4x4x4 slice. The times are simulated.
128 devices in a mesh: seq: 32 (over z, y, core), head: 4 (over x).
Axes of the slice: x: 4, y: 4, z: 4, core: 2. Of those that a mesh axis runs over, the one named last changes fastest.
Arguments:
- queries: bfloat16 [32768, 2048], P('seq', 'head'), may hold values from -100 to 100
- values: bfloat16 [32768, 2048], P('seq', 'head'), may hold values from -6 to 6
- codes: int32 [32768, 16], P('seq', 'head'), may hold values from 0 to 511
- codebook: bfloat16 [16, 512, 128], P('head'), may hold values from -4 to 4
- out_weight: bfloat16 [2048, 2048], P('head'), may hold values from -0.125 to 0.125
- grad_out: bfloat16 [32768, 2048], P('seq', 'head'), may hold values from -6 to 6
Outputs:
- grad_queries: bfloat16 [32768, 2048], P('seq', 'head')
- grad_values: bfloat16 [32768, 2048], P('seq', 'head')
- grad_codebook: float32 [16, 512, 128], P('head')
All inputs are finite; a program needn't handle non-finite values.
Results may differ from a plain program's by a relative error of at most 0.012.
The roundings to bfloat16 on the way count: a program that leaves them out, or rounds other values in their place, can miss the bound.
Values may be sent and summed in bfloat16 or wider, within the bound.
No kernel may reach another device: no remote copies, remote signals or barrier semaphores. Data moves between devices by JAX's collectives and lax.ppermute only.
A program may use at most 192 MiB of HBM per device.

v0:
```python
from functools import reduce

import jax
import jax.numpy as jnp
from jax import lax
from jax.sharding import Mesh
from jax.sharding import PartitionSpec as P

BLOCK = 512
SEQ = ("seq_0", "seq_1", "seq_2")


def nothing_yet(array, identity):
    return jax.tree.map(
        lambda a, e: jnp.broadcast_to(jnp.asarray(e, a.dtype), a.shape), array, identity
    )


def carried_in(array, axes, combine, identity, reverse):
    before = start = nothing_yet(array, identity)
    subtotal = array
    for axis in reversed(axes):
        count, here = (lax.axis_size(axis), lax.axis_index(axis))
        pieces = jax.tree.map(lambda part: lax.all_gather(part, axis), subtotal)
        inside, subtotal = (start, start)
        for k in reversed(range(count)) if reverse else range(count):
            passed = k > here if reverse else k < here
            subtotal = combine(subtotal, jax.tree.map(lambda part: part[k], pieces))
            inside = jax.tree.map(lambda new, old: jnp.where(passed, new, old), subtotal, inside)
        before = combine(inside, before)
    return before


def split_up(array, dim, count):
    before, after = (array.shape[:dim], array.shape[dim + 1 :])
    return jnp.moveaxis(array.reshape(*before, count, -1, *after), dim, 0)


def sent_and_summed(array, axis, dim):
    count = lax.axis_size(axis)
    tiles = lax.all_to_all(split_up(array, dim, count), axis, 0, 0, tiled=True)
    return jnp.sum(tiles, axis=0)


def sum_by_axis(array, axes, dim):
    far, near = axes
    own = sent_and_summed(split_up(array, dim, lax.axis_size(far)), near, dim + 1)
    return jnp.sum(lax.all_to_all(own, far, 0, 0, tiled=True), axis=0)


def rows_for(lines, count):
    spare = -len(lines) % count
    return jnp.pad(lines, [(0, spare)] + [(0, 0)] * (lines.ndim - 1))


def sent_to_all(array, axis):
    count = lax.axis_size(axis)
    return lax.all_to_all(
        jnp.broadcast_to(array[None], (count, *array.shape)), axis, 0, 0, tiled=True
    )


def in_order(tiles, dim):
    dims = list(tiles.shape[1:])
    dims[dim] *= tiles.shape[0]
    return jnp.moveaxis(tiles, 0, dim).reshape(dims)


def gather_axes(array, axes, dim):
    far, near = axes
    tiles = sent_to_all(sent_to_all(array, far), near)
    return in_order(tiles.swapaxes(0, 1).reshape(-1, *array.shape), dim)


def sum_by_parts(array, axes):
    lines = array.reshape(-1, array.shape[-1])
    own = sum_by_axis(rows_for(lines, lax.axis_size(axes[0]) * lax.axis_size(axes[1])), axes, 0)
    whole = gather_axes(own, axes, 0)
    return whole[: len(lines)].reshape(array.shape)


def add_tree(earlier, later):
    return jax.tree.map(jnp.add, earlier, later)


def attend_block(query, value, onehot, dout, codebook, prefix_values, prefix_counts):
    block_rows, heads_here, head_width = query.shape
    scale = head_width ** (-0.5)
    keys = jnp.einsum("ths,hse->the", onehot, codebook, preferred_element_type=jnp.float32).astype(
        jnp.bfloat16
    )
    scores = jnp.einsum("the,uhe->htu", query, keys, preferred_element_type=jnp.float32) * scale
    positions = lax.iota(jnp.int32, block_rows)
    causal = positions[:, None] >= positions[None, :]
    cache_scores = (
        jnp.einsum("the,hce->htc", query, codebook, preferred_element_type=jnp.float32) * scale
    )
    counts_row = prefix_counts[:, None, :]
    present = counts_row > 0.0
    highest = jnp.maximum(
        jnp.max(jnp.where(causal, scores, -jnp.inf), axis=-1, keepdims=True),
        jnp.max(jnp.where(present, cache_scores, -jnp.inf), axis=-1, keepdims=True),
    )
    local_exp = jnp.where(causal, jnp.exp(jnp.where(causal, scores - highest, 0.0)), 0.0)
    cache_exp = jnp.where(present, jnp.exp(jnp.where(present, cache_scores - highest, 0.0)), 0.0)
    total = jnp.sum(local_exp, axis=-1, keepdims=True) + jnp.sum(
        cache_exp * counts_row, axis=-1, keepdims=True
    )
    local_prob = local_exp / total
    cache_prob = cache_exp / total
    local_low = local_prob.astype(jnp.bfloat16)
    cache_low = cache_prob.astype(jnp.bfloat16)
    cache_values = prefix_values.astype(jnp.bfloat16)
    attended = jnp.einsum(
        "htu,uhe->hte", local_low, value, preferred_element_type=jnp.float32
    ) + jnp.einsum("htc,hce->hte", cache_low, cache_values, preferred_element_type=jnp.float32)
    delta = jnp.sum(jnp.transpose(dout.astype(jnp.float32), (1, 0, 2)) * attended, axis=-1)[
        ..., None
    ]
    local_grad = jnp.einsum("the,uhe->htu", dout, value, preferred_element_type=jnp.float32)
    local_score_grad = (local_prob * (local_grad - delta) * scale).astype(jnp.bfloat16)
    cache_grad = jnp.einsum("the,hce->htc", dout, cache_values, preferred_element_type=jnp.float32)
    cache_score_grad = (cache_prob * (cache_grad - delta * counts_row) * scale).astype(jnp.bfloat16)
    grad_query = (
        jnp.einsum("htu,uhe->the", local_score_grad, keys, preferred_element_type=jnp.float32)
        + jnp.einsum("htc,hce->the", cache_score_grad, codebook, preferred_element_type=jnp.float32)
    ).astype(jnp.bfloat16)
    key_grad = jnp.einsum(
        "htu,the->uhe", local_score_grad, query, preferred_element_type=jnp.float32
    ).astype(jnp.bfloat16)
    grad_code = jnp.einsum(
        "ths,the->hse", onehot, key_grad, preferred_element_type=jnp.float32
    ) + jnp.einsum("htc,the->hce", cache_score_grad, query, preferred_element_type=jnp.float32)
    value_part = jnp.einsum("htc,the->hce", cache_low, dout, preferred_element_type=jnp.float32)
    local_values = jnp.einsum("htu,the->uhe", local_low, dout, preferred_element_type=jnp.float32)
    return (grad_query, local_values, grad_code, value_part)


def per_device(queries, values, codes, codebook, out_weight, grad_out):
    row_count = queries.shape[0]
    heads_here, entries, head_width = codebook.shape
    grad_heads = jnp.einsum(
        "tn,hn->th",
        lax.all_gather(grad_out, "head", axis=1, tiled=True),
        out_weight,
        preferred_element_type=jnp.float32,
    )
    grad_heads = grad_heads.astype(jnp.bfloat16).reshape(row_count, heads_here, head_width)
    query_rows = queries.reshape(row_count, heads_here, head_width)
    value_rows = values.reshape(row_count, heads_here, head_width)
    levels = lax.iota(jnp.int32, entries)
    onehot = (codes[:, :, None] == levels[None, None, :]).astype(jnp.bfloat16)
    nblocks = row_count // BLOCK
    spans = [(index * BLOCK, (index + 1) * BLOCK) for index in range(nblocks)]
    own_values = [
        jnp.einsum(
            "ths,the->hse",
            onehot[lower:upper],
            value_rows[lower:upper],
            preferred_element_type=jnp.float32,
        )
        for lower, upper in spans
    ]
    own_counts = [
        jnp.sum(onehot[lower:upper].astype(jnp.float32), axis=0) for lower, upper in spans
    ]
    device_values = reduce(jnp.add, own_values)
    device_counts = reduce(jnp.add, own_counts)
    zero_values = jnp.zeros((heads_here, entries, head_width), jnp.float32)
    zero_counts = jnp.zeros((heads_here, entries), jnp.float32)
    prefix_values, prefix_counts = carried_in(
        (device_values, device_counts), SEQ, add_tree, (zero_values, zero_counts), False
    )
    grad_queries = []
    local_parts = []
    value_parts = []
    code_total = zero_values
    for index in range(nblocks):
        lower, upper = spans[index]
        grad_query, local_values, grad_code, value_part = attend_block(
            query_rows[lower:upper],
            value_rows[lower:upper],
            onehot[lower:upper],
            grad_heads[lower:upper],
            codebook,
            prefix_values,
            prefix_counts,
        )
        grad_queries.append(grad_query)
        local_parts.append(local_values)
        value_parts.append(value_part)
        code_total = code_total + grad_code
        prefix_values = prefix_values + own_values[index]
        prefix_counts = prefix_counts + own_counts[index]
    device_grads = reduce(jnp.add, value_parts)
    later = carried_in(device_grads, SEQ, add_tree, zero_values, True)
    grad_values = [None] * nblocks
    for index in reversed(range(nblocks)):
        lower, upper = spans[index]
        lookup = jnp.einsum(
            "ths,hse->the",
            onehot[lower:upper],
            later.astype(jnp.bfloat16),
            preferred_element_type=jnp.float32,
        )
        grad_values[index] = (local_parts[index] + lookup).astype(jnp.bfloat16)
        later = later + value_parts[index]
    grad_codebook = sum_by_parts(code_total, (("seq_0", "seq_1"), "seq_2"))
    grad_query_all = jnp.concatenate(grad_queries, axis=0).reshape(
        row_count, heads_here * head_width
    )
    grad_value_all = jnp.concatenate(grad_values, axis=0).reshape(
        row_count, heads_here * head_width
    )
    return (grad_query_all, grad_value_all, grad_codebook)


def solution(mesh):
    finer = Mesh(
        mesh.devices.reshape(4, 4, 2, mesh.shape["head"]), ("seq_0", "seq_1", "seq_2", "head")
    )
    placed = (
        P(SEQ, "head"),
        P(SEQ, "head"),
        P(SEQ, "head"),
        P("head", None, None),
        P("head", None),
        P(SEQ, "head"),
    )
    return jax.shard_map(
        per_device,
        mesh=finer,
        in_specs=placed,
        out_specs=(P(SEQ, "head"), P(SEQ, "head"), P("head", None, None)),
        check_vma=False,
    )
```

profile of v0, /device:TPU:1, one launch (start us, length us, event | category | flops | bytes accessed | tf_op | source)
XLA Modules:
  0.0 354.6 jit_solution(7681426328673760972)
XLA Ops:
  7.2 1.4 fusion.88
  8.6 1.0 copy.303
  9.6 4.1 %fusion.70 = (bf16[1024,4,512]{2,0,1:T(8,128)(2,1)}, pred[1024,4,512]{2,0,1:T(32,128)(4,1)}) fusion(s32[1024,4]{0,1:T(4,128)} %param.8), kind=kLoop, calls=%fused_computation.125 | loop fusion | flops 4194304 | bytes 6307840 | tf_op jit(solution)/shard_map/convert_element_type | solution.py:152
  14.0 2.5 fusion.16
  16.5 1.0 copy-done.30
  17.5 2.0 fusion.18
  20.3 2.1 fusion.87
  22.4 1.3 copy.305
  23.6 1.0 copy.302
  24.7 2.9 convert_reduce_fusion
  27.5 2.9 all-gather.6
  30.5 9.6 %all-gather.7 = f32[4,4,512]{2,1,0:T(4,128)S(1)} all-gather(f32[1,4,512]{2,1,0:T(4,128)S(1)} %slice_add_fusion.20), channel_id=5, replica_groups=mesh['seq_0'=4,'seq_1'=4,'seq_2'=2,'head'=4] {'seq_1'}, dimensions={0}, use_global_device_ids=true | all-gather | bytes 40960 | tf_op jit(solution)/shard_map/all_gather | solution.py:24
  40.1 10.2 %all_gather.45 = f32[4,4,512]{2,1,0:T(4,128)S(1)} all-gather(f32[1,4,512]{2,1,0:T(4,128)S(1)} %slice_add_fusion.17), channel_id=1, replica_groups=mesh['seq_0'=4,'seq_1'=4,'seq_2'=2,'head'=4] {'seq_0'}, dimensions={0}, use_global_device_ids=true | all-gather | bytes 40960 | tf_op jit(solution)/shard_map/all_gather | solution.py:24
  50.4 2.8 slice_add_fusion.13
  53.9 2.1 fusion.33
  57.5 1.2 select_reduce_fusion.1
  58.8 1.3 fusion.4
  60.1 1.2 select_reduce_fusion
  61.4 5.5 %fusion.11 = (f32[4,512]{1,0:T(4,128)S(1)}, f32[4,512]{1,0:T(4,128)S(1)}, f32[4,512]{1,0:T(4,128)S(1)}, f32[4,512]{1,0:T(4,128)S(1)}) fusion(f32[4,512,512]{2,1,0:T(8,128)S(1)} %get-tuple-element.39, f32[4,512]{1,0:T(4,128)S(1)} %max.16, pred[512,512]{0,1:T(8,128)(4,1)S(1)} %iota_compare_fusion.1, f32[4,512]{1,0:T(4,128)S(1)} %max.17, ...), kind=kLoop, calls=%fused_computation.28 | loop fusion | flops 23060480 | bytes 17108992 | tf_op jit(solution)/shard_map/reduce_sum | solution.py:106
  66.9 20.5 %all-gather.16.cloned.1.call-done = bf16[1024,2048]{1,0:T(8,128)(2,1)} async-done(((bf16[1024,512]{1,0:T(8,128)(2,1)}), bf16[1024,2048]{1,0:T(8,128)(2,1)}) %all-gather.16.cloned.1.call-update) | async-done | bytes 4194320 | tf_op jit(solution)/shard_map/all_gather | solution.py:144
  87.4 4.7 %convolution_convert_fusion = bf16[1024,512]{0,1:T(8,128)(2,1)S(1)} fusion(bf16[1024,2048]{1,0:T(8,128)(2,1)} %all-gather.16.cloned.1.call-done, bf16[512,2048]{1,0:T(8,128)(2,1)S(1)} %copy-done), kind=kOutput, calls=%fused_computation.35 | convolution fusion | flops 2148007936 | bytes 7340032 | tf_op jit(solution)/shard_map/tn,hn->th/dot_general | solution.py:142
  92.2 1.9 fusion.54
  94.7 2.4 convolution_add_fusion.6
  97.2 41.1 %all-gather.26.cloned.1.call-done = f32[16,512,128]{2,1,0:T(8,128)} async-done(((f32[4,512,128]{2,1,0:T(8,128)}), f32[16,512,128]{2,1,0:T(8,128)}) %all-gather.26.cloned.1.call-update) | async-done | bytes 4194320 | tf_op jit(solution)/shard_map/all_gather | solution.py:24
  138.3 3.3 fusion.53
  141.7 12.7 %all-gather.24.cloned.1.call-done = f32[8,512,128]{2,1,0:T(8,128)} async-done(((f32[4,512,128]{2,1,0:T(8,128)}), f32[8,512,128]{2,1,0:T(8,128)}) %all-gather.24.cloned.1.call-update) | async-done | bytes 2097168 | tf_op jit(solution)/shard_map/all_gather | solution.py:24
  154.5 2.6 slice_add_fusion.6
  157.4 4.8 %fusion.58 = f32[4,128,512]{2,1,0:T(8,128)} fusion(bf16[512,4,128]{0,2,1:T(8,128)(2,1)S(1)} %bitcast.199, f32[4,512,512]{2,1,0:T(8,128)} %copy-done.2, f32[4,512]{1,0:T(4,128)S(1)} %add.336, f32[4,512]{1,0:T(4,128)S(1)} %max.17, pred[512,512]{0,1:T(8,128)(4,1)S(1)} %iota_compare_fusion.1), kind=kOutput, calls=%fused_computation.112 | convolution fusion | flops 274726912 | bytes 6045696 | tf_op jit(solution)/shard_map/htu,the->uhe/dot_general | solution.py:135
  162.2 2.6 fusion.64
  164.8 41.2 %all-gather.18.cloned.1.call-done = f32[4,4,512,128]{3,2,1,0:T(8,128)} async-done(((f32[1,4,512,128]{3,2,1,0:T(8,128)}), f32[4,4,512,128]{3,2,1,0:T(8,128)}) %all-gather.18.cloned.1.call-update) | async-done | bytes 4194320 | tf_op jit(solution)/shard_map/all_gather | solution.py:24
  206.0 4.7 %add_convert_fusion.1 = (bf16[4,512,128]{2,1,0:T(8,128)(2,1)S(1)}, bf16[4,512,128]{2,1,0:T(8,128)(2,1)S(1)}) fusion(f32[4,512,128]{2,1,0:T(8,128)} %copy-done.30, f32[8,512,128]{2,1,0:T(8,128)S(1)} %copy-done.19, pred[]{:T(512)S(6)} %gt.55, pred[]{:T(512)S(6)} %gt.54, pred[]{:T(512)S(6)} %gt.53, pred[]{:T(512)S(6)} %gt.52, ...), kind=kLoop, calls=%fused_computation.107 | loop fusion | flops 5767168 | bytes 12582922 | tf_op jit(solution)/shard_map/convert_element_type | solution.py:113
  210.9 2.4 fusion.56
  213.3 2.0 fusion.62
  215.8 1.6 fusion.30
  217.4 3.3 multiply_convert_fusion.2
  220.6 36.0 %all-gather.28.cloned.1.call-done = f32[16,512,128]{2,1,0:T(8,128)} async-done(((f32[4,512,128]{2,1,0:T(8,128)}), f32[16,512,128]{2,1,0:T(8,128)}) %all-gather.28.cloned.1.call-update) | async-done | bytes 4194320 | tf_op jit(solution)/shard_map/all_gather | solution.py:24
  256.6 3.3 fusion.49
  260.0 2.3 fusion.90
  262.3 4.5 %fusion.31 = f32[4,512]{1,0:T(4,128)S(1)} fusion(f32[4,512,128]{1,2,0:T(8,128)} %fusion.56, bf16[512,4,128]{0,2,1:T(8,128)(2,1)} %bitcast.193, bf16[512,4,128]{0,2,1:T(8,128)(2,1)} %bitcast.200, f32[4,512,512]{2,1,0:T(8,128)} %copy-done.2, f32[4,512]{1,0:T(4,128)S(1)} %add.336, f32[4,512]{1,0:T(4,128)S(1)} %max.17, pred[512,512]{0,1:T(8,128)(4,1)S(1)} %iota_compare_fusion.1), kind=kOutput, calls=%fused_computation.62 | convolution fusion | flops 275773440 | bytes 6578176 | tf_op jit(solution)/shard_map/htu,uhe->hte/dot_general | solution.py:114
  266.8 2.2 multiply_convert_fusion
  269.0 1.3 copy-done.18
  270.4 1.7 fusion.91
  272.1 3.3 multiply_convert_fusion.3
  275.4 4.2 %convolution_add_fusion.1 = f32[4,512,128]{2,1,0:T(8,128)} fusion(f32[4,512,128]{2,1,0:T(8,128)S(1)} %fusion.90, bf16[4,512,512]{1,2,0:T(8,128)(2,1)} %multiply_convert_fusion.3, bf16[512,4,128]{0,2,1:T(8,128)(2,1)S(1)} %bitcast.186, pred[1024,4,512]{2,0,1:T(32,128)(4,1)} %get-tuple-element.38), kind=kOutput, calls=%fused_computation.43 | convolution fusion | flops 537395200 | bytes 5767168 | tf_op jit(solution)/shard_map/ths,the->hse/dot_general | solution.py:131
  279.6 5.8 %multiply_convert_fusion.1 = bf16[4,512,512]{1,2,0:T(8,128)(2,1)} fusion(bf16[512,4,128]{0,2,1:T(8,128)(2,1)} %bitcast.201, bf16[512,4,128]{0,2,1:T(8,128)(2,1)} %bitcast.194, f32[4,512]{1,0:T(4,128)S(1)} %fusion.31, f32[4,512]{1,0:T(4,128)S(1)} %add.336, f32[4,512]{1,0:T(4,128)S(1)} %max.17, f32[4,512,512]{2,1,0:T(8,128)} %copy-done.2, ...), kind=kOutput, calls=%fused_computation.14 | convolution fusion | flops 277872640 | bytes 7626752 | tf_op jit(solution)/shard_map/the,uhe->htu/dot_general | solution.py:120
  285.4 4.6 %fusion.21 = f32[4,512,128]{2,1,0:T(8,128)} fusion(f32[4,512,128]{2,1,0:T(8,128)} %convolution_add_fusion.1, f32[4,512,128]{2,1,0:T(8,128)} %fusion.91, bf16[4,512,512]{1,2,0:T(8,128)(2,1)} %multiply_convert_fusion.1, bf16[512,4,128]{0,2,1:T(8,128)(2,1)S(1)} %bitcast.182, pred[1024,4,512]{2,0,1:T(32,128)(4,1)S(1)} %copy-done.23), kind=kOutput, calls=%fused_computation.42 | convolution fusion | flops 537657344 | bytes 6815744 | tf_op jit(solution)/shard_map/ths,the->hse/dot_general | solution.py:131
  290.1 1.3 copy.307
  291.4 4.8 %all_to_all.20 = f32[2,16,64,128]{3,2,1,0:T(8,128)S(1)} all-to-all(f32[2,16,64,128]{3,2,1,0:T(8,128)S(1)} %bitcast.189), channel_id=1, replica_groups=mesh['seq_0'=4,'seq_1'=4,'seq_2'=2,'head'=4] {'seq_2'}, dimensions={0} | all-to-all | bytes 2097152 | tf_op jit(solution)/shard_map/all_to_all | solution.py:41
  296.2 0.9 reduce_sum.98
  297.1 5.8 %all-to-all-start.1 = ((f32[16,64,128]{2,1,0:T(8,128)}), f32[16,64,128]{2,1,0:T(8,128)S(1)}, u32[]{:S(2)}, u32[]{:S(2)}) async-start(f32[16,64,128]{2,1,0:T(8,128)} %reduce_sum.98), calls=%async_computation.1 | async-start | bytes 1048576 | tf_op jit(solution)/shard_map/all_to_all | solution.py:48
  303.0 2.2 convolution_bitcast_fusion
  305.2 3.1 fusion.28
  308.3 5.4 %all-to-all-done.1 = f32[16,64,128]{2,1,0:T(8,128)S(1)} async-done(((f32[16,64,128]{2,1,0:T(8,128)}), f32[16,64,128]{2,1,0:T(8,128)S(1)}, u32[]{:S(2)}, u32[]{:S(2)}) %all-to-all-start.1) | async-done | bytes 524320 | tf_op jit(solution)/shard_map/all_to_all | solution.py:48
  314.6 5.3 %all-to-all-start.2 = ((f32[16,64,128]{2,1,0:T(8,128)}), f32[16,64,128]{2,1,0:T(8,128)}, u32[]{:S(2)}, u32[]{:S(2)}) async-start(f32[16,64,128]{2,1,0:T(8,128)} %broadcast_in_dim.108), calls=%async_computation.2 | async-start | bytes 1048576 | tf_op jit(solution)/shard_map/all_to_all | solution.py:58
  320.4 1.1 copy-done.25
  322.1 1.3 copy.256
  323.4 7.0 %all-to-all-done.2 = f32[16,64,128]{2,1,0:T(8,128)} async-done(((f32[16,64,128]{2,1,0:T(8,128)}), f32[16,64,128]{2,1,0:T(8,128)}, u32[]{:S(2)}, u32[]{:S(2)}) %all-to-all-start.2) | async-done | bytes 524320 | tf_op jit(solution)/shard_map/all_to_all | solution.py:58
  330.5 1.2 broadcast_in_dim.109
  331.6 6.4 %all_to_all.21 = f32[2,16,64,128]{3,2,1,0:T(8,128)S(1)} all-to-all(f32[2,16,64,128]{3,2,1,0:T(8,128)S(1)} %broadcast_in_dim.109), channel_id=1, replica_groups=mesh['seq_0'=4,'seq_1'=4,'seq_2'=2,'head'=4] {'seq_2'}, dimensions={0} | all-to-all | bytes 2097152 | tf_op jit(solution)/shard_map/all_to_all | solution.py:58
  338.0 1.1 copy.255
  339.1 4.3 %fusion.48 = f32[4,512,128]{2,1,0:T(8,128)S(1)} fusion(f32[4,4,512,128]{3,2,1,0:T(8,128)} %all-gather.20.cloned.1.call-done, f32[16,512,128]{2,1,0:T(8,128)} %all-gather.28.cloned.1.call-done, f32[8,512,128]{2,1,0:T(8,128)S(1)} %copy-done.20, pred[]{:T(512)S(6)} %lt.35, pred[]{:T(512)S(6)} %lt.36, pred[]{:T(512)S(6)} %lt.37, pred[]{:T(512)S(6)} %lt.38, ...), kind=kLoop, calls=%fused_computation.80 | loop fusion | flops 4980736 | bytes 11534346 | tf_op jit(solution)/shard_map/add | solution.py:83
  343.5 0.9 fusion.36
  345.0 1.0 fusion.37
  346.1 1.3 copy.257
  (125 shorter events, 8.1 us)
Async XLA Ops:
  7.2 80.2 %copy-start = (bf16[512,2048]{1,0:T(8,128)(2,1)S(1)}, bf16[512,2048]{1,0:T(8,128)(2,1)}, u32[]{:S(2)}) copy-start(bf16[512,2048]{1,0:T(8,128)(2,1)} %param.10) | copy-start | bytes 6291460
  7.2 43.3 %all-gather.22.cloned.1.call-start = ((), (), s32[]{:S(2)}) async-start(), calls=%async_computation.7 | async-start | bytes 3145728 | tf_op jit(solution)/shard_map/all_gather | solution.py:24
  14.0 5.5 %copy-start.36 = (bf16[512,512]{0,1:T(8,128)(2,1)}, bf16[512,512]{0,1:T(8,128)(2,1)S(1)}, u32[]{:S(2)}) copy-start(bf16[512,512]{0,1:T(8,128)(2,1)S(1)} %copy.304) | copy-start | bytes 1572868
  14.0 3.5 copy-start.21
  16.5 1.0 copy-start.30
  19.5 67.9 %all-gather.16.cloned.1.call-start = ((), (), s32[]{:S(2)}) async-start(), calls=%async_computation.4 | async-start | bytes 5242880 | tf_op jit(solution)/shard_map/all_gather | solution.py:144
  20.2 118.1 %all-gather.26.cloned.1.call-start = ((), (), s32[]{:S(2)}) async-start(), calls=%async_computation.9 | async-start | bytes 5242880 | tf_op jit(solution)/shard_map/all_gather | solution.py:24
  24.7 29.2 %copy-start.14 = (bf16[4,512,128]{2,1,0:T(8,128)(2,1)S(1)}, bf16[4,512,128]{2,1,0:T(8,128)(2,1)}, u32[]{:S(2)}) copy-start(bf16[4,512,128]{2,1,0:T(8,128)(2,1)} %param.9) | copy-start | bytes 1572868
  53.3 101.2 %all-gather.24.cloned.1.call-start = ((), (), s32[]{:S(2)}) async-start(), calls=%async_computation.8 | async-start | bytes 3145728 | tf_op jit(solution)/shard_map/all_gather | solution.py:24
  53.9 2.1 copy-start.22
  56.0 1.5 copy-start.28
  56.0 1.5 copy-start.15
  56.8 2.0 copy-start.26
  57.5 3.9 %copy-start.2 = (f32[4,512,512]{2,1,0:T(8,128)}, f32[4,512,512]{2,1,0:T(8,128)S(1)}, u32[]{:S(2)}) copy-start(f32[4,512,512]{2,1,0:T(8,128)S(1)} %fusion.89) | copy-start | bytes 12582916
  58.8 2.6 copy-start.11
  60.1 6.8 %copy-start.3 = (f32[4,512,512]{2,1,0:T(8,128)}, f32[4,512,512]{2,1,0:T(8,128)S(1)}, u32[]{:S(2)}) copy-start(f32[4,512,512]{2,1,0:T(8,128)S(1)} %get-tuple-element.39) | copy-start | bytes 12582916
  61.3 5.5 %copy-start.7 = (f32[4,512,512]{1,2,0:T(8,128)}, f32[4,512,512]{1,2,0:T(8,128)S(1)}, u32[]{:S(2)}) copy-start(f32[4,512,512]{1,2,0:T(8,128)S(1)} %get-tuple-element.43) | copy-start | bytes 12582916
  87.4 4.8 %copy-start.8 = (f32[4,512,512]{1,2,0:T(8,128)S(1)}, f32[4,512,512]{1,2,0:T(8,128)}, u32[]{:S(2)}) copy-start(f32[4,512,512]{1,2,0:T(8,128)} %copy-done.7) | copy-start | bytes 12582916
  92.2 1.9 copy-start.41
  92.2 65.2 %copy-start.39 = (bf16[512,512]{0,1:T(8,128)(2,1)}, bf16[512,512]{0,1:T(8,128)(2,1)S(1)}, u32[]{:S(2)}) copy-start(bf16[512,512]{0,1:T(8,128)(2,1)S(1)} %get-tuple-element.32) | copy-start | bytes 1572868
  92.2 2.6 copy-start.12
  94.1 3.0 copy-start.31
  97.1 108.9 %all-gather.18.cloned.1.call-start = ((), (), s32[]{:S(2)}) async-start(), calls=%async_computation.5 | async-start | bytes 5242880 | tf_op jit(solution)/shard_map/all_gather | solution.py:24
  141.7 114.9 %all-gather.28.cloned.1.call-start = ((), (), s32[]{:S(2)}) async-start(), calls=%async_computation.10 | async-start | bytes 5242880 | tf_op jit(solution)/shard_map/all_gather | solution.py:24
  157.1 182.0 %all-gather.20.cloned.1.call-start = ((), (), s32[]{:S(2)}) async-start(), calls=%async_computation.6 | async-start | bytes 5242880 | tf_op jit(solution)/shard_map/all_gather | solution.py:24
  157.4 4.9 %copy-start.4 = (f32[4,512,512]{2,1,0:T(8,128)S(1)}, f32[4,512,512]{2,1,0:T(8,128)}, u32[]{:S(2)}) copy-start(f32[4,512,512]{2,1,0:T(8,128)} %copy-done.3) | copy-start | bytes 12582916
  157.4 4.9 %copy-start.42 = (bf16[512,512]{0,1:T(8,128)(2,1)S(1)}, bf16[512,512]{0,1:T(8,128)(2,1)}, u32[]{:S(2)}) copy-start(bf16[512,512]{0,1:T(8,128)(2,1)} %copy-done.41) | copy-start | bytes 1572868
  162.2 43.8 %copy-start.19 = (f32[8,512,128]{2,1,0:T(8,128)S(1)}, f32[8,512,128]{2,1,0:T(8,128)}, u32[]{:S(2)}) copy-start(f32[8,512,128]{2,1,0:T(8,128)} %all-gather.22.cloned.1.call-done) | copy-start | bytes 6291460
  206.0 5.0 %copy-start.9 = (f32[4,512,512]{1,2,0:T(8,128)S(1)}, f32[4,512,512]{1,2,0:T(8,128)}, u32[]{:S(2)}) copy-start(f32[4,512,512]{1,2,0:T(8,128)} %copy-done.7) | copy-start | bytes 12582916
  210.7 2.6 copy-start.34
  210.9 2.4 copy-start.13
  213.3 2.2 copy-start.5
  213.3 2.3 copy-start.37
  213.3 2.5 copy-start.43
  220.6 39.3 %copy-start.16 = (bf16[512,512]{0,1:T(8,128)(2,1)S(1)}, bf16[512,512]{0,1:T(8,128)(2,1)}, u32[]{:S(2)}) copy-start(bf16[512,512]{0,1:T(8,128)(2,1)} %copy.302) | copy-start | bytes 1572868
  262.2 4.5 %copy-start.10 = (f32[4,512,512]{1,2,0:T(8,128)S(1)}, f32[4,512,512]{1,2,0:T(8,128)}, u32[]{:S(2)}) copy-start(f32[4,512,512]{1,2,0:T(8,128)} %copy-done.7) | copy-start | bytes 12582916
  262.3 4.5 %copy-start.35 = (bf16[4,512,128]{2,1,0:T(8,128)(2,1)S(1)}, bf16[4,512,128]{2,1,0:T(8,128)(2,1)}, u32[]{:S(2)}) copy-start(bf16[4,512,128]{2,1,0:T(8,128)(2,1)} %copy-done.34) | copy-start | bytes 1572868
  262.3 4.5 %copy-start.40 = (bf16[512,512]{0,1:T(8,128)(2,1)S(1)}, bf16[512,512]{0,1:T(8,128)(2,1)}, u32[]{:S(2)}) copy-start(bf16[512,512]{0,1:T(8,128)(2,1)} %copy-done.39) | copy-start | bytes 1572868
  266.8 5.3 %copy-start.6 = (f32[4,512,512]{2,1,0:T(8,128)S(1)}, f32[4,512,512]{2,1,0:T(8,128)}, u32[]{:S(2)}) copy-start(f32[4,512,512]{2,1,0:T(8,128)} %copy-done.3) | copy-start | bytes 12582916
  266.8 5.2 %copy-start.38 = (bf16[512,512]{0,1:T(8,128)(2,1)S(1)}, bf16[512,512]{0,1:T(8,128)(2,1)}, u32[]{:S(2)}) copy-start(bf16[512,512]{0,1:T(8,128)(2,1)} %copy.303) | copy-start | bytes 1572868
  266.8 5.2 %copy-start.44 = (bf16[512,512]{0,1:T(8,128)(2,1)S(1)}, bf16[512,512]{0,1:T(8,128)(2,1)}, u32[]{:S(2)}) copy-start(bf16[512,512]{0,1:T(8,128)(2,1)} %copy-done.41) | copy-start | bytes 1572868
  269.0 1.4 copy-start.18
  279.6 5.8 %copy-start.23 = (pred[1024,4,512]{2,0,1:T(32,128)(4,1)S(1)}, pred[1024,4,512]{2,0,1:T(32,128)(4,1)}, u32[]{:S(2)}) copy-start(pred[1024,4,512]{2,0,1:T(32,128)(4,1)} %get-tuple-element.38) | copy-start | bytes 6291460
  297.1 16.5 %all-to-all-start.1 = ((f32[16,64,128]{2,1,0:T(8,128)}), f32[16,64,128]{2,1,0:T(8,128)S(1)}, u32[]{:S(2)}, u32[]{:S(2)}) async-start(f32[16,64,128]{2,1,0:T(8,128)} %reduce_sum.98), calls=%async_computation.1 | async-start | bytes 1048576 | tf_op jit(solution)/shard_map/all_to_all | solution.py:48
  303.0 16.9 %copy-start.17 = (bf16[4,512,512]{1,2,0:T(8,128)(2,1)S(1)}, bf16[4,512,512]{1,2,0:T(8,128)(2,1)}, u32[]{:S(2)}) copy-start(bf16[4,512,512]{1,2,0:T(8,128)(2,1)} %multiply_convert_fusion.2) | copy-start | bytes 6291460
  313.7 6.7 %copy-start.27 = (bf16[512,4,128]{2,0,1:T(8,128)(2,1)S(1)}, bf16[512,4,128]{2,0,1:T(8,128)(2,1)}, u32[]{:S(2)}) copy-start(bf16[512,4,128]{2,0,1:T(8,128)(2,1)} %copy-done.26) | copy-start | bytes 1572868
  314.6 15.9 %all-to-all-start.2 = ((f32[16,64,128]{2,1,0:T(8,128)}), f32[16,64,128]{2,1,0:T(8,128)}, u32[]{:S(2)}, u32[]{:S(2)}) async-start(f32[16,64,128]{2,1,0:T(8,128)} %broadcast_in_dim.108), calls=%async_computation.2 | async-start | bytes 1048576 | tf_op jit(solution)/shard_map/all_to_all | solution.py:58
  319.9 1.6 copy-start.25
  319.9 2.1 copy-start.29
  322.1 17.0 %copy-start.20 = (f32[8,512,128]{2,1,0:T(8,128)S(1)}, f32[8,512,128]{2,1,0:T(8,128)}, u32[]{:S(2)}) copy-start(f32[8,512,128]{2,1,0:T(8,128)} %all-gather.24.cloned.1.call-done) | copy-start | bytes 6291460
  339.1 4.3 %copy-start.45 = (f32[4,128,512]{2,1,0:T(8,128)S(1)}, f32[4,128,512]{2,1,0:T(8,128)}, u32[]{:S(2)}) copy-start(f32[4,128,512]{2,1,0:T(8,128)} %fusion.58) | copy-start | bytes 3145732
  339.1 4.4 %copy-start.24 = (pred[1024,4,512]{2,0,1:T(32,128)(4,1)S(1)}, pred[1024,4,512]{2,0,1:T(32,128)(4,1)}, u32[]{:S(2)}) copy-start(pred[1024,4,512]{2,0,1:T(32,128)(4,1)} %get-tuple-element.38) | copy-start | bytes 6291460
  343.5 1.2 copy-start.32
  343.5 1.5 copy-start.33
  343.5 4.0 %copy-start.1 = (bf16[512,2048]{1,0:T(8,128)(2,1)S(1)}, bf16[512,2048]{1,0:T(8,128)(2,1)}, u32[]{:S(2)}) copy-start(bf16[512,2048]{1,0:T(8,128)(2,1)} %param.10) | copy-start | bytes 6291460
Sparse Core Ops, SparseCore 0:
  19.6 16.9 all-gather.21
  38.2 49.0 all-gather.15
  89.6 48.6 all-gather.25
  140.4 14.0 all-gather.23
  156.6 49.3 all-gather.17
  208.1 48.4 all-gather.27
  260.1 53.5 all-gather.19
where the time goes:
time: 360 us; the launch traced here: 355 us
  waiting for transfers between devices  165 us (46%)
  matrix products  74.1 us (21%)
  other arithmetic  34.9 us (10%)
  blocking collectives  33.9 us (9%)
  local copies, waits for them, and re-layouts  19.7 us (5%)
  between operations  15.1 us (4%)
  starting transfers between devices  12.1 us (3%)
    all_gather x6, waiting for transfers between devices, carried_in(): pieces = jax.tree.map(lambda part: lax.all_gather(part, axis), subtotal)  131 us
    all_gather x3, blocking collectives, carried_in(): pieces = jax.tree.map(lambda part: lax.all_gather(part, axis), subtotal)  22.7 us
    all_gather x1, waiting for transfers between devices, per_device(): lax.all_gather(grad_out, 'head', axis=1, tiled=True)  20.5 us
    add x7, other arithmetic, add_tree(): return jax.tree.map(jnp.add, earlier, later)  16.4 us
    unnamed x98, local copies, waits for them, and re-layouts  11.7 us
    dot_general x2, matrix products, attend_block(): jnp.einsum('the,uhe->htu', dout, value, preferred_element_type=jnp.float32)  9.15 us
    dot_general x2, matrix products, attend_block(): jnp.einsum('ths,the->hse', onehot, key_grad, preferred_element_type=jnp.f...  8.84 us
    dot_general x2, matrix products, attend_block(): jnp.einsum('htu,the->uhe', local_low, dout, preferred_element_type=jnp.fl...  7.4 us
  transfers between devices with their start and end apart: 9, of which 7 were waited for; matrix products, arithmetic and copies ran while one was open for 28% of the time, Pallas kernels for 0%

commit v1 on v0

v1 whole, which is shorter than its diff:
```python
import functools
import math

import jax
import jax.numpy as jnp
from jax import lax
from jax.experimental import pallas as pl
from jax.experimental.pallas import tpu as pltpu
from jax.sharding import PartitionSpec as P

BLOCK = 512
TILE = 128
HALF = 64
ROWS = 80
F32 = jnp.float32
BF16 = jnp.bfloat16
VMEM_LIMIT = 56 << 20


def dot(left, right):
    return lax.dot_general(left, right, (((1,), (0,)), ((), ())), preferred_element_type=F32)


def dot_nt(left, right):
    return lax.dot_general(left, right, (((1,), (1,)), ((), ())), preferred_element_type=F32)


def params(count=1):
    return pltpu.CompilerParams(
        dimension_semantics=("arbitrary",) * count, vmem_limit_bytes=VMEM_LIMIT
    )


def onehot_rows(codes_row, start):
    shape = (TILE, codes_row.shape[1])
    entry = lax.broadcasted_iota(jnp.int32, shape, 0) + start
    return jnp.where(entry == codes_row, 1.0, 0.0).astype(BF16)


def own_kernel(codes_ref, value_ref, send_ref, first_ref):
    entries = first_ref.shape[1]
    ones = jnp.ones((BLOCK, TILE), BF16)
    count_rows = []
    for i in range(entries // TILE):
        total = None
        row_total = None
        for b in range(codes_ref.shape[2] // BLOCK):
            span = slice(b * BLOCK, (b + 1) * BLOCK)
            hot = onehot_rows(codes_ref[0, :, span], i * TILE)
            part = dot(hot, value_ref[span, :])
            if b == 0:
                first_ref[0, i * TILE : (i + 1) * TILE, :TILE] = part
                first_ref[0, i * TILE : (i + 1) * TILE, TILE:] = dot(hot, ones)
            row = dot_nt(jnp.ones((16, BLOCK), BF16), hot)
            total = part if total is None else total + part
            row_total = row if row_total is None else row_total + row
        high = jnp.floor(row_total * (1.0 / 256.0))
        low = row_total - high * 256.0
        place = lax.broadcasted_iota(jnp.int32, (16, TILE), 0)
        extra = jnp.where(place == 0, high, jnp.where(place == 1, low, 0.0)).astype(BF16)
        for k in range(2):
            send_ref[2 * i + k, :HALF, :] = total[k * HALF : (k + 1) * HALF].astype(BF16)
            send_ref[2 * i + k, HALF:, :] = extra


def own_sums(codes_rows, values, heads, entries):
    tokens = values.shape[0]
    slices = entries // HALF
    return pl.pallas_call(
        own_kernel,
        grid=(heads,),
        in_specs=[
            pl.BlockSpec((1, 1, tokens), lambda h: (h, 0, 0)),
            pl.BlockSpec((tokens, TILE), lambda h: (0, h)),
        ],
        out_specs=[
            pl.BlockSpec((slices, ROWS, TILE), lambda h: (h, 0, 0)),
            pl.BlockSpec((1, entries, 2 * TILE), lambda h: (h, 0, 0)),
        ],
        out_shape=[
            jax.ShapeDtypeStruct((heads * slices, ROWS, TILE), BF16),
            jax.ShapeDtypeStruct((heads, entries, 2 * TILE), F32),
        ],
        compiler_params=params(),
        name="own_sums",
    )(codes_rows, values)


def prefix_kernel(in_ref, out_ref):
    count = in_ref.shape[0]
    running = jnp.zeros((HALF, TILE), F32)
    number = jnp.zeros((1, TILE), F32)
    place = lax.broadcasted_iota(jnp.int32, (16, TILE), 0)
    for d in range(count):
        out_ref[d, :HALF, :] = running.astype(BF16)
        high = jnp.floor(number * (1.0 / 256.0))
        low = number - high * 256.0
        extra = jnp.where(place == 0, high, jnp.where(place == 1, low, 0.0))
        out_ref[d, HALF:, :] = extra.astype(BF16)
        running = running + in_ref[d, :HALF, :].astype(F32)
        rows = in_ref[d, HALF:, :].astype(F32)
        number = number + rows[0:1] * 256.0 + rows[1:2]


def prefix_scan(pieces):
    return pl.pallas_call(
        prefix_kernel,
        out_shape=jax.ShapeDtypeStruct(pieces.shape, BF16),
        compiler_params=pltpu.CompilerParams(vmem_limit_bytes=VMEM_LIMIT),
        name="prefix_scan",
    )(pieces)


def suffix_kernel(in_ref, out_ref):
    count = in_ref.shape[0]
    running = jnp.zeros((HALF, TILE), F32)
    total = jnp.zeros((HALF, TILE), F32)
    for d in reversed(range(count)):
        out_ref[d, :HALF, :] = running.astype(BF16)
        running = running + in_ref[d, :HALF, :].astype(F32)
        total = total + in_ref[d, HALF:, :].astype(F32)
    low = total.astype(BF16)
    for d in range(count):
        out_ref[d, HALF:, :] = low


def suffix_scan(pieces):
    return pl.pallas_call(
        suffix_kernel,
        out_shape=jax.ShapeDtypeStruct(pieces.shape, BF16),
        compiler_params=pltpu.CompilerParams(vmem_limit_bytes=VMEM_LIMIT),
        name="suffix_scan",
    )(pieces)


def fold(array):
    rows, lanes = array.shape
    return jnp.sum(array.reshape(rows // 8, 8, lanes), axis=0)


def fold_max(array):
    rows, lanes = array.shape
    return jnp.max(array.reshape(rows // 8, 8, lanes), axis=0)


def attend_kernel(block, refs):
    if block == 0:
        (codes_ref, query_ref, value_ref, cotangent_ref, weight_ref, book_ref, book_t_ref,
         prefix_ref, grad_query_ref, local_ref, part_ref, code_ref,
         hot, dout, rows_k, rows_v, counts, scores, grads, score_grad, key_grad) = refs
    else:
        (codes_ref, query_ref, value_ref, cotangent_ref, weight_ref, book_ref, book_t_ref,
         prefix_ref, first_ref, part0_ref, code0_ref, _, _,
         grad_query_ref, local_ref, part_ref, send_ref,
         hot, dout, rows_k, rows_v, counts, scores, grads, score_grad, key_grad) = refs
    head = pl.program_id(0)
    entries, width = book_ref.shape[1:]
    tiles = BLOCK // TILE
    entry_tiles = entries // TILE
    scale = width ** -0.5
    factor = scale * math.log2(math.e)

    @pl.when(head == 0)
    def _():
        score_grad[...] = jnp.zeros_like(score_grad)
        for part in range(2):
            rows = slice(part * 256, (part + 1) * 256)
            total = None
            for k in range(cotangent_ref.shape[0]):
                columns = slice(k * BLOCK, (k + 1) * BLOCK)
                term = dot_nt(cotangent_ref[k, rows, :], weight_ref[:, columns])
                total = term if total is None else total + term
            for h in range(dout.shape[0]):
                dout[h, rows, :] = total[:, h * TILE : (h + 1) * TILE].astype(BF16)

    codes_row = codes_ref[0]
    for i in range(entry_tiles):
        hot[i * TILE : (i + 1) * TILE, :] = onehot_rows(codes_row, i * TILE)
    keys_t = dot(book_t_ref[0], hot[...])
    rows_k[:BLOCK, :] = keys_t.T.astype(BF16)
    keys_t = keys_t.astype(BF16)
    rows_k[BLOCK:, :] = book_ref[0]
    rows_v[:BLOCK, :] = value_ref[...]
    diagonal = lax.broadcasted_iota(jnp.int32, (TILE, TILE), 0) == lax.broadcasted_iota(
        jnp.int32, (TILE, TILE), 1
    )
    ones = jnp.ones((TILE, TILE), BF16)
    for i in range(entry_tiles):
        rows = slice(i * TILE, (i + 1) * TILE)
        line = prefix_ref[2 * i, HALF:, :].astype(F32)
        high = jnp.where(diagonal, line[0:1] * 256.0, 0.0).astype(BF16)
        low = jnp.where(diagonal, line[1:2], 0.0).astype(BF16)
        number = dot(high, ones) + dot(low, ones)
        for k in range(2):
            at = i * TILE + k * HALF
            sums = prefix_ref[2 * i + k, :HALF, :]
            if block > 0:
                sums = (sums.astype(F32) + first_ref[0, at : at + HALF, :TILE]).astype(BF16)
            rows_v[BLOCK + at : BLOCK + at + HALF, :] = sums
        if block > 0:
            number = number + first_ref[0, rows, TILE:]
        counts[rows, :] = number

    causal = lax.broadcasted_iota(jnp.int32, (TILE, TILE), 1) >= lax.broadcasted_iota(
        jnp.int32, (TILE, TILE), 0
    )
    top = [jnp.full((8, TILE), -jnp.inf, F32) for _ in range(tiles)]
    for i in range(tiles + entry_tiles):
        local = i < tiles
        start = i if local else 0
        rows = slice(i * TILE, (i + 1) * TILE)
        score = dot_nt(rows_k[rows, :], query_ref[start * TILE :, :])
        if not local:
            present = counts[(i - tiles) * TILE : (i - tiles + 1) * TILE, :] > 0.0
        for j in range(start, tiles):
            piece = score[:, (j - start) * TILE : (j - start + 1) * TILE]
            if local:
                if j == i:
                    piece = jnp.where(causal, piece, -jnp.inf)
            else:
                piece = jnp.where(present, piece, -jnp.inf)
            top[j] = jnp.maximum(top[j], fold_max(piece))
            scores[rows, j * TILE : (j + 1) * TILE] = piece
    top = [jnp.max(t, axis=0, keepdims=True) for t in top]
    total = [jnp.zeros((8, TILE), F32) for _ in range(tiles)]
    for i in range(tiles + entry_tiles):
        local = i < tiles
        rows = slice(i * TILE, (i + 1) * TILE)
        for j in range(i if local else 0, tiles):
            columns = slice(j * TILE, (j + 1) * TILE)
            piece = jnp.exp2((scores[rows, columns] - top[j]) * factor)
            scores[rows, columns] = piece
            if not local:
                piece = piece * counts[(i - tiles) * TILE : (i - tiles + 1) * TILE, :]
            total[j] = total[j] + fold(piece)
    inverse = [1.0 / jnp.sum(t, axis=0, keepdims=True) for t in total]
    mine = dout[head]
    delta = [jnp.zeros((8, TILE), F32) for _ in range(tiles)]
    for i in range(tiles + entry_tiles):
        local = i < tiles
        start = i if local else 0
        rows = slice(i * TILE, (i + 1) * TILE)
        grad = dot_nt(rows_v[rows, :], mine[start * TILE :, :])
        pieces = []
        for j in range(start, tiles):
            columns = slice(j * TILE, (j + 1) * TILE)
            low = (scores[rows, columns] * inverse[j]).astype(BF16)
            pieces.append(low)
            piece = grad[:, (j - start) * TILE : (j - start + 1) * TILE]
            grads[rows, columns] = piece
            delta[j] = delta[j] + fold(low.astype(F32) * piece)
        low = pieces[0] if len(pieces) == 1 else jnp.concatenate(pieces, axis=1)
        result = dot(low, mine[start * TILE :, :])
        if local:
            local_ref[rows, :] = result
        else:
            part_ref[0, (i - tiles) * TILE : (i - tiles + 1) * TILE, :] = result
    delta = [jnp.sum(t, axis=0, keepdims=True) for t in delta]
    inverse = [t * scale for t in inverse]
    code = []
    for i in range(tiles + entry_tiles):
        local = i < tiles
        start = i if local else 0
        rows = slice(i * TILE, (i + 1) * TILE)
        pieces = []
        for j in range(start, tiles):
            columns = slice(j * TILE, (j + 1) * TILE)
            shift = delta[j]
            if not local:
                shift = shift * counts[(i - tiles) * TILE : (i - tiles + 1) * TILE, :]
            piece = scores[rows, columns] * ((grads[rows, columns] - shift) * inverse[j])
            piece = piece.astype(BF16)
            pieces.append(piece)
            score_grad[rows, columns] = piece
        low = pieces[0] if len(pieces) == 1 else jnp.concatenate(pieces, axis=1)
        result = dot(low, query_ref[start * TILE :, :])
        if local:
            key_grad[rows, :] = result.astype(BF16)
        else:
            code.append(result)
    grad_t = dot(keys_t, score_grad[:BLOCK, :]) + dot(book_t_ref[0], score_grad[BLOCK:, :])
    grad_query_ref[...] = grad_t.T.astype(BF16)
    for i in range(entry_tiles):
        rows = slice(i * TILE, (i + 1) * TILE)
        result = code[i] + dot(hot[rows, :], key_grad[...])
        if block == 0:
            code_ref[0, rows, :] = result
        else:
            result = result + code0_ref[0, rows, :]
            parts = part_ref[0, rows, :] + part0_ref[0, rows, :]
            for k in range(2):
                half = slice(k * HALF, (k + 1) * HALF)
                send_ref[2 * i + k, :HALF, :] = parts[half].astype(BF16)
                send_ref[2 * i + k, HALF:, :] = result[half].astype(BF16)


def attend(block, codes_rows, queries, values, cotangent, weight, book, book_t, prefix, extra=None):
    heads, entries, width = book.shape
    tokens = queries.shape[0]
    slices = entries // HALF
    rows_of = lambda h: (block, h)
    whole3 = lambda h: (0, 0, 0)
    by_head = lambda h: (h, 0, 0)
    in_specs = [
        pl.BlockSpec((1, 1, BLOCK), lambda h: (h, 0, block)),
        pl.BlockSpec((BLOCK, width), rows_of),
        pl.BlockSpec((BLOCK, width), rows_of),
        pl.BlockSpec(cotangent.shape, whole3),
        pl.BlockSpec(weight.shape, lambda h: (0, 0)),
        pl.BlockSpec((1, entries, width), by_head),
        pl.BlockSpec((1, width, entries), by_head),
        pl.BlockSpec((slices, ROWS, TILE), by_head),
    ]
    args = [codes_rows, queries, values, cotangent, weight, book, book_t, prefix]
    per_head = pl.BlockSpec((1, entries, width), by_head)
    out_specs = [pl.BlockSpec((BLOCK, width), rows_of), pl.BlockSpec((BLOCK, width), rows_of), per_head]
    out_shape = [
        jax.ShapeDtypeStruct((tokens, heads * width), BF16),
        jax.ShapeDtypeStruct((tokens, heads * width), F32),
        jax.ShapeDtypeStruct(book.shape, F32),
    ]
    aliases = {}
    if block == 0:
        out_specs.append(per_head)
        out_shape.append(jax.ShapeDtypeStruct(book.shape, F32))
    else:
        first, part0, code0, grad_query, local = extra
        args += [first, part0, code0, grad_query, local]
        in_specs += [
            pl.BlockSpec((1, entries, 2 * width), by_head),
            per_head,
            per_head,
            pl.BlockSpec(memory_space=pl.ANY),
            pl.BlockSpec(memory_space=pl.ANY),
        ]
        aliases = {11: 0, 12: 1}
        out_specs.append(pl.BlockSpec((slices, 2 * HALF, TILE), by_head))
        out_shape.append(jax.ShapeDtypeStruct((heads * slices, 2 * HALF, TILE), BF16))
    both = BLOCK + entries
    return pl.pallas_call(
        lambda *refs: attend_kernel(block, refs),
        grid=(heads,),
        in_specs=in_specs,
        out_specs=out_specs,
        out_shape=out_shape,
        scratch_shapes=[
            pltpu.VMEM((entries, BLOCK), BF16),
            pltpu.VMEM((heads, BLOCK, width), BF16),
            pltpu.VMEM((both, width), BF16),
            pltpu.VMEM((both, width), BF16),
            pltpu.VMEM((entries, TILE), F32),
            pltpu.VMEM((both, BLOCK), F32),
            pltpu.VMEM((both, BLOCK), F32),
            pltpu.VMEM((both, BLOCK), BF16),
            pltpu.VMEM((BLOCK, width), BF16),
        ],
        input_output_aliases=aliases,
        compiler_params=params(),
        name=f"attend_block_{block}",
    )(*args)


def finish_kernel(codes_ref, local_ref, later_ref, part_ref, out_ref, book_ref):
    heads, entries, width = part_ref.shape
    slices = entries // HALF
    first = pl.program_id(0) == 0
    levels = lax.broadcasted_iota(jnp.int32, (BLOCK, entries), 1)
    for h in range(heads):
        pieces = later_ref[h * slices : (h + 1) * slices]
        later = pieces[:, :HALF, :].reshape(entries, width)
        total = (later.astype(F32) + jnp.where(first, part_ref[h], 0.0)).astype(BF16)
        hot = jnp.where(levels == codes_ref[:, h : h + 1], 1.0, 0.0).astype(BF16)
        columns = slice(h * width, (h + 1) * width)
        out_ref[:, columns] = (local_ref[:, columns] + dot(hot, total)).astype(BF16)
        book_ref[h] = pieces[:, HALF:, :].reshape(entries, width).astype(F32)


def finish(codes, local, later, part):
    heads, entries, width = part.shape
    tokens = local.shape[0]
    return pl.pallas_call(
        finish_kernel,
        grid=(tokens // BLOCK,),
        in_specs=[
            pl.BlockSpec((BLOCK, heads), lambda b: (b, 0)),
            pl.BlockSpec((BLOCK, heads * width), lambda b: (b, 0)),
            pl.BlockSpec(later.shape, lambda b: (0, 0, 0)),
            pl.BlockSpec(part.shape, lambda b: (0, 0, 0)),
        ],
        out_specs=[
            pl.BlockSpec((BLOCK, heads * width), lambda b: (b, 0)),
            pl.BlockSpec(part.shape, lambda b: (0, 0, 0)),
        ],
        out_shape=[
            jax.ShapeDtypeStruct(local.shape, BF16),
            jax.ShapeDtypeStruct(part.shape, F32),
        ],
        compiler_params=params(),
        name="finish_values",
    )(codes, local, later, part)


def per_device(queries, values, codes, codebook, out_weight, grad_out):
    heads, entries, width = codebook.shape
    exchange = functools.partial(
        lax.all_to_all, axis_name="seq", split_axis=0, concat_axis=0, tiled=True
    )
    gathered = [
        lax.all_gather(grad_out[b * BLOCK : (b + 1) * BLOCK], "head") for b in range(2)
    ]
    codes_rows = codes.T.reshape(heads, 1, -1)
    book_t = jnp.swapaxes(codebook, 1, 2)
    send, first = own_sums(codes_rows, values, heads, entries)
    prefix = exchange(prefix_scan(exchange(send)))
    common = (codes_rows, queries, values)
    grad_query, local, part0, code0 = attend(
        0, *common, gathered[0], out_weight, codebook, book_t, prefix
    )
    grad_query, local, part1, send = attend(
        1, *common, gathered[1], out_weight, codebook, book_t, prefix,
        (first, part0, code0, grad_query, local),
    )
    later = exchange(suffix_scan(exchange(send)))
    grad_values, grad_book = finish(codes, local, later, part1)
    return grad_query, grad_values, grad_book


def solution(mesh):
    rows = P("seq", "head")
    return jax.shard_map(
        per_device,
        mesh=mesh,
        in_specs=(rows, rows, rows, P("head", None, None), P("head", None), rows),
        out_specs=(rows, rows, P("head", None, None)),
        check_vma=False,
    )
```

time: 360 us -> 155 us (0.43); the launches traced: 355 us -> 154 us
  waiting for transfers between devices: 165 us -> 30.7 us
  matrix products: 74.1 us -> 0 us
  Pallas kernels: 0 us -> 46.9 us
  other arithmetic: 34.9 us -> 0 us
  blocking collectives: 33.9 us -> 47.7 us
  local copies, waits for them, and re-layouts: 19.7 us -> 6.81 us
  starting transfers between devices: 12.1 us -> 8.15 us
    all_gather x7 -> x2, waiting for transfers between devices: 152 us -> 1.71 us  [per_device(): lax.all_gather(grad_out[b * BLOCK:(b + 1) * BLOCK], 'head')]
    dot_general x31 -> x0, matrix products: 74.1 us -> none  [the longest x2 9.15 us: attend_block(): jnp.einsum('the,uhe->htu', dout, value, preferred_element_type=jnp.float32)]
    pallas_call x0 -> x6, Pallas kernels: none -> 46.9 us  [the longest x2 32.4 us: attend(): pl.pallas_call(lambda *refs: attend_kernel(block, refs), grid=(heads,), i...]
    all_to_all x2, blocking collectives: 11.2 us -> 47.7 us  [the longest x1 25 us: per_device(): later = exchange(suffix_scan(exchange(send)))]
    all_gather x3 -> x0, blocking collectives: 22.7 us -> none  [carried_in(): pieces = jax.tree.map(lambda part: lax.all_gather(part, axis), subtotal)]
    add x9 -> x0, other arithmetic: 16.4 us -> none  [the longest x7 16.4 us: add_tree(): return jax.tree.map(jnp.add, earlier, later)]
    all_to_all x2, waiting for transfers between devices: 12.4 us -> 28.2 us  [the longest x1 16.2 us: per_device(): later = exchange(suffix_scan(exchange(send)))]
    reduce_sum x4 -> x0, other arithmetic: 9.25 us -> none  [the longest x1 5.46 us: attend_block(): jnp.sum(local_exp, axis=-1, keepdims=True)]
  transfers between devices with their start and end apart: 9 -> 4, of which waited for: 7 -> 3; matrix products, arithmetic and copies ran while one was open for 28% -> 2% of each run, Pallas kernels for 0% -> 15%
where the time goes in v1:
time: 155 us; the launch traced here: 154 us
  blocking collectives  47.7 us (31%)
  Pallas kernels  46.9 us (30%)
  waiting for transfers between devices  30.7 us (20%)
  between operations  14.1 us (9%)
  starting transfers between devices  8.15 us (5%)
  local copies, waits for them, and re-layouts  6.81 us (4%)
    pallas_call x2, Pallas kernels, attend(): pl.pallas_call(lambda *refs: attend_kernel(block, refs), grid=(heads,), i...  32.4 us
    all_to_all x1, blocking collectives, per_device(): later = exchange(suffix_scan(exchange(send)))  25 us
    all_to_all x1, blocking collectives, per_device(): prefix = exchange(prefix_scan(exchange(send)))  22.7 us
    all_to_all x1, waiting for transfers between devices, per_device(): later = exchange(suffix_scan(exchange(send)))  16.2 us
    all_to_all x1, waiting for transfers between devices, per_device(): prefix = exchange(prefix_scan(exchange(send)))  12 us
    pallas_call x1, Pallas kernels, own_sums(): pl.pallas_call(own_kernel, grid=(heads,), in_specs=[pl.BlockSpec((1, 1, t...  5.39 us
    pallas_call x1, Pallas kernels, finish(): pl.pallas_call(finish_kernel, grid=(tokens // BLOCK,), in_specs=[pl.Block...  4.64 us
    all_to_all x1, starting transfers between devices, per_device(): prefix = exchange(prefix_scan(exchange(send)))  4.09 us
  transfers between devices with their start and end apart: 4, of which 3 were waited for; matrix products, arithmetic and copies ran while one was open for 2% of the time, Pallas kernels for 15%

profile of v1, /device:TPU:1, one launch (start us, length us, event | category | flops | bytes accessed | tf_op | source)
XLA Modules:
  0.0 154.3 jit_solution(1162775479175496603)
XLA Ops:
  7.2 0.0 copy-start.3
  7.2 0.0 all-gather.7.cloned.1.call-start
  7.2 2.2 %fusion = (bf16[512,512]{1,0:T(8,128)(2,1)}, bf16[512,512]{1,0:T(8,128)(2,1)}) fusion(bf16[1024,512]{1,0:T(8,128)(2,1)} %param.11), kind=kLoop, calls=%fused_computation | loop fusion | bytes 2097152 | tf_op jit(solution)/shard_map/slice | solution.py:409
  9.5 0.0 all-gather.7.cloned.1.call-update
  9.5 0.0 all-gather.5.cloned.1.call-start
  9.5 0.7 all-gather.5.cloned.1.call-update
  10.2 0.0 copy-done.3
  10.2 0.6 reshape.9.codes_ref.refs_0_
  10.9 5.4 %own_sums.1 = (bf16[32,80,128]{2,1,0:T(8,128)(2,1)}, f32[4,512,256]{2,1,0:T(8,128)}) custom-call(s32[4,1,1024]{2,1,0:T(1,128)} %reshape.9.codes_ref.refs_0_, bf16[1024,512]{1,0:T(8,128)(2,1)} %refs_2_.3), custom_call_target="tpu_custom_call" | custom-call | tf_op jit(solution)/shard_map/own_sums/pallas_call | solution.py:69
  16.3 0.0 copy-start.1
  16.3 22.7 %all_to_all.20.in_ref = bf16[32,80,128]{2,1,0:T(8,128)(2,1)} all-to-all(bf16[32,80,128]{2,1,0:T(8,128)(2,1)} %get-tuple-element.15), channel_id=1, replica_groups=mesh['seq'=32,'head'=4] {'seq'}, dimensions={0} | all-to-all | bytes 1310720 | tf_op jit(solution)/shard_map/all_to_all | solution.py:414
  39.0 2.1 %prefix_scan.1 = bf16[32,80,128]{2,1,0:T(8,128)(2,1)} custom-call(bf16[32,80,128]{2,1,0:T(8,128)(2,1)} %all_to_all.20.in_ref), custom_call_target="tpu_custom_call" | custom-call | tf_op jit(solution)/shard_map/prefix_scan/pallas_call | solution.py:106
  41.1 4.1 %all-to-all-start.1 = ((bf16[32,80,128]{2,1,0:T(8,128)(2,1)}), bf16[32,80,128]{2,1,0:T(8,128)(2,1)S(1)}, u32[]{:S(2)}, u32[]{:S(2)}) async-start(bf16[32,80,128]{2,1,0:T(8,128)(2,1)} %prefix_scan.1), calls=%async_computation.1 | async-start | bytes 1310720 | tf_op jit(solution)/shard_map/all_to_all | solution.py:414
  45.2 0.0 copy-done.1
  45.2 1.0 copy.11
  46.2 12.0 %all-to-all-done.1.refs_7_ = bf16[32,80,128]{2,1,0:T(8,128)(2,1)S(1)} async-done(((bf16[32,80,128]{2,1,0:T(8,128)(2,1)}), bf16[32,80,128]{2,1,0:T(8,128)(2,1)S(1)}, u32[]{:S(2)}, u32[]{:S(2)}) %all-to-all-start.1) | async-done | bytes 655392 | tf_op jit(solution)/shard_map/all_to_all | solution.py:414
  58.2 0.0 copy-start
  58.2 0.0 all-gather.7.cloned.1.call-done
  58.2 0.9 copy-done
  59.1 16.0 %attend_block_0.1 = (bf16[1024,512]{1,0:T(8,128)(2,1)}, f32[1024,512]{1,0:T(8,128)}, f32[4,512,128]{2,1,0:T(8,128)}, f32[4,512,128]{2,1,0:T(8,128)}) custom-call(s32[4,1,1024]{2,1,0:T(1,128)} %reshape.9.codes_ref.refs_0_, bf16[1024,512]{1,0:T(8,128)(2,1)} %refs_1_.3, bf16[1024,512]{1,0:T(8,128)(2,1)} %refs_2_.3, bf16[4,512,512]{2,1,0:T(8,128)(2,1)} %bitcast.7, ...), custom_call_target="tpu_custom_call" | custom-call | tf_op jit(solution)/shard_map/attend_block_0/pallas_call | solution.py:340
  75.1 1.7 %all-gather.5.cloned.1.call-done = bf16[2048,512]{1,0:T(8,128)(2,1)} async-done(((bf16[512,512]{1,0:T(8,128)(2,1)}), bf16[2048,512]{1,0:T(8,128)(2,1)}) %all-gather.5.cloned.1.call-update) | async-done | bytes 2097168 | tf_op jit(solution)/shard_map/all_gather | solution.py:409
  76.8 16.4 %attend_block_1.1 = (bf16[1024,512]{1,0:T(8,128)(2,1)}, f32[1024,512]{1,0:T(8,128)}, f32[4,512,128]{2,1,0:T(8,128)}, bf16[32,128,128]{2,1,0:T(8,128)(2,1)}) custom-call(s32[4,1,1024]{2,1,0:T(1,128)} %reshape.9.codes_ref.refs_0_, bf16[1024,512]{1,0:T(8,128)(2,1)} %refs_1_.3, ...), custom_call_target="tpu_custom_call", output_to_operand_aliasing={{0}: (11, {}), {1}: (12, {})} | custom-call | tf_op jit(solution)/shard_map/attend_block_1/pallas_call | solution.py:340
  93.2 25.0 %all_to_all.21.in_ref = bf16[32,128,128]{2,1,0:T(8,128)(2,1)} all-to-all(bf16[32,128,128]{2,1,0:T(8,128)(2,1)} %get-tuple-element.23), channel_id=1, replica_groups=mesh['seq'=32,'head'=4] {'seq'}, dimensions={0} | all-to-all | bytes 2097152 | tf_op jit(solution)/shard_map/all_to_all | solution.py:423
  118.2 2.4 %suffix_scan.1 = bf16[32,128,128]{2,1,0:T(8,128)(2,1)} custom-call(bf16[32,128,128]{2,1,0:T(8,128)(2,1)} %all_to_all.21.in_ref), custom_call_target="tpu_custom_call" | custom-call | tf_op jit(solution)/shard_map/suffix_scan/pallas_call | solution.py:128
  120.6 4.0 %all-to-all-start.3 = ((bf16[32,128,128]{2,1,0:T(8,128)(2,1)}), bf16[32,128,128]{2,1,0:T(8,128)(2,1)S(1)}, u32[]{:S(2)}, u32[]{:S(2)}) async-start(bf16[32,128,128]{2,1,0:T(8,128)(2,1)} %suffix_scan.1), calls=%async_computation.3 | async-start | bytes 2097152 | tf_op jit(solution)/shard_map/all_to_all | solution.py:423
  124.6 1.1 copy.12.codes_ref
  125.6 16.2 %all-to-all-done.3.later_ref = bf16[32,128,128]{2,1,0:T(8,128)(2,1)S(1)} async-done(((bf16[32,128,128]{2,1,0:T(8,128)(2,1)}), bf16[32,128,128]{2,1,0:T(8,128)(2,1)S(1)}, u32[]{:S(2)}, u32[]{:S(2)}) %all-to-all-start.3) | async-done | bytes 1048608 | tf_op jit(solution)/shard_map/all_to_all | solution.py:423
  141.9 0.0 copy-start.2
  141.9 1.0 copy-done.2
  142.9 4.6 %finish_values.1 = (bf16[1024,512]{1,0:T(8,128)(2,1)}, f32[4,512,128]{2,1,0:T(8,128)}) custom-call(s32[1024,4]{1,0:T(8,128)} %copy.12.codes_ref, f32[1024,512]{1,0:T(8,128)} %get-tuple-element.22.local_ref, bf16[32,128,128]{2,1,0:T(8,128)(2,1)} %copy-done.2, f32[4,512,128]{2,1,0:T(8,128)} %get-tuple-element.24.part_ref), custom_call_target="tpu_custom_call" | custom-call | tf_op jit(solution)/shard_map/finish_values/pallas_call | solution.py:381
Async XLA Ops:
  7.2 3.1 %copy-start.3 = (s32[1024,4]{0,1:T(4,128)S(1)}, s32[1024,4]{0,1:T(4,128)}, u32[]{:S(2)}) copy-start(s32[1024,4]{0,1:T(4,128)} %param.8) | copy-start | bytes 49156
  7.2 51.0 %all-gather.7.cloned.1.call-start = ((), (), s32[]{:S(2)}) async-start(), calls=%async_computation.5 | async-start | bytes 2621440 | tf_op jit(solution)/shard_map/all_gather | solution.py:409
  9.5 67.3 %all-gather.5.cloned.1.call-start = ((), (), s32[]{:S(2)}) async-start(), calls=%async_computation.4 | async-start | bytes 2621440 | tf_op jit(solution)/shard_map/all_gather | solution.py:409
  16.3 28.9 %copy-start.1 = (bf16[4,512,128]{2,1,0:T(8,128)(2,1)S(1)}, bf16[4,512,128]{2,1,0:T(8,128)(2,1)}, u32[]{:S(2)}) copy-start(bf16[4,512,128]{2,1,0:T(8,128)(2,1)} %refs_5_.3) | copy-start | bytes 1572868
  41.1 17.1 %all-to-all-start.1 = ((bf16[32,80,128]{2,1,0:T(8,128)(2,1)}), bf16[32,80,128]{2,1,0:T(8,128)(2,1)S(1)}, u32[]{:S(2)}, u32[]{:S(2)}) async-start(bf16[32,80,128]{2,1,0:T(8,128)(2,1)} %prefix_scan.1), calls=%async_computation.1 | async-start | bytes 1310720 | tf_op jit(solution)/shard_map/all_to_all | solution.py:414
  58.2 0.9 copy-start
  120.6 21.3 %all-to-all-start.3 = ((bf16[32,128,128]{2,1,0:T(8,128)(2,1)}), bf16[32,128,128]{2,1,0:T(8,128)(2,1)S(1)}, u32[]{:S(2)}, u32[]{:S(2)}) async-start(bf16[32,128,128]{2,1,0:T(8,128)(2,1)} %suffix_scan.1), calls=%async_computation.3 | async-start | bytes 2097152 | tf_op jit(solution)/shard_map/all_to_all | solution.py:423
  141.9 1.0 copy-start.2
Sparse Core Ops, SparseCore 0:
  10.2 34.0 all-gather.6
  46.0 30.8 all-gather.4

commit v2 on v0

v2 whole, which is shorter than its diff:
```python
import functools
import math

import jax
import jax.numpy as jnp
from jax import lax
from jax.experimental import pallas as pl
from jax.experimental.pallas import tpu as pltpu
from jax.sharding import PartitionSpec as P

BLOCK = 512
PART = 256
TILE = 128
HALF = 64
F32 = jnp.float32
BF16 = jnp.bfloat16
VMEM_LIMIT = 48 << 20
ANY = pl.BlockSpec(memory_space=pl.ANY)


def dot(left, right):
    return lax.dot_general(left, right, (((1,), (0,)), ((), ())), preferred_element_type=F32)


def dot_nt(left, right):
    return lax.dot_general(left, right, (((1,), (1,)), ((), ())), preferred_element_type=F32)


def call(kernel, name, grid, in_specs, outs, scratch=(), aliases=None, prefetch=0, flops=0, size=0):
    return pl.pallas_call(
        kernel,
        grid_spec=pltpu.PrefetchScalarGridSpec(
            num_scalar_prefetch=prefetch,
            grid=grid,
            in_specs=in_specs,
            out_specs=[spec for _, _, spec in outs],
            scratch_shapes=list(scratch),
        ),
        out_shape=[jax.ShapeDtypeStruct(shape, dtype) for shape, dtype, _ in outs],
        input_output_aliases=aliases or {},
        compiler_params=pltpu.CompilerParams(
            dimension_semantics=("arbitrary",) * len(grid), vmem_limit_bytes=VMEM_LIMIT
        ),
        cost_estimate=pl.CostEstimate(flops=flops, bytes_accessed=size, transcendentals=0),
        name=name,
    )


def onehot_rows(codes_row, entries):
    entry = lax.broadcasted_iota(jnp.int32, (entries, codes_row.shape[1]), 0)
    return jnp.where(entry == codes_row, 1.0, 0.0).astype(BF16)


def fold(array):
    rows, lanes = array.shape
    return jnp.sum(array.reshape(rows // 8, 8, lanes), axis=0)


def fold_max(array):
    rows, lanes = array.shape
    return jnp.max(array.reshape(rows // 8, 8, lanes), axis=0)


def count_kernel(codes_ref, total_ref, first_ref):
    heads, entries = total_ref.shape[0], total_ref.shape[2]
    levels = lax.broadcasted_iota(jnp.int32, (BLOCK, entries), 1)
    for h in range(heads):
        total = None
        for b in range(codes_ref.shape[0] // BLOCK):
            column = codes_ref[b * BLOCK : (b + 1) * BLOCK, h : h + 1]
            part = jnp.sum(fold(jnp.where(levels == column, 1.0, 0.0)), axis=0, keepdims=True)
            if b == 0:
                first_ref[h] = part
            total = part if total is None else total + part
        total_ref[h] = total


def own_counts(codes, entries):
    tokens, heads = codes.shape
    shape = (heads, 1, entries)
    spec = pl.BlockSpec(shape, lambda i: (0, 0, 0))
    return call(
        count_kernel, "own_counts", (1,),
        [pl.BlockSpec(codes.shape, lambda i: (0, 0))],
        [(shape, F32, spec), (shape, F32, spec)],
        size=1 << 20,
    )(codes)


def sum_kernel(codes_ref, value_ref, send_ref, first_ref):
    entries = first_ref.shape[1]
    total = None
    for b in range(codes_ref.shape[2] // BLOCK):
        span = slice(b * BLOCK, (b + 1) * BLOCK)
        part = dot(onehot_rows(codes_ref[0, :, span], entries), value_ref[span, :])
        if b == 0:
            first_ref[0] = part
        total = part if total is None else total + part
    for k in range(entries // HALF):
        send_ref[k] = total[k * HALF : (k + 1) * HALF].astype(BF16)


def own_sums(codes_rows, values, heads, entries):
    tokens = values.shape[0]
    slices = entries // HALF
    by_head = lambda h: (h, 0, 0)
    return call(
        sum_kernel, "own_sums", (heads,),
        [
            pl.BlockSpec((1, 1, tokens), by_head),
            pl.BlockSpec((tokens, TILE), lambda h: (0, h)),
        ],
        [
            ((heads * slices, HALF, TILE), BF16, pl.BlockSpec((slices, HALF, TILE), by_head)),
            ((heads, entries, TILE), F32, pl.BlockSpec((1, entries, TILE), by_head)),
        ],
        flops=1 << 30, size=4 << 20,
    )(codes_rows, values)


def prefix_kernel(in_ref, out_ref):
    running = jnp.zeros(in_ref.shape[1:], F32)
    for d in range(in_ref.shape[0]):
        out_ref[d] = running.astype(BF16)
        running = running + in_ref[d].astype(F32)


def suffix_kernel(in_ref, out_ref):
    running = jnp.zeros(in_ref.shape[1:], F32)
    for d in reversed(range(in_ref.shape[0])):
        out_ref[d] = running.astype(BF16)
        running = running + in_ref[d].astype(F32)


def total_kernel(in_ref, out_ref):
    running = jnp.zeros(in_ref.shape[1:], F32)
    for d in range(in_ref.shape[0]):
        running = running + in_ref[d].astype(F32)
    low = running.astype(BF16)
    for d in range(in_ref.shape[0]):
        out_ref[d] = low


def scanned(kernel, name, pieces):
    spec = pl.BlockSpec(pieces.shape, lambda i: (0, 0, 0))
    return call(
        kernel, name, (1,), [spec], [(pieces.shape, BF16, spec)], size=1 << 20
    )(pieces)[0]


def forward_kernel(block, me_ref, codes_ref, query_ref, book_ref, book_t_ref, all_ref, first_ref,
                   low_ref, keys_ref, rows_k, counts, scores):
    entries, width = book_ref.shape[1:]
    entry_tiles = entries // TILE
    factor = width ** -0.5 * math.log2(math.e)
    keys_t = dot(book_t_ref[0], onehot_rows(codes_ref[0], entries))
    keys_ref[0] = keys_t.astype(BF16)
    rows_k[:entries, :] = book_ref[0]
    rows_k[entries:, :] = keys_t.T.astype(BF16)
    number = jnp.zeros((1, entries), F32)
    for d in range(all_ref.shape[0]):
        number = number + jnp.where(d < me_ref[0], all_ref[d, 0], 0.0)
    if block > 0:
        number = number + first_ref[0]
    for i in range(entry_tiles):
        rows = slice(i * TILE, (i + 1) * TILE)
        counts[rows, :] = jnp.broadcast_to(number[:, rows], (TILE, TILE)).T
    causal = lax.broadcasted_iota(jnp.int32, (TILE, TILE), 1) >= lax.broadcasted_iota(
        jnp.int32, (TILE, TILE), 0
    )
    for n in range(BLOCK // PART):
        used = entries + PART * (n + 1)
        span = slice(n * PART, (n + 1) * PART)
        scores[n, :used, :] = dot_nt(rows_k[:used, :], query_ref[span, :])
    for n in range(BLOCK // PART):
        used = entries + PART * (n + 1)
        for j in range(PART // TILE):
            columns = slice(j * TILE, (j + 1) * TILE)
            target = slice(n * PART + j * TILE, n * PART + (j + 1) * TILE)
            pieces = range(entry_tiles + 2 * n + j + 1)
            top = jnp.full((8, TILE), -jnp.inf, F32)
            for i in pieces:
                rows = slice(i * TILE, (i + 1) * TILE)
                piece = scores[n, rows, columns]
                if i < entry_tiles:
                    piece = jnp.where(counts[rows, :] > 0.0, piece, -jnp.inf)
                    scores[n, rows, columns] = piece
                elif i == pieces[-1]:
                    piece = jnp.where(causal, piece, -jnp.inf)
                    scores[n, rows, columns] = piece
                top = jnp.maximum(top, fold_max(piece))
            top = jnp.max(top, axis=0, keepdims=True)
            total = jnp.zeros((8, TILE), F32)
            for i in pieces:
                rows = slice(i * TILE, (i + 1) * TILE)
                piece = jnp.exp2((scores[n, rows, columns] - top) * factor)
                scores[n, rows, columns] = piece
                if i < entry_tiles:
                    piece = piece * counts[rows, :]
                total = total + fold(piece)
            inverse = 1.0 / jnp.sum(total, axis=0, keepdims=True)
            for i in pieces:
                rows = slice(i * TILE, (i + 1) * TILE)
                low_ref[0, rows, target] = (scores[n, rows, columns] * inverse).astype(BF16)
            if j == 0:
                low_ref[0, used - TILE : used, target] = jnp.zeros((TILE, TILE), BF16)


def forward(block, me, codes_rows, queries, book, book_t, every, first):
    heads, entries, width = book.shape
    both = entries + BLOCK
    by_head = lambda h, *_: (h, 0, 0)
    row = pl.BlockSpec((1, 1, entries), by_head)
    return call(
        functools.partial(forward_kernel, block), f"forward_{block}", (heads,),
        [
            pl.BlockSpec((1, 1, BLOCK), lambda h, *_: (h, 0, block)),
            pl.BlockSpec((BLOCK, width), lambda h, *_: (block, h)),
            pl.BlockSpec((1, entries, width), by_head),
            pl.BlockSpec((1, width, entries), by_head),
            pl.BlockSpec((every.shape[0], 1, 1, entries), lambda h, *_: (0, h, 0, 0)),
            row,
        ],
        [
            ((heads, both, BLOCK), BF16, pl.BlockSpec((1, both, BLOCK), by_head)),
            ((heads, width, BLOCK), BF16, pl.BlockSpec((1, width, BLOCK), by_head)),
        ],
        [
            pltpu.VMEM((both, width), BF16),
            pltpu.VMEM((entries, TILE), F32),
            pltpu.VMEM((2, both, PART), F32),
        ],
        prefetch=1, flops=3 << 30, size=8 << 20,
    )(me, codes_rows, queries, book, book_t, every, first)


def values_kernel(block, *refs):
    (_, own_ref, left_ref, right_ref, low_half_ref, high_half_ref,
     own_w, left_w, right_w, far_w, probs_ref) = refs[:11]
    if block == 0:
        dout_ref, local_ref, part_ref, dout = refs[11:]
    else:
        part0_ref, _, dout_ref, local_ref, part_ref, send_ref, dout = refs[11:]
    head = pl.program_id(0)
    entries, width = part_ref.shape[1:]

    @pl.when(head == 0)
    def _():
        for n in range(BLOCK // PART):
            span = slice(n * PART, (n + 1) * PART)
            far = low_half_ref[...] if n == 0 else high_half_ref[...]
            total = dot_nt(own_ref[span, :], own_w[...]) + dot_nt(left_ref[span, :], left_w[...])
            total = total + dot_nt(right_ref[span, :], right_w[...]) + dot_nt(far, far_w[...])
            for h in range(dout.shape[0]):
                dout[h, span, :] = total[:, h * width : (h + 1) * width].astype(BF16)

    mine = dout[head]
    dout_ref[0] = mine
    used = entries + PART
    low = dot(probs_ref[0, :used, :PART], mine[:PART])
    high = dot(probs_ref[0, :, PART:], mine[PART:])
    local_ref[:PART, :] = low[entries:] + high[entries:used]
    local_ref[PART:, :] = high[used:]
    part = low[:entries] + high[:entries]
    part_ref[0] = part
    if block > 0:
        part = part + part0_ref[0]
        for k in range(entries // HALF):
            send_ref[k] = part[k * HALF : (k + 1) * HALF].astype(BF16)


def value_grads(block, me, pieces, weight, probs, extra=()):
    heads, both, _ = probs.shape
    entries = both - BLOCK
    width = weight.shape[0] // heads
    columns = weight.shape[1] // 4
    tokens = 2 * BLOCK
    slices = entries // HALF
    by_head = lambda h, *_: (h, 0, 0)
    per_head = pl.BlockSpec((1, entries, width), by_head)
    full = lambda h, *_: (0, 0)

    def chunk(offset):
        return pl.BlockSpec(
            (weight.shape[0], columns), lambda h, me: (0, lax.rem(me[0] + offset, 4))
        )

    in_specs = [pl.BlockSpec((BLOCK, columns), lambda h, *_: (block, 0))]
    in_specs += [pl.BlockSpec(piece.shape, full) for piece in pieces[1:]]
    in_specs += [chunk(0), chunk(3), chunk(1), chunk(2), pl.BlockSpec((1, both, BLOCK), by_head)]
    outs = [
        ((heads, BLOCK, width), BF16, pl.BlockSpec((1, BLOCK, width), by_head)),
        ((tokens, heads * width), F32, pl.BlockSpec((BLOCK, width), lambda h, *_: (block, h))),
        ((heads, entries, width), F32, per_head),
    ]
    aliases = {}
    if block > 0:
        in_specs += [per_head, ANY]
        aliases = {12: 1}
        outs.append(
            ((heads * slices, HALF, width), BF16, pl.BlockSpec((slices, HALF, width), by_head))
        )
    return call(
        functools.partial(values_kernel, block), f"value_grads_{block}", (heads,), in_specs, outs,
        [pltpu.VMEM((heads, BLOCK, width), BF16)],
        aliases=aliases, prefetch=1, flops=3 << 30, size=12 << 20,
    )(me, *pieces, *[weight] * 4, probs, *extra)


def scores_kernel(block, me_ref, *refs):
    (codes_ref, query_ref, value_ref, dout_ref, probs_ref, keys_ref, book_t_ref, prefix_ref,
     all_ref) = refs[:9]
    if block == 0:
        (grad_query_ref, code_ref, hot, rows_v, counts, grads, score_grad, key_grad,
         wide_t) = refs[9:]
    else:
        (first_ref, first_count_ref, code0_ref, _, grad_query_ref, send_ref,
         hot, rows_v, counts, grads, score_grad, key_grad, wide_t) = refs[9:]
    width, entries = book_t_ref.shape[1:]
    entry_tiles = entries // TILE
    scale = width ** -0.5
    hot[...] = onehot_rows(codes_ref[0], entries)
    wide_t[:, :entries] = book_t_ref[0]
    wide_t[:, entries:] = keys_ref[0]
    sums = prefix_ref[...].reshape(entries, width)
    if block > 0:
        sums = (sums.astype(F32) + first_ref[0]).astype(BF16)
    rows_v[:entries, :] = sums
    rows_v[entries:, :] = value_ref[...]
    number = jnp.zeros((1, entries), F32)
    for d in range(all_ref.shape[0]):
        number = number + jnp.where(d < me_ref[0], all_ref[d, 0], 0.0)
    if block > 0:
        number = number + first_count_ref[0]
    for i in range(entry_tiles):
        rows = slice(i * TILE, (i + 1) * TILE)
        counts[rows, :] = jnp.broadcast_to(number[:, rows], (TILE, TILE)).T
    for n in range(BLOCK // PART):
        used = entries + PART * (n + 1)
        span = slice(n * PART, (n + 1) * PART)
        grads[n, :used, :] = dot_nt(rows_v[:used, :], dout_ref[0, span, :])
    sums_k = None
    for n in range(BLOCK // PART):
        used = entries + PART * (n + 1)
        span = slice(n * PART, (n + 1) * PART)
        for j in range(PART // TILE):
            columns = slice(j * TILE, (j + 1) * TILE)
            source = slice(n * PART + j * TILE, n * PART + (j + 1) * TILE)
            pieces = range(entry_tiles + 2 * n + j + 1)
            delta = jnp.zeros((8, TILE), F32)
            for i in pieces:
                rows = slice(i * TILE, (i + 1) * TILE)
                delta = delta + fold(
                    probs_ref[0, rows, source].astype(F32) * grads[n, rows, columns]
                )
            delta = jnp.sum(delta, axis=0, keepdims=True) * scale
            for i in pieces:
                rows = slice(i * TILE, (i + 1) * TILE)
                shift = delta
                if i < entry_tiles:
                    shift = delta * counts[rows, :]
                piece = grads[n, rows, columns] * scale - shift
                piece = probs_ref[0, rows, source].astype(F32) * piece
                score_grad[n, rows, columns] = piece.astype(BF16)
            if j == 0:
                score_grad[n, used - TILE : used, columns] = jnp.zeros((TILE, TILE), BF16)
        result = dot(score_grad[n, :used, :], query_ref[span, :])
        grad_t = dot(wide_t[:, :used], score_grad[n, :used, :])
        grad_query_ref[span, :] = grad_t.T.astype(BF16)
        if n == 0:
            sums_k = result
        else:
            middle = entries + PART
            key_grad[:PART, :] = (sums_k[entries:] + result[entries:middle]).astype(BF16)
            key_grad[PART:, :] = result[middle:].astype(BF16)
            code = sums_k[:entries] + result[:entries]
    code = code + dot(hot[...], key_grad[...])
    if block == 0:
        code_ref[0] = code
    else:
        code = code + code0_ref[0]
        for k in range(entries // HALF):
            send_ref[k] = code[k * HALF : (k + 1) * HALF].astype(BF16)


def score_grads(block, me, codes_rows, queries, values, dout, probs, keys_t, book_t, prefix, every,
                extra=()):
    heads, width, entries = book_t.shape
    both = entries + BLOCK
    slices = entries // HALF
    by_head = lambda h, *_: (h, 0, 0)
    rows_of = lambda h, *_: (block, h)
    row = pl.BlockSpec((1, 1, entries), by_head)
    per_head = pl.BlockSpec((1, entries, width), by_head)
    in_specs = [
        pl.BlockSpec((1, 1, BLOCK), lambda h, *_: (h, 0, block)),
        pl.BlockSpec((BLOCK, width), rows_of),
        pl.BlockSpec((BLOCK, width), rows_of),
        pl.BlockSpec((1, BLOCK, width), by_head),
        pl.BlockSpec((1, both, BLOCK), by_head),
        pl.BlockSpec((1, width, BLOCK), by_head),
        pl.BlockSpec((1, width, entries), by_head),
        pl.BlockSpec((slices, HALF, width), by_head),
        pl.BlockSpec((every.shape[0], 1, 1, entries), lambda h, *_: (0, h, 0, 0)),
    ]
    outs = [(queries.shape, BF16, pl.BlockSpec((BLOCK, width), rows_of))]
    aliases = {}
    if block == 0:
        outs.append(((heads, entries, width), F32, per_head))
    else:
        in_specs += [per_head, row, per_head, ANY]
        aliases = {13: 0}
        outs.append(
            ((heads * slices, HALF, width), BF16, pl.BlockSpec((slices, HALF, width), by_head))
        )
    return call(
        functools.partial(scores_kernel, block), f"score_grads_{block}", (heads,), in_specs, outs,
        [
            pltpu.VMEM((entries, BLOCK), BF16),
            pltpu.VMEM((both, width), BF16),
            pltpu.VMEM((entries, TILE), F32),
            pltpu.VMEM((2, both, PART), F32),
            pltpu.VMEM((2, both, PART), BF16),
            pltpu.VMEM((BLOCK, width), BF16),
            pltpu.VMEM((width, both), BF16),
        ],
        aliases=aliases, prefetch=1, flops=5 << 30, size=12 << 20,
    )(me, codes_rows, queries, values, dout, probs, keys_t, book_t, prefix, every, *extra)


def finish_kernel(codes_ref, local_ref, later_ref, part_ref, out_ref):
    heads, entries, width = part_ref.shape
    slices = entries // HALF
    first = pl.program_id(0) == 0
    levels = lax.broadcasted_iota(jnp.int32, (BLOCK, entries), 1)
    for h in range(heads):
        later = later_ref[h * slices : (h + 1) * slices].reshape(entries, width)
        total = (later.astype(F32) + jnp.where(first, part_ref[h], 0.0)).astype(BF16)
        hot = jnp.where(levels == codes_ref[:, h : h + 1], 1.0, 0.0).astype(BF16)
        columns = slice(h * width, (h + 1) * width)
        out_ref[:, columns] = (local_ref[:, columns] + dot(hot, total)).astype(BF16)


def finish(codes, local, later, part):
    heads, entries, width = part.shape
    whole = lambda b: (0, 0, 0)
    rows = pl.BlockSpec((BLOCK, heads * width), lambda b: (b, 0))
    return call(
        finish_kernel, "finish_values", (local.shape[0] // BLOCK,),
        [
            pl.BlockSpec((BLOCK, heads), lambda b: (b, 0)),
            rows,
            pl.BlockSpec(later.shape, whole),
            pl.BlockSpec(part.shape, whole),
        ],
        [(local.shape, BF16, rows)],
        flops=1 << 30, size=4 << 20,
    )(codes, local, later, part)[0]


def ring_pieces(array):
    count = lax.axis_size("head")
    up = [(i, (i + 1) % count) for i in range(count)]
    down = [(i, (i - 1) % count) for i in range(count)]
    left = lax.ppermute(array, "head", up)
    right = lax.ppermute(array, "head", down)
    half = array.shape[0] // 2
    return left, right, lax.ppermute(left[:half], "head", up), lax.ppermute(right[half:], "head", down)


def per_device(queries, values, codes, codebook, out_weight, grad_out):
    heads, entries, width = codebook.shape
    exchange = functools.partial(
        lax.all_to_all, axis_name="seq", split_axis=0, concat_axis=0, tiled=True
    )
    me_seq = lax.axis_index("seq").astype(jnp.int32).reshape(1)
    me_head = lax.axis_index("head").astype(jnp.int32).reshape(1)
    pieces = [
        (grad_out, *ring_pieces(grad_out[b * BLOCK : (b + 1) * BLOCK])) for b in range(2)
    ]
    total, first_count = own_counts(codes, entries)
    every = exchange(jnp.broadcast_to(total[None], (lax.axis_size("seq"), *total.shape)))
    codes_rows = codes.T.reshape(heads, 1, -1)
    book_t = jnp.swapaxes(codebook, 1, 2)
    send, first = own_sums(codes_rows, values, heads, entries)
    prefix = exchange(scanned(prefix_kernel, "prefix_scan", exchange(send)))
    probs, keys = zip(*[
        forward(b, me_seq, codes_rows, queries, codebook, book_t, every, first_count)
        for b in range(2)
    ])
    dout0, local, part0 = value_grads(0, me_head, pieces[0], out_weight, probs[0])
    dout1, local, part1, send = value_grads(
        1, me_head, pieces[1], out_weight, probs[1], (part0, local)
    )
    later = exchange(scanned(suffix_kernel, "suffix_scan", exchange(send)))
    grad_query, code0 = score_grads(
        0, me_seq, codes_rows, queries, values, dout0, probs[0], keys[0], book_t, prefix, every
    )
    grad_query, send = score_grads(
        1, me_seq, codes_rows, queries, values, dout1, probs[1], keys[1], book_t, prefix, every,
        (first, first_count, code0, grad_query),
    )
    grad_book = exchange(scanned(total_kernel, "total_scan", exchange(send)))
    grad_values = finish(codes, local, later, part1)
    return grad_query, grad_values, grad_book.reshape(codebook.shape).astype(F32)


def solution(mesh):
    rows = P("seq", "head")
    return jax.shard_map(
        per_device,
        mesh=mesh,
        in_specs=(rows, rows, rows, P("head", None, None), P("head", None), rows),
        out_specs=(rows, rows, P("head", None, None)),
        check_vma=False,
    )
```

time: 360 us -> 172 us (0.48); the launches traced: 355 us -> 170 us
  waiting for transfers between devices: 165 us -> 29.4 us
  matrix products: 74.1 us -> 0 us
  Pallas kernels: 0 us -> 50.3 us
  starting transfers between devices: 12.1 us -> 61.3 us
  blocking collectives: 33.9 us -> 0 us
  other arithmetic: 34.9 us -> 2.08 us
  between operations: 15.1 us -> 0.95 us
  local copies, waits for them, and re-layouts: 19.7 us -> 26.4 us
    all_gather x7 -> x0, waiting for transfers between devices: 152 us -> none  [the longest x6 131 us: carried_in(): pieces = jax.tree.map(lambda part: lax.all_gather(part, axis), subtotal)]
    dot_general x31 -> x0, matrix products: 74.1 us -> none  [the longest x2 9.15 us: attend_block(): jnp.einsum('the,uhe->htu', dout, value, preferred_element_type=jnp.float32)]
    pallas_call x0 -> x12, Pallas kernels: none -> 50.3 us  [the longest x2 18.4 us: score_grads(): call(functools.partial(scores_kernel, block), f'score_grads_{block}', (he...]
    all_to_all x2 -> x7, starting transfers between devices: 11.1 us -> 50.1 us  [the longest x2 15.9 us: per_device(): prefix = exchange(scanned(prefix_kernel, 'prefix_scan', exchange(send)))]
    all_gather x3 -> x0, blocking collectives: 22.7 us -> none  [carried_in(): pieces = jax.tree.map(lambda part: lax.all_gather(part, axis), subtotal)]
    add x9 -> x0, other arithmetic: 16.4 us -> none  [the longest x7 16.4 us: add_tree(): return jax.tree.map(jnp.add, earlier, later)]
    all_to_all x2 -> x7, waiting for transfers between devices: 12.4 us -> 28.6 us  [the longest x2 18.9 us: per_device(): grad_book = exchange(scanned(total_kernel, 'total_scan', exchange(send)))]
    ppermute x0 -> x8, starting transfers between devices: none -> 11.2 us  [the longest x2 5.97 us: ring_pieces(): lax.ppermute(right[half:], 'head', down)]
  transfers between devices with their start and end apart: 9 -> 15, of which waited for: 7 -> 4; matrix products, arithmetic and copies ran while one was open for 28% -> 3% of each run, Pallas kernels for 0% -> 29%
where the time goes in v2:
time: 172 us; the launch traced here: 170 us
  starting transfers between devices  61.3 us (36%)
  Pallas kernels  50.3 us (29%)
  waiting for transfers between devices  29.4 us (17%)
  local copies, waits for them, and re-layouts  26.4 us (15%)
  other arithmetic  2.08 us (1%)
    unnamed x67, local copies, waits for them, and re-layouts  21 us
    all_to_all x2, waiting for transfers between devices, per_device(): grad_book = exchange(scanned(total_kernel, 'total_scan', exchange(send)))  18.9 us
    pallas_call x2, Pallas kernels, score_grads(): call(functools.partial(scores_kernel, block), f'score_grads_{block}', (he...  18.4 us
    all_to_all x2, starting transfers between devices, per_device(): prefix = exchange(scanned(prefix_kernel, 'prefix_scan', exchange(send)))  15.9 us
    pallas_call x2, Pallas kernels, value_grads(): call(functools.partial(values_kernel, block), f'value_grads_{block}', (he...  14 us
    all_to_all x2, starting transfers between devices, per_device(): later = exchange(scanned(suffix_kernel, 'suffix_scan', exchange(send)))  12.5 us
    all_to_all x2, starting transfers between devices, per_device(): grad_book = exchange(scanned(total_kernel, 'total_scan', exchange(send)))  12.1 us
    pallas_call x2, Pallas kernels, forward(): call(functools.partial(forward_kernel, block), f'forward_{block}', (heads...  10.6 us
  transfers between devices with their start and end apart: 15, of which 4 were waited for; matrix products, arithmetic and copies ran while one was open for 3% of the time, Pallas kernels for 29%

profile of v2, /device:TPU:1, one launch (start us, length us, event | category | flops | bytes accessed | tf_op | source)
XLA Modules:
  0.0 170.5 jit_solution(16381165041391258649)
XLA Ops:
  0.7 0.0 copy-start.6
  0.7 1.0 copy.12.codes_ref
  1.7 0.9 own_counts.1
  2.6 0.9 broadcast_in_dim.9
  3.5 9.6 %all-to-all-start = ((f32[32,4,1,512]{3,2,1,0:T(1,128)}), f32[32,4,1,512]{3,2,1,0:T(1,128)S(1)}, u32[]{:S(2)}, u32[]{:S(2)}) async-start(f32[32,4,1,512]{3,2,1,0:T(1,128)} %broadcast_in_dim.9), calls=%async_computation | async-start | bytes 524288 | tf_op jit(solution)/shard_map/all_to_all | solution.py:482
  13.1 1.0 fusion
  14.2 2.5 %collective-permute-start.5 = (bf16[512,512]{1,0:T(8,128)(2,1)}, bf16[512,512]{1,0:T(8,128)(2,1)S(1)}, u32[]{:S(2)}, u32[]{:S(2)}) collective-permute-start(bf16[512,512]{1,0:T(8,128)(2,1)} %get-tuple-element.41), channel_id=1, source_target_pairs={{0,3},{1,0},{2,1},{3,2},{4,7},{5,4},{6,5},{7,6},{8,11},{9,8},{10,9... | collective-permute-start | bytes 1572872 | tf_op jit(solution)/shard_map/ppermute | solution.py:466
  16.6 0.0 collective-permute-start.4
  16.6 2.7 %collective-permute-start.1 = (bf16[512,512]{1,0:T(8,128)(2,1)}, bf16[512,512]{1,0:T(8,128)(2,1)}, u32[]{:S(2)}, u32[]{:S(2)}) collective-permute-start(bf16[512,512]{1,0:T(8,128)(2,1)} %get-tuple-element.42), channel_id=1, source_target_pairs={{0,3},{1,0},{2,1},{3,2},{4,7},{5,4},{6,5},{7,6},{8,11},{9,8},{10,9... | collective-permute-start | bytes 1572872 | tf_op jit(solution)/shard_map/ppermute | solution.py:466
  19.3 1.0 copy.11
  20.4 1.2 copy-done.17
  21.6 2.0 %own_sums.1 = (bf16[32,64,128]{2,1,0:T(8,128)(2,1)S(1)}, f32[4,512,128]{2,1,0:T(8,128)S(1)}) custom-call(s32[4,1,1024]{2,1,0:T(1,128)S(1)} %reshape.22.codes_ref.refs_0_, bf16[1024,512]{1,0:T(8,128)(2,1)S(1)} %copy-done.17), custom_call_target="tpu_custom_call" | custom-call | flops 1073741824 | bytes 4194304 | tf_op jit(solution)/shard_map/own_sums/pallas_call | solution.py:107
  23.6 0.8 copy-done.10
  24.4 1.0 copy-done.24
  25.4 0.0 all-to-all-done.all_ref.refs_8_
  25.4 8.2 %all-to-all-start.1 = ((bf16[32,64,128]{2,1,0:T(8,128)(2,1)}), bf16[32,64,128]{2,1,0:T(8,128)(2,1)S(1)}, u32[]{:S(2)}, u32[]{:S(2)}) async-start(bf16[32,64,128]{2,1,0:T(8,128)(2,1)} %copy-done.10), calls=%async_computation.1 | async-start | bytes 1048576 | tf_op jit(solution)/shard_map/all_to_all | solution.py:486
  33.6 0.0 copy-start.7
  33.6 1.0 copy-done.7
  34.7 1.0 copy-done.8
  35.7 1.2 copy-done.14
  36.9 5.3 %forward_0.1 = (bf16[4,1024,512]{2,1,0:T(8,128)(2,1)}, bf16[4,128,512]{2,1,0:T(8,128)(2,1)S(1)}) custom-call(s32[1]{0:T(128)} %bitcast.me_ref, s32[4,1,1024]{2,1,0:T(1,128)S(1)} %reshape.22.codes_ref.refs_0_, bf16[1024,512]{1,0:T(8,128)(2,1)S(1)} %copy-done.14, bf16[4,512,128]{2,1,0:T(8,128)(2,1)S(1)} %copy-done.7, bf16[4,128,512]{2,1,0:T(8,128)(2,1)S(1)} %bitcast.11, ...), custom_call_target="tpu_custom_call" | custom-call | flops 3221225472 | bytes 8388608 | tf_op jit(solution)/shard_map/forward_0/pallas_call | solution.py:214
  42.2 0.0 collective-permute-done.5.refs_3_
  42.2 0.8 slice.27
  43.0 3.0 %collective-permute-start.7 = (bf16[256,512]{1,0:T(8,128)(2,1)}, bf16[256,512]{1,0:T(8,128)(2,1)S(1)}, u32[]{:S(2)}, u32[]{:S(2)}) collective-permute-start(bf16[256,512]{1,0:T(8,128)(2,1)} %slice.27), channel_id=1, source_target_pairs={{0,3},{1,0},{2,1},{3,2},{4,7},{5,4},{6,5},{7,6},{8,11},{9,8},{10,9... | collective-permute-start | bytes 786440 | tf_op jit(solution)/shard_map/ppermute | solution.py:468
  45.9 0.7 slice.26
  46.7 0.9 copy-done.12
  47.6 5.3 %forward_1.1 = (bf16[4,1024,512]{2,1,0:T(8,128)(2,1)}, bf16[4,128,512]{2,1,0:T(8,128)(2,1)S(1)}) custom-call(s32[1]{0:T(128)} %bitcast.me_ref, s32[4,1,1024]{2,1,0:T(1,128)S(1)} %reshape.22.codes_ref.refs_0_, bf16[1024,512]{1,0:T(8,128)(2,1)S(1)} %copy-done.14, bf16[4,512,128]{2,1,0:T(8,128)(2,1)S(1)} %copy-done.7, bf16[4,128,512]{2,1,0:T(8,128)(2,1)S(1)} %bitcast.12, ...), custom_call_target="tpu_custom_call" | custom-call | flops 3221225472 | bytes 8388608 | tf_op jit(solution)/shard_map/forward_1/pallas_call | solution.py:214
  53.0 0.8 copy-done.27
  53.8 0.9 prefix_scan.1
  54.6 7.7 %all-to-all-start.2 = ((bf16[32,64,128]{2,1,0:T(8,128)(2,1)}), bf16[32,64,128]{2,1,0:T(8,128)(2,1)}, u32[]{:S(2)}, u32[]{:S(2)}) async-start(bf16[32,64,128]{2,1,0:T(8,128)(2,1)} %prefix_scan.1), calls=%async_computation.2 | async-start | bytes 1048576 | tf_op jit(solution)/shard_map/all_to_all | solution.py:486
  62.4 1.0 slice.25
  63.4 3.0 %collective-permute-start.3 = (bf16[256,512]{1,0:T(8,128)(2,1)S(1)}, bf16[256,512]{1,0:T(8,128)(2,1)S(1)}, u32[]{:S(2)}, u32[]{:S(2)}) collective-permute-start(bf16[256,512]{1,0:T(8,128)(2,1)S(1)} %slice.25), channel_id=1, source_target_pairs={{0,3},{1,0},{2,1},{3,2},{4,7},{5,4},{6,5},{7,6},{8,11},{9,8},{10,9... | collective-permute-start | bytes 786440 | tf_op jit(solution)/shard_map/ppermute | solution.py:468
  66.4 1.0 slice.24
  67.3 0.1 collective-permute-start.2
  67.5 6.8 %value_grads_0.1 = (bf16[4,512,128]{2,1,0:T(8,128)(2,1)S(1)}, f32[1024,512]{1,0:T(8,128)}, f32[4,512,128]{2,1,0:T(8,128)S(1)}) custom-call(s32[1]{0:T(128)} %bitcast.2.refs_0_, bf16[1024,512]{1,0:T(8,128)(2,1)S(1)} %copy-done, bf16[512,512]{1,0:T(8,128)(2,1)S(1)} %collective-permute-done.4.refs_2_, bf16[512,512]{1,0:T(8,128)(2,1)S(1)} %collective-permute-done.5.refs_3_, ...), custom_call_target="tpu_custom_call" | custom-call | flops 3221225472 | bytes 12582912 | tf_op jit(solution)/shard_map/value_grads_0/pallas_call | solution.py:303
  74.2 0.8 copy-done.22
  75.0 0.9 collective-permute-done.2.refs_4_
  75.9 7.2 %value_grads_1.1 = (bf16[4,512,128]{2,1,0:T(8,128)(2,1)S(1)}, f32[1024,512]{1,0:T(8,128)}, f32[4,512,128]{2,1,0:T(8,128)S(1)}, bf16[32,64,128]{2,1,0:T(8,128)(2,1)}) custom-call(s32[1]{0:T(128)} %bitcast.2.refs_0_, bf16[1024,512]{1,0:T(8,128)(2,1)S(1)} %copy-done, bf16[512,512]{1,0:T(8,128)(2,1)} %collective-permute-done.refs_2_, ...), custom_call_target="tpu_custom_call", output_to_operand_aliasing={{1}: (12, {})} | custom-call | flops 3221225472 | bytes 12582912 | tf_op jit(solution)/shard_map/value_grads_1/pallas_call | solution.py:303
  83.1 1.0 copy-done.4
  84.0 0.8 copy-done.20
  84.9 8.5 %all-to-all-start.3 = ((bf16[32,64,128]{2,1,0:T(8,128)(2,1)}), bf16[32,64,128]{2,1,0:T(8,128)(2,1)S(1)}, u32[]{:S(2)}, u32[]{:S(2)}) async-start(bf16[32,64,128]{2,1,0:T(8,128)(2,1)} %get-tuple-element.38), calls=%async_computation.3 | async-start | bytes 1048576 | tf_op jit(solution)/shard_map/all_to_all | solution.py:495
  93.4 0.0 copy-start.15
  93.4 1.2 copy-done.15
  94.6 1.2 copy-done.18
  95.8 1.0 copy-done.23
  96.9 1.0 copy-done.30
  97.9 8.9 %score_grads_0.1 = (bf16[1024,512]{1,0:T(8,128)(2,1)}, f32[4,512,128]{2,1,0:T(8,128)S(1)}) custom-call(s32[1]{0:T(128)} %bitcast.me_ref, s32[4,1,1024]{2,1,0:T(1,128)S(1)} %reshape.22.codes_ref.refs_0_, bf16[1024,512]{1,0:T(8,128)(2,1)S(1)} %copy-done.15, bf16[1024,512]{1,0:T(8,128)(2,1)S(1)} %copy-done.18, bf16[4,512,128]{2,1,0:T(8,128)(2,1)S(1)} %copy-done.23, ...), custom_call_target="tpu_custom_call" | custom-call | flops 5368709120 | bytes 12582912 | tf_op jit(solution)/shard_map/score_grads_0/pallas_call | solution.py:416
  106.8 1.0 copy-done.26
  107.8 9.5 %score_grads_1.1 = (bf16[1024,512]{1,0:T(8,128)(2,1)}, bf16[32,64,128]{2,1,0:T(8,128)(2,1)}) custom-call(s32[1]{0:T(128)} %bitcast.me_ref, s32[4,1,1024]{2,1,0:T(1,128)S(1)} %reshape.22.codes_ref.refs_0_, bf16[1024,512]{1,0:T(8,128)(2,1)S(1)} %copy-done.16, bf16[1024,512]{1,0:T(8,128)(2,1)S(1)} %copy-done.19, ...), custom_call_target="tpu_custom_call", output_to_operand_aliasing={{0}: (13, {})} | custom-call | flops 5368709120 | bytes 12582912 | tf_op jit(solution)/shard_map/score_grads_1/pallas_call | solution.py:416
  117.3 7.4 %all-to-all-start.5 = ((bf16[32,64,128]{2,1,0:T(8,128)(2,1)}), bf16[32,64,128]{2,1,0:T(8,128)(2,1)}, u32[]{:S(2)}, u32[]{:S(2)}) async-start(bf16[32,64,128]{2,1,0:T(8,128)(2,1)} %get-tuple-element.40), calls=%async_computation.5 | async-start | bytes 1048576 | tf_op jit(solution)/shard_map/all_to_all | solution.py:503
  124.8 0.1 suffix_scan.1
  124.9 0.0 copy-start.3
  124.9 0.8 copy-done.3
  125.7 10.7 %all-to-all-done.5.in_ref = bf16[32,64,128]{2,1,0:T(8,128)(2,1)} async-done(((bf16[32,64,128]{2,1,0:T(8,128)(2,1)}), bf16[32,64,128]{2,1,0:T(8,128)(2,1)}, u32[]{:S(2)}, u32[]{:S(2)}) %all-to-all-start.5) | async-done | bytes 524320 | tf_op jit(solution)/shard_map/all_to_all | solution.py:503
  136.4 4.0 %all-to-all-start.4 = ((bf16[32,64,128]{2,1,0:T(8,128)(2,1)}), bf16[32,64,128]{2,1,0:T(8,128)(2,1)S(1)}, u32[]{:S(2)}, u32[]{:S(2)}) async-start(bf16[32,64,128]{2,1,0:T(8,128)(2,1)} %copy-done.3), calls=%async_computation.4 | async-start | bytes 1048576 | tf_op jit(solution)/shard_map/all_to_all | solution.py:495
  140.3 1.1 total_scan.1
  141.5 0.0 copy-start.2
  141.5 0.8 copy-done.2
  142.3 9.7 %all-to-all-done.4.later_ref = bf16[32,64,128]{2,1,0:T(8,128)(2,1)S(1)} async-done(((bf16[32,64,128]{2,1,0:T(8,128)(2,1)}), bf16[32,64,128]{2,1,0:T(8,128)(2,1)S(1)}, u32[]{:S(2)}, u32[]{:S(2)}) %all-to-all-start.4) | async-done | bytes 524320 | tf_op jit(solution)/shard_map/all_to_all | solution.py:495
  152.0 4.6 %all-to-all-start.6 = ((bf16[32,64,128]{2,1,0:T(8,128)(2,1)}), bf16[32,64,128]{2,1,0:T(8,128)(2,1)}, u32[]{:S(2)}, u32[]{:S(2)}) async-start(bf16[32,64,128]{2,1,0:T(8,128)(2,1)} %copy-done.2), calls=%async_computation.6 | async-start | bytes 1048576 | tf_op jit(solution)/shard_map/all_to_all | solution.py:503
  156.7 1.2 copy-done.5
  157.9 2.3 %finish_values.1 = bf16[1024,512]{1,0:T(8,128)(2,1)} custom-call(s32[1024,4]{1,0:T(8,128)S(1)} %copy.12.codes_ref, f32[1024,512]{1,0:T(8,128)S(1)} %copy-done.1, bf16[32,64,128]{2,1,0:T(8,128)(2,1)S(1)} %all-to-all-done.4.later_ref, f32[4,512,128]{2,1,0:T(8,128)S(1)} %copy-done.5), custom_call_target="tpu_custom_call" | custom-call | flops 1073741824 | bytes 4194304 | tf_op jit(solution)/shard_map/finish_values/pallas_call | solution.py:448
  160.2 8.2 %all-to-all-done.6 = bf16[32,64,128]{2,1,0:T(8,128)(2,1)} async-done(((bf16[32,64,128]{2,1,0:T(8,128)(2,1)}), bf16[32,64,128]{2,1,0:T(8,128)(2,1)}, u32[]{:S(2)}, u32[]{:S(2)}) %all-to-all-start.6) | async-done | bytes 524320 | tf_op jit(solution)/shard_map/all_to_all | solution.py:503
  168.4 2.1 %bitcast_convert_fusion = f32[4,512,128]{2,1,0:T(8,128)} fusion(bf16[4,512,128]{2,1,0:T(8,128)(2,1)} %bitcast.10), kind=kLoop, calls=%fused_computation | loop fusion | flops 262144 | bytes 1572864 | tf_op jit(solution)/shard_map/convert_element_type | solution.py:505
  (53 shorter events, 0.1 us)
Async XLA Ops:
  0.6 18.7 %copy-start.31 = (s32[1024,4]{0,1:T(4,128)S(1)}, s32[1024,4]{0,1:T(4,128)}, u32[]{:S(2)}) copy-start(s32[1024,4]{0,1:T(4,128)} %param.8) | copy-start | bytes 49156
  0.6 12.5 %copy-start = (bf16[1024,512]{1,0:T(8,128)(2,1)S(1)}, bf16[1024,512]{1,0:T(8,128)(2,1)}, u32[]{:S(2)}) copy-start(bf16[1024,512]{1,0:T(8,128)(2,1)} %refs_1_.5) | copy-start | bytes 3145732
  0.7 18.7 %copy-start.6 = (bf16[4,512,128]{2,1,0:T(8,128)(2,1)S(1)}, bf16[4,512,128]{2,1,0:T(8,128)(2,1)}, u32[]{:S(2)}) copy-start(bf16[4,512,128]{2,1,0:T(8,128)(2,1)} %book_ref.3) | copy-start | bytes 1572868
  3.5 21.9 %all-to-all-start = ((f32[32,4,1,512]{3,2,1,0:T(1,128)}), f32[32,4,1,512]{3,2,1,0:T(1,128)S(1)}, u32[]{:S(2)}, u32[]{:S(2)}) async-start(f32[32,4,1,512]{3,2,1,0:T(1,128)} %broadcast_in_dim.9), calls=%async_computation | async-start | bytes 524288 | tf_op jit(solution)/shard_map/all_to_all | solution.py:482
  14.2 28.0 %collective-permute-start.5 = (bf16[512,512]{1,0:T(8,128)(2,1)}, bf16[512,512]{1,0:T(8,128)(2,1)S(1)}, u32[]{:S(2)}, u32[]{:S(2)}) collective-permute-start(bf16[512,512]{1,0:T(8,128)(2,1)} %get-tuple-element.41), channel_id=1, source_target_pairs={{0,3},{1,0},{2,1},{3,2},{4,7},{5,4},{6,5},{7,6},{8,11},{9,8},{10,9... | collective-permute-start | bytes 1572872 | tf_op jit(solution)/shard_map/ppermute | solution.py:466
  16.6 29.3 %collective-permute-start.4 = (bf16[512,512]{1,0:T(8,128)(2,1)}, bf16[512,512]{1,0:T(8,128)(2,1)S(1)}, u32[]{:S(2)}, u32[]{:S(2)}) collective-permute-start(bf16[512,512]{1,0:T(8,128)(2,1)} %get-tuple-element.41), channel_id=1, source_target_pairs={{0,1},{1,2},{2,3},{3,0},{4,5},{5,6},{6,7},{7,4},{8,9},{9,10},{10,1... | collective-permute-start | bytes 1572872 | tf_op jit(solution)/shard_map/ppermute | solution.py:465
  16.6 45.7 %collective-permute-start.1 = (bf16[512,512]{1,0:T(8,128)(2,1)}, bf16[512,512]{1,0:T(8,128)(2,1)}, u32[]{:S(2)}, u32[]{:S(2)}) collective-permute-start(bf16[512,512]{1,0:T(8,128)(2,1)} %get-tuple-element.42), channel_id=1, source_target_pairs={{0,3},{1,0},{2,1},{3,2},{4,7},{5,4},{6,5},{7,6},{8,11},{9,8},{10,9... | collective-permute-start | bytes 1572872 | tf_op jit(solution)/shard_map/ppermute | solution.py:466
  19.3 47.1 %collective-permute-start = (bf16[512,512]{1,0:T(8,128)(2,1)}, bf16[512,512]{1,0:T(8,128)(2,1)}, u32[]{:S(2)}, u32[]{:S(2)}) collective-permute-start(bf16[512,512]{1,0:T(8,128)(2,1)} %get-tuple-element.42), channel_id=1, source_target_pairs={{0,1},{1,2},{2,3},{3,0},{4,5},{5,6},{6,7},{7,4},{8,9},{9,10},{10,1... | collective-permute-start | bytes 1572872 | tf_op jit(solution)/shard_map/ppermute | solution.py:465
  20.4 1.2 copy-start.17
  23.6 0.8 copy-start.10
  24.4 1.0 copy-start.24
  25.4 16.8 %copy-start.11 = (f32[32,4,1,512]{3,2,1,0:T(1,128)}, f32[32,4,1,512]{3,2,1,0:T(1,128)S(1)}, u32[]{:S(2)}) copy-start(f32[32,4,1,512]{3,2,1,0:T(1,128)S(1)} %all-to-all-done.all_ref.refs_8_) | copy-start | bytes 786436
  25.4 28.4 %all-to-all-start.1 = ((bf16[32,64,128]{2,1,0:T(8,128)(2,1)}), bf16[32,64,128]{2,1,0:T(8,128)(2,1)S(1)}, u32[]{:S(2)}, u32[]{:S(2)}) async-start(bf16[32,64,128]{2,1,0:T(8,128)(2,1)} %copy-done.10), calls=%async_computation.1 | async-start | bytes 1048576 | tf_op jit(solution)/shard_map/all_to_all | solution.py:486
  33.6 1.0 copy-start.7
  34.7 1.0 copy-start.8
  35.7 1.2 copy-start.14
  42.2 4.5 %copy-start.29 = (bf16[4,128,512]{2,1,0:T(8,128)(2,1)}, bf16[4,128,512]{2,1,0:T(8,128)(2,1)S(1)}, u32[]{:S(2)}) copy-start(bf16[4,128,512]{2,1,0:T(8,128)(2,1)S(1)} %get-tuple-element.33.refs_5_) | copy-start | bytes 1572868
  43.0 24.5 %collective-permute-start.7 = (bf16[256,512]{1,0:T(8,128)(2,1)}, bf16[256,512]{1,0:T(8,128)(2,1)S(1)}, u32[]{:S(2)}, u32[]{:S(2)}) collective-permute-start(bf16[256,512]{1,0:T(8,128)(2,1)} %slice.27), channel_id=1, source_target_pairs={{0,3},{1,0},{2,1},{3,2},{4,7},{5,4},{6,5},{7,6},{8,11},{9,8},{10,9... | collective-permute-start | bytes 786440 | tf_op jit(solution)/shard_map/ppermute | solution.py:468
  46.7 20.8 %collective-permute-start.6 = (bf16[256,512]{1,0:T(8,128)(2,1)}, bf16[256,512]{1,0:T(8,128)(2,1)}, u32[]{:S(2)}, u32[]{:S(2)}) collective-permute-start(bf16[256,512]{1,0:T(8,128)(2,1)} %slice.26), channel_id=1, source_target_pairs={{0,1},{1,2},{2,3},{3,0},{4,5},{5,6},{6,7},{7,4},{8,9},{9,10},{10,1... | collective-permute-start | bytes 786440 | tf_op jit(solution)/shard_map/ppermute | solution.py:468
  46.7 1.0 copy-start.12
  53.0 0.8 copy-start.27
  54.6 30.2 %all-to-all-start.2 = ((bf16[32,64,128]{2,1,0:T(8,128)(2,1)}), bf16[32,64,128]{2,1,0:T(8,128)(2,1)}, u32[]{:S(2)}, u32[]{:S(2)}) async-start(bf16[32,64,128]{2,1,0:T(8,128)(2,1)} %prefix_scan.1), calls=%async_computation.2 | async-start | bytes 1048576 | tf_op jit(solution)/shard_map/all_to_all | solution.py:486
  63.4 11.7 %collective-permute-start.3 = (bf16[256,512]{1,0:T(8,128)(2,1)S(1)}, bf16[256,512]{1,0:T(8,128)(2,1)S(1)}, u32[]{:S(2)}, u32[]{:S(2)}) collective-permute-start(bf16[256,512]{1,0:T(8,128)(2,1)S(1)} %slice.25), channel_id=1, source_target_pairs={{0,3},{1,0},{2,1},{3,2},{4,7},{5,4},{6,5},{7,6},{8,11},{9,8},{10,9... | collective-permute-start | bytes 786440 | tf_op jit(solution)/shard_map/ppermute | solution.py:468
  67.3 8.5 %collective-permute-start.2 = (bf16[256,512]{1,0:T(8,128)(2,1)S(1)}, bf16[256,512]{1,0:T(8,128)(2,1)S(1)}, u32[]{:S(2)}, u32[]{:S(2)}) collective-permute-start(bf16[256,512]{1,0:T(8,128)(2,1)S(1)} %slice.24), channel_id=1, source_target_pairs={{0,1},{1,2},{2,3},{3,0},{4,5},{5,6},{6,7},{7,4},{8,9},{9,10},{10,1... | collective-permute-start | bytes 786440 | tf_op jit(solution)/shard_map/ppermute | solution.py:468
  74.2 0.8 copy-start.22
  75.9 17.4 %copy-start.9 = (bf16[4,512,128]{1,2,0:T(8,128)(2,1)S(1)}, bf16[4,512,128]{1,2,0:T(8,128)(2,1)}, u32[]{:S(2)}) copy-start(bf16[4,512,128]{1,2,0:T(8,128)(2,1)} %copy.11) | copy-start | bytes 1572868
  75.9 17.5 %copy-start.13 = (f32[32,4,1,512]{3,2,1,0:T(1,128)S(1)}, f32[32,4,1,512]{3,2,1,0:T(1,128)}, u32[]{:S(2)}) copy-start(f32[32,4,1,512]{3,2,1,0:T(1,128)} %copy-done.11) | copy-start | bytes 786436
  83.1 1.0 copy-start.4
  84.0 0.8 copy-start.20
  84.9 32.4 %all-to-all-start.3 = ((bf16[32,64,128]{2,1,0:T(8,128)(2,1)}), bf16[32,64,128]{2,1,0:T(8,128)(2,1)S(1)}, u32[]{:S(2)}, u32[]{:S(2)}) async-start(bf16[32,64,128]{2,1,0:T(8,128)(2,1)} %get-tuple-element.38), calls=%async_computation.3 | async-start | bytes 1048576 | tf_op jit(solution)/shard_map/all_to_all | solution.py:495
  93.4 1.2 copy-start.15
  94.6 1.2 copy-start.18
  95.8 1.0 copy-start.23
  96.9 1.0 copy-start.30
  97.9 9.9 %copy-start.16 = (bf16[1024,512]{1,0:T(8,128)(2,1)S(1)}, bf16[1024,512]{1,0:T(8,128)(2,1)}, u32[]{:S(2)}) copy-start(bf16[1024,512]{1,0:T(8,128)(2,1)} %refs_1_.7) | copy-start | bytes 3145732
  97.9 9.9 %copy-start.19 = (bf16[1024,512]{1,0:T(8,128)(2,1)S(1)}, bf16[1024,512]{1,0:T(8,128)(2,1)}, u32[]{:S(2)}) copy-start(bf16[1024,512]{1,0:T(8,128)(2,1)} %refs_2_.3) | copy-start | bytes 3145732
  97.9 9.9 %copy-start.21 = (bf16[4,512,128]{2,1,0:T(8,128)(2,1)S(1)}, bf16[4,512,128]{2,1,0:T(8,128)(2,1)}, u32[]{:S(2)}) copy-start(bf16[4,512,128]{2,1,0:T(8,128)(2,1)} %copy-done.20) | copy-start | bytes 1572868
  97.9 9.9 %copy-start.25 = (f32[4,512,128]{2,1,0:T(8,128)S(1)}, f32[4,512,128]{2,1,0:T(8,128)}, u32[]{:S(2)}) copy-start(f32[4,512,128]{2,1,0:T(8,128)} %copy-done.24) | copy-start | bytes 3145732
  97.9 9.9 %copy-start.28 = (bf16[4,128,512]{2,1,0:T(8,128)(2,1)S(1)}, bf16[4,128,512]{2,1,0:T(8,128)(2,1)}, u32[]{:S(2)}) copy-start(bf16[4,128,512]{2,1,0:T(8,128)(2,1)} %copy-done.27) | copy-start | bytes 1572868
  106.8 1.0 copy-start.26
  117.3 19.1 %all-to-all-start.5 = ((bf16[32,64,128]{2,1,0:T(8,128)(2,1)}), bf16[32,64,128]{2,1,0:T(8,128)(2,1)}, u32[]{:S(2)}, u32[]{:S(2)}) async-start(bf16[32,64,128]{2,1,0:T(8,128)(2,1)} %get-tuple-element.40), calls=%async_computation.5 | async-start | bytes 1048576 | tf_op jit(solution)/shard_map/all_to_all | solution.py:503
  124.7 31.9 %copy-start.1 = (f32[1024,512]{1,0:T(8,128)S(1)}, f32[1024,512]{1,0:T(8,128)}, u32[]{:S(2)}) copy-start(f32[1024,512]{1,0:T(8,128)} %get-tuple-element.37.local_ref) | copy-start | bytes 6291460
  124.9 0.8 copy-start.3
  136.4 15.7 %all-to-all-start.4 = ((bf16[32,64,128]{2,1,0:T(8,128)(2,1)}), bf16[32,64,128]{2,1,0:T(8,128)(2,1)S(1)}, u32[]{:S(2)}, u32[]{:S(2)}) async-start(bf16[32,64,128]{2,1,0:T(8,128)(2,1)} %copy-done.3), calls=%async_computation.4 | async-start | bytes 1048576 | tf_op jit(solution)/shard_map/all_to_all | solution.py:495
  141.5 0.8 copy-start.2
  152.0 16.4 %all-to-all-start.6 = ((bf16[32,64,128]{2,1,0:T(8,128)(2,1)}), bf16[32,64,128]{2,1,0:T(8,128)(2,1)}, u32[]{:S(2)}, u32[]{:S(2)}) async-start(bf16[32,64,128]{2,1,0:T(8,128)(2,1)} %copy-done.2), calls=%async_computation.6 | async-start | bytes 1048576 | tf_op jit(solution)/shard_map/all_to_all | solution.py:503
  156.7 1.2 copy-start.5

commit v3 on v2

v3 whole, which is shorter than its diff:
```python
import functools
import math

import jax
import jax.numpy as jnp
from jax import lax
from jax.experimental import pallas as pl
from jax.experimental.pallas import tpu as pltpu
from jax.sharding import PartitionSpec as P

BLOCK = 512
PART = 256
TILE = 128
HALF = 64
ROWS = 96
F32 = jnp.float32
BF16 = jnp.bfloat16
VMEM_LIMIT = 60 << 20


def dot(left, right):
    return lax.dot_general(left, right, (((1,), (0,)), ((), ())), preferred_element_type=F32)


def dot_nt(left, right):
    return lax.dot_general(left, right, (((1,), (1,)), ((), ())), preferred_element_type=F32)


def call(kernel, name, grid, in_specs, outs, scratch=(), aliases=None, prefetch=0, flops=0, size=0):
    return pl.pallas_call(
        kernel,
        grid_spec=pltpu.PrefetchScalarGridSpec(
            num_scalar_prefetch=prefetch,
            grid=grid,
            in_specs=in_specs,
            out_specs=[spec for _, _, spec in outs],
            scratch_shapes=list(scratch),
        ),
        out_shape=[jax.ShapeDtypeStruct(shape, dtype) for shape, dtype, _ in outs],
        input_output_aliases=aliases or {},
        compiler_params=pltpu.CompilerParams(
            dimension_semantics=("arbitrary",) * len(grid), vmem_limit_bytes=VMEM_LIMIT
        ),
        cost_estimate=pl.CostEstimate(flops=flops, bytes_accessed=size, transcendentals=0),
        name=name,
    )


def onehot_rows(codes_row, entries):
    entry = lax.broadcasted_iota(jnp.int32, (entries, codes_row.shape[1]), 0)
    return jnp.where(entry == codes_row, 1.0, 0.0).astype(BF16)


def fold(array):
    rows, lanes = array.shape
    return jnp.sum(array.reshape(rows // 8, 8, lanes), axis=0)


def fold_max(array):
    rows, lanes = array.shape
    return jnp.max(array.reshape(rows // 8, 8, lanes), axis=0)


def sum_kernel(codes_ref, columns_ref, value_ref, send_ref, first_ref, first_count_ref):
    heads, entries, width = first_ref.shape
    slices = entries // HALF
    blocks = value_ref.shape[0] // BLOCK
    levels = lax.broadcasted_iota(jnp.int32, (BLOCK, entries), 1)
    lines = []
    for h in range(heads):
        total = None
        number = None
        for b in range(blocks):
            span = slice(b * BLOCK, (b + 1) * BLOCK)
            hot = onehot_rows(codes_ref[h, :, span], entries)
            part = dot(hot, value_ref[span, h * width : (h + 1) * width])
            same = jnp.where(levels == columns_ref[span, h : h + 1], 1.0, 0.0)
            amount = jnp.sum(fold(same), axis=0, keepdims=True)
            if b == 0:
                first_ref[h] = part
                first_count_ref[h] = amount
            total = part if b == 0 else total + part
            number = amount if b == 0 else number + amount
        for k in range(slices):
            send_ref[h * slices + k, :HALF, :] = total[k * HALF : (k + 1) * HALF].astype(BF16)
        lines += [number[:, i * TILE : (i + 1) * TILE] for i in range(entries // TILE)]
    lines = jnp.concatenate(lines, axis=0)
    high = jnp.floor(lines * (1.0 / 256.0))
    digits = jnp.concatenate([high, lines - high * 256.0], axis=0).astype(BF16)
    for k in range(heads * slices):
        send_ref[k, HALF:, :] = digits


def own_sums(codes_rows, codes, values, heads, entries):
    tokens = values.shape[0]
    width = values.shape[1] // heads
    slices = entries // HALF
    whole = lambda i: (0, 0, 0)
    return call(
        sum_kernel, "own_sums", (1,),
        [
            pl.BlockSpec(codes_rows.shape, whole),
            pl.BlockSpec(codes.shape, lambda i: (0, 0)),
            pl.BlockSpec(values.shape, lambda i: (0, 0)),
        ],
        [
            ((heads * slices, ROWS, TILE), BF16, pl.BlockSpec((heads * slices, ROWS, TILE), whole)),
            ((heads, entries, width), F32, pl.BlockSpec((heads, entries, width), whole)),
            ((heads, 1, entries), F32, pl.BlockSpec((heads, 1, entries), whole)),
        ],
        flops=1 << 30, size=4 << 20,
    )(codes_rows, codes, values)


def prefix_kernel(me_ref, in_ref, first_ref, out_ref, count_ref):
    running = jnp.zeros(out_ref.shape[1:], F32)
    lines = (ROWS - HALF) // 2
    number = jnp.zeros((lines, TILE), F32)
    for d in range(in_ref.shape[0]):
        out_ref[d] = running.astype(BF16)
        running = running + in_ref[d, :HALF, :].astype(F32)
        digits = in_ref[d, HALF:, :].astype(F32)
        digits = digits[:lines] * 256.0 + digits[lines:]
        number = number + jnp.where(d < me_ref[0], digits, 0.0)
    heads = first_ref.shape[0]
    per = lines // heads
    for h in range(heads):
        for i in range(per):
            line = number[h * per + i : h * per + i + 1]
            columns = slice(i * TILE, (i + 1) * TILE)
            count_ref[0, h, :, columns] = line
            count_ref[1, h, :, columns] = line + first_ref[h, :, columns]


def prefix_scan(me, pieces, first):
    count = pieces.shape[0]
    heads, _, entries = first.shape
    whole = lambda i, *_: (0, 0, 0)
    shape = (2, heads, 1, entries)
    return call(
        prefix_kernel, "prefix_scan", (1,),
        [pl.BlockSpec(pieces.shape, whole), pl.BlockSpec(first.shape, whole)],
        [
            ((count, HALF, TILE), BF16, pl.BlockSpec((count, HALF, TILE), whole)),
            (shape, F32, pl.BlockSpec(shape, lambda i, *_: (0, 0, 0, 0))),
        ],
        prefetch=1, size=1 << 20,
    )(me, pieces, first)


def suffix_kernel(in_ref, out_ref):
    running = jnp.zeros((HALF, TILE), F32)
    total = jnp.zeros((HALF, TILE), F32)
    for d in reversed(range(in_ref.shape[0])):
        out_ref[d, :HALF, :] = running.astype(BF16)
        running = running + in_ref[d, :HALF, :].astype(F32)
        total = total + in_ref[d, HALF:, :].astype(F32)
    low = total.astype(BF16)
    for d in range(in_ref.shape[0]):
        out_ref[d, HALF:, :] = low


def suffix_scan(pieces):
    spec = pl.BlockSpec(pieces.shape, lambda i: (0, 0, 0))
    return call(
        suffix_kernel, "suffix_scan", (1,), [spec], [(pieces.shape, BF16, spec)], size=2 << 20
    )(pieces)[0]


def count_columns(number):
    tiles = [
        jnp.broadcast_to(number[:, i * TILE : (i + 1) * TILE], (TILE, TILE)).T
        for i in range(number.shape[1] // TILE)
    ]
    return jnp.concatenate(tiles, axis=0)


def forward_kernel(codes_ref, query_ref, book_ref, book_t_ref, count_ref,
                   low_ref, keys_ref, rows_k, counts, scores):
    entries, width = book_ref.shape[1:]
    entry_tiles = entries // TILE
    factor = width ** -0.5 * math.log2(math.e)
    causal = lax.broadcasted_iota(jnp.int32, (TILE, TILE), 1) >= lax.broadcasted_iota(
        jnp.int32, (TILE, TILE), 0
    )
    parts = BLOCK // PART
    blocks = low_ref.shape[0]

    def prepare(b):
        keys_t = dot(
            book_t_ref[0], onehot_rows(codes_ref[0, :, b * BLOCK : (b + 1) * BLOCK], entries)
        )
        keys_ref[b, 0] = keys_t.astype(BF16)
        rows_k[b, :entries, :] = book_ref[0]
        rows_k[b, entries:, :] = keys_t.T.astype(BF16)
        counts[b] = count_columns(count_ref[b, 0])

    def multiply(b, n):
        used = entries + PART * (n + 1)
        at = b * BLOCK + n * PART
        scores[b, n, :used, :] = dot_nt(rows_k[b, :used, :], query_ref[at : at + PART, :])

    def soften(b, n):
        used = entries + PART * (n + 1)
        for j in range(PART // TILE):
            columns = slice(j * TILE, (j + 1) * TILE)
            target = slice(n * PART + j * TILE, n * PART + (j + 1) * TILE)
            pieces = range(entry_tiles + 2 * n + j + 1)
            top = jnp.full((8, TILE), -jnp.inf, F32)
            for i in pieces:
                rows = slice(i * TILE, (i + 1) * TILE)
                piece = scores[b, n, rows, columns]
                if i < entry_tiles:
                    piece = jnp.where(counts[b, rows, :] > 0.0, piece, -jnp.inf)
                    scores[b, n, rows, columns] = piece
                elif i == pieces[-1]:
                    piece = jnp.where(causal, piece, -jnp.inf)
                    scores[b, n, rows, columns] = piece
                top = jnp.maximum(top, fold_max(piece))
            top = jnp.max(top, axis=0, keepdims=True)
            total = jnp.zeros((8, TILE), F32)
            for i in pieces:
                rows = slice(i * TILE, (i + 1) * TILE)
                piece = jnp.exp2((scores[b, n, rows, columns] - top) * factor)
                scores[b, n, rows, columns] = piece
                if i < entry_tiles:
                    piece = piece * counts[b, rows, :]
                total = total + fold(piece)
            inverse = 1.0 / jnp.sum(total, axis=0, keepdims=True)
            for i in pieces:
                rows = slice(i * TILE, (i + 1) * TILE)
                low_ref[b, 0, rows, target] = (scores[b, n, rows, columns] * inverse).astype(BF16)
            if j == 0:
                low_ref[b, 0, used - TILE : used, target] = jnp.zeros((TILE, TILE), BF16)

    order = [(b, n) for b in range(blocks) for n in range(parts)]
    for b in range(blocks):
        prepare(b)
    multiply(*order[0])
    for k, item in enumerate(order):
        if k + 1 < len(order):
            multiply(*order[k + 1])
        soften(*item)


def forward(codes_rows, queries, book, book_t, counts):
    heads, entries, width = book.shape
    tokens = queries.shape[0]
    blocks = tokens // BLOCK
    both = entries + BLOCK
    by_head = lambda h: (h, 0, 0)
    in_blocks = lambda h: (0, h, 0, 0)
    return call(
        forward_kernel, "forward", (heads,),
        [
            pl.BlockSpec((1, 1, tokens), by_head),
            pl.BlockSpec((tokens, width), lambda h: (0, h)),
            pl.BlockSpec((1, entries, width), by_head),
            pl.BlockSpec((1, width, entries), by_head),
            pl.BlockSpec((blocks, 1, 1, entries), in_blocks),
        ],
        [
            ((blocks, heads, both, BLOCK), BF16, pl.BlockSpec((blocks, 1, both, BLOCK), in_blocks)),
            ((blocks, heads, width, BLOCK), BF16, pl.BlockSpec((blocks, 1, width, BLOCK), in_blocks)),
        ],
        [
            pltpu.VMEM((blocks, both, width), BF16),
            pltpu.VMEM((blocks, entries, TILE), F32),
            pltpu.VMEM((blocks, 2, both, PART), F32),
        ],
        flops=6 << 30, size=12 << 20,
    )(codes_rows, queries, book, book_t, counts)


def backward_kernel(_, own_ref, left_ref, right_ref, far0_ref, far1_ref, own_w, left_w, right_w,
                    far_w, codes_ref, query_ref, value_ref, probs_ref, keys_ref, book_t_ref,
                    prefix_ref, count_ref, first_ref,
                    grad_query_ref, local_ref, part_ref, send_ref,
                    dout, hot, rows_v, counts, grads, score_grad, key_grad, wide_t):
    width, entries = book_t_ref.shape[1:]
    entry_tiles = entries // TILE
    parts = BLOCK // PART
    blocks = probs_ref.shape[0]
    scale = width ** -0.5
    head = pl.program_id(0)

    @pl.when(head == 0)
    def _():
        count = own_ref.shape[0] // PART
        for n in range(count):
            span = slice(n * PART, (n + 1) * PART)
            total = dot_nt(own_ref[span, :], own_w[...]) + dot_nt(left_ref[span, :], left_w[...])
            total = total + dot_nt(right_ref[span, :], right_w[...])
            if n < count // 2:
                far = far0_ref[span, :]
            else:
                far = far1_ref[(n - count // 2) * PART : (n + 1 - count // 2) * PART, :]
            total = total + dot_nt(far, far_w[...])
            for h in range(dout.shape[0]):
                dout[h, span, :] = total[:, h * width : (h + 1) * width].astype(BF16)

    def prepare(b):
        hot[b] = onehot_rows(codes_ref[0, :, b * BLOCK : (b + 1) * BLOCK], entries)
        wide_t[b, :, :entries] = book_t_ref[0]
        wide_t[b, :, entries:] = keys_ref[b, 0]
        sums = prefix_ref[...].reshape(entries, width)
        if b > 0:
            sums = (sums.astype(F32) + first_ref[0]).astype(BF16)
        rows_v[b, :entries, :] = sums
        rows_v[b, entries:, :] = value_ref[b * BLOCK : (b + 1) * BLOCK, :]
        counts[b] = count_columns(count_ref[b, 0])

    def multiply(b, n):
        used = entries + PART * (n + 1)
        at = b * BLOCK + n * PART
        grads[b, n, :used, :] = dot_nt(rows_v[b, :used, :], dout[head, at : at + PART, :])

    def combine(b, n):
        used = entries + PART * (n + 1)
        for j in range(PART // TILE):
            columns = slice(j * TILE, (j + 1) * TILE)
            source = slice(n * PART + j * TILE, n * PART + (j + 1) * TILE)
            pieces = range(entry_tiles + 2 * n + j + 1)
            delta = jnp.zeros((8, TILE), F32)
            for i in pieces:
                rows = slice(i * TILE, (i + 1) * TILE)
                delta = delta + fold(
                    probs_ref[b, 0, rows, source].astype(F32) * grads[b, n, rows, columns]
                )
            delta = jnp.sum(delta, axis=0, keepdims=True) * scale
            for i in pieces:
                rows = slice(i * TILE, (i + 1) * TILE)
                shift = delta
                if i < entry_tiles:
                    shift = delta * counts[b, rows, :]
                piece = grads[b, n, rows, columns] * scale - shift
                piece = probs_ref[b, 0, rows, source].astype(F32) * piece
                score_grad[b, n, rows, columns] = piece.astype(BF16)
            if j == 0:
                score_grad[b, n, used - TILE : used, columns] = jnp.zeros((TILE, TILE), BF16)

    sums_k = [[None] * parts for _ in range(blocks)]
    sums_v = [[None] * parts for _ in range(blocks)]

    def outputs(b, n):
        used = entries + PART * (n + 1)
        at = b * BLOCK + n * PART
        span = slice(at, at + PART)
        sums_v[b][n] = dot(probs_ref[b, 0, :used, n * PART : (n + 1) * PART], dout[head, span, :])
        sums_k[b][n] = dot(score_grad[b, n, :used, :], query_ref[span, :])
        grad_t = dot(wide_t[b, :, :used], score_grad[b, n, :used, :])
        grad_query_ref[span, :] = grad_t.T.astype(BF16)

    order = [(b, n) for b in range(blocks) for n in range(parts)]
    for b in range(blocks):
        prepare(b)
    multiply(*order[0])
    code = None
    part = None
    middle = entries + PART
    for k, item in enumerate(order):
        if k + 1 < len(order):
            multiply(*order[k + 1])
        combine(*item)
        outputs(*item)
        b, n = item
        if n == parts - 1:
            first, last = sums_v[b]
            at = b * BLOCK
            local_ref[at : at + PART, :] = first[entries:] + last[entries:middle]
            local_ref[at + PART : at + BLOCK, :] = last[middle:]
            mine = first[:entries] + last[:entries]
            if b == blocks - 1:
                part_ref[0] = mine
            part = mine if b == 0 else part + mine
            first, last = sums_k[b]
            key_grad[b, :PART, :] = (first[entries:] + last[entries:middle]).astype(BF16)
            key_grad[b, PART:, :] = last[middle:].astype(BF16)
            mine = first[:entries] + last[:entries] + dot(hot[b], key_grad[b])
            code = mine if b == 0 else code + mine
    for k in range(entries // HALF):
        rows = slice(k * HALF, (k + 1) * HALF)
        send_ref[k, :HALF, :] = part[rows].astype(BF16)
        send_ref[k, HALF:, :] = code[rows].astype(BF16)


def backward(me, pieces, weight, codes_rows, queries, values, probs, keys, book_t, prefix, counts,
             first):
    heads, width, entries = book_t.shape
    tokens = queries.shape[0]
    blocks = tokens // BLOCK
    both = entries + BLOCK
    columns = weight.shape[1] // 4
    slices = entries // HALF
    by_head = lambda h, *_: (h, 0, 0)
    in_blocks = lambda h, *_: (0, h, 0, 0)
    rows_of = pl.BlockSpec((tokens, width), lambda h, *_: (0, h))
    per_head = pl.BlockSpec((1, entries, width), by_head)

    def chunk(offset):
        return pl.BlockSpec(
            (weight.shape[0], columns), lambda h, me: (0, lax.rem(me[0] + offset, 4))
        )

    in_specs = [pl.BlockSpec(piece.shape, lambda h, *_: (0, 0)) for piece in pieces]
    in_specs += [chunk(0), chunk(3), chunk(1), chunk(2)]
    in_specs += [
        pl.BlockSpec((1, 1, tokens), by_head),
        rows_of,
        rows_of,
        pl.BlockSpec((blocks, 1, both, BLOCK), in_blocks),
        pl.BlockSpec((blocks, 1, width, BLOCK), in_blocks),
        pl.BlockSpec((1, width, entries), by_head),
        pl.BlockSpec((slices, HALF, width), by_head),
        pl.BlockSpec((blocks, 1, 1, entries), in_blocks),
        per_head,
    ]
    outs = [
        (queries.shape, BF16, rows_of),
        (queries.shape, F32, rows_of),
        ((heads, entries, width), F32, per_head),
        ((heads * slices, 2 * HALF, width), BF16, pl.BlockSpec((slices, 2 * HALF, width), by_head)),
    ]
    return call(
        backward_kernel, "backward", (heads,), in_specs, outs,
        [
            pltpu.VMEM((heads, tokens, width), BF16),
            pltpu.VMEM((blocks, entries, BLOCK), BF16),
            pltpu.VMEM((blocks, both, width), BF16),
            pltpu.VMEM((blocks, entries, TILE), F32),
            pltpu.VMEM((blocks, 2, both, PART), F32),
            pltpu.VMEM((blocks, 2, both, PART), BF16),
            pltpu.VMEM((blocks, BLOCK, width), BF16),
            pltpu.VMEM((blocks, width, both), BF16),
        ],
        prefetch=1, flops=20 << 30, size=24 << 20,
    )(me, *pieces, *[weight] * 4, codes_rows, queries, values, probs, keys, book_t, prefix, counts,
      first)


def finish_kernel(codes_ref, local_ref, later_ref, part_ref, out_ref, book_ref, tables):
    heads, entries, width = part_ref.shape
    slices = entries // HALF
    step = pl.program_id(0)

    @pl.when(step == 0)
    def _():
        for h in range(heads):
            pieces = later_ref[h * slices : (h + 1) * slices]
            later = pieces[:, :HALF, :].reshape(entries, width)
            tables[1, h] = later
            tables[0, h] = (later.astype(F32) + part_ref[h]).astype(BF16)
            book_ref[h] = pieces[:, HALF:, :].reshape(entries, width).astype(F32)

    block = step // (pl.num_programs(0) // 2)
    levels = lax.broadcasted_iota(jnp.int32, (codes_ref.shape[0], entries), 1)
    for h in range(heads):
        hot = jnp.where(levels == codes_ref[:, h : h + 1], 1.0, 0.0).astype(BF16)
        columns = slice(h * width, (h + 1) * width)
        out_ref[:, columns] = (local_ref[:, columns] + dot(hot, tables[block, h])).astype(BF16)


def finish(codes, local, later, part):
    heads, entries, width = part.shape
    whole = lambda b: (0, 0, 0)
    rows = pl.BlockSpec((PART, heads * width), lambda b: (b, 0))
    return call(
        finish_kernel, "finish_values", (local.shape[0] // PART,),
        [
            pl.BlockSpec((PART, heads), lambda b: (b, 0)),
            rows,
            pl.BlockSpec(later.shape, whole),
            pl.BlockSpec(part.shape, whole),
        ],
        [(local.shape, BF16, rows), (part.shape, F32, pl.BlockSpec(part.shape, whole))],
        [pltpu.VMEM((2, heads, entries, width), BF16)],
        flops=1 << 30, size=4 << 20,
    )(codes, local, later, part)


def ring_pieces(array):
    count = lax.axis_size("head")
    up = [(i, (i + 1) % count) for i in range(count)]
    down = [(i, (i - 1) % count) for i in range(count)]
    left = lax.ppermute(array, "head", up)
    right = lax.ppermute(array, "head", down)
    half = array.shape[0] // 2
    far = lax.ppermute(left[:half], "head", up), lax.ppermute(right[half:], "head", down)
    return array, left, right, *far


def per_device(queries, values, codes, codebook, out_weight, grad_out):
    heads, entries, width = codebook.shape
    exchange = functools.partial(
        lax.all_to_all, axis_name="seq", split_axis=0, concat_axis=0, tiled=True
    )
    me_seq = lax.axis_index("seq").astype(jnp.int32).reshape(1)
    me_head = lax.axis_index("head").astype(jnp.int32).reshape(1)
    pieces = ring_pieces(grad_out)
    codes_rows = codes.T.reshape(heads, 1, -1)
    book_t = jnp.swapaxes(codebook, 1, 2)
    send, first, first_count = own_sums(codes_rows, codes, values, heads, entries)
    prefix, counts = prefix_scan(me_seq, exchange(send), first_count)
    prefix = exchange(prefix)
    probs, keys = forward(codes_rows, queries, codebook, book_t, counts)
    grad_query, local, part, send = backward(
        me_head, pieces, out_weight, codes_rows, queries, values, probs, keys, book_t, prefix,
        counts, first,
    )
    later = exchange(suffix_scan(exchange(send)))
    grad_values, grad_book = finish(codes, local, later, part)
    return grad_query, grad_values, grad_book


def solution(mesh):
    rows = P("seq", "head")
    return jax.shard_map(
        per_device,
        mesh=mesh,
        in_specs=(rows, rows, rows, P("head", None, None), P("head", None), rows),
        out_specs=(rows, rows, P("head", None, None)),
        check_vma=False,
    )
```

time: 172 us -> 135 us (0.78)
  blocking collectives: 0 us -> 47.6 us
  starting transfers between devices: 61.3 us -> 19.6 us
  local copies, waits for them, and re-layouts: 26.4 us -> 6.9 us
  waiting for transfers between devices: 29.4 us -> 14.6 us
  Pallas kernels: 50.3 us -> 44.7 us
  other arithmetic: 2.08 us -> 0 us
    all_to_all x0 -> x2, blocking collectives: none -> 47.6 us  [per_device(): later = exchange(suffix_scan(exchange(send)))]
    all_to_all x7 -> x2, starting transfers between devices: 50.1 us -> 13.6 us  [the longest x1 9.45 us: per_device(): prefix, counts = prefix_scan(me_seq, exchange(send), first_count)]
    unnamed x67 -> x12, local copies, waits for them, and re-layouts: 21 us -> 4.22 us
    all_to_all x7 -> x2, waiting for transfers between devices: 28.6 us -> 13.2 us  [the longest x1 13.2 us: per_device(): prefix, counts = prefix_scan(me_seq, exchange(send), first_count)]
    pallas_call x12 -> x6, Pallas kernels: 50.3 us -> 44.7 us  [the longest x1 20.6 us: backward(): call(backward_kernel, 'backward', (heads,), in_specs, outs, [pltpu.VMEM((...]
    ppermute x2 -> x1, starting transfers between devices: 5.15 us -> 1.35 us  [ring_pieces(): right = lax.ppermute(array, 'head', down)]
    ppermute x2 -> x1, starting transfers between devices: 5.97 us -> 2.48 us  [ring_pieces(): lax.ppermute(right[half:], 'head', down)]
    ppermute x2 -> x1, starting transfers between devices: 0.01 us -> 2.11 us  [ring_pieces(): left = lax.ppermute(array, 'head', up)]
  transfers between devices with their start and end apart: 15 -> 6, of which waited for: 4 -> 3; matrix products, arithmetic and copies ran while one was open for 3% -> 4% of each run, Pallas kernels for 29% -> 12%
where the time goes in v3:
time: 135 us; the launch traced here: 134 us
  blocking collectives  47.6 us (35%)
  Pallas kernels  44.7 us (33%)
  starting transfers between devices  19.6 us (15%)
  waiting for transfers between devices  14.6 us (11%)
  local copies, waits for them, and re-layouts  6.9 us (5%)
    all_to_all x2, blocking collectives, per_device(): later = exchange(suffix_scan(exchange(send)))  47.6 us
    pallas_call x1, Pallas kernels, backward(): call(backward_kernel, 'backward', (heads,), in_specs, outs, [pltpu.VMEM((...  20.6 us
    all_to_all x1, waiting for transfers between devices, per_device(): prefix, counts = prefix_scan(me_seq, exchange(send), first_count)  13.2 us
    all_to_all x1, starting transfers between devices, per_device(): prefix, counts = prefix_scan(me_seq, exchange(send), first_count)  9.45 us
    pallas_call x1, Pallas kernels, forward(): call(forward_kernel, 'forward', (heads,), [pl.BlockSpec((1, 1, tokens), b...  9.36 us
    pallas_call x1, Pallas kernels, finish(): call(finish_kernel, 'finish_values', (local.shape[0] // PART,), [pl.Block...  5.53 us
    pallas_call x1, Pallas kernels, own_sums(): call(sum_kernel, 'own_sums', (1,), [pl.BlockSpec(codes_rows.shape, whole)...  4.76 us
    unnamed x12, local copies, waits for them, and re-layouts  4.22 us
  transfers between devices with their start and end apart: 6, of which 3 were waited for; matrix products, arithmetic and copies ran while one was open for 4% of the time, Pallas kernels for 12%

profile of v3, /device:TPU:1, one launch (start us, length us, event | category | flops | bytes accessed | tf_op | source)
XLA Modules:
  0.0 134.1 jit_solution(4099534528029799217)
XLA Ops:
  0.6 2.1 %collective-permute-start = (bf16[1024,512]{1,0:T(8,128)(2,1)}, bf16[1024,512]{1,0:T(8,128)(2,1)S(1)}, u32[]{:S(2)}, u32[]{:S(2)}) collective-permute-start(bf16[1024,512]{1,0:T(8,128)(2,1)} %own_ref.1), channel_id=1, source_target_pairs={{0,1},{1,2},{2,3},{3,0},{4,5},{5,6},{6,7},{7,4},{8,9},{9,10},{10,1... | collective-permute-start | bytes 3145736 | tf_op jit(solution)/shard_map/ppermute | solution.py:485
  2.7 1.4 %collective-permute-start.1 = (bf16[1024,512]{1,0:T(8,128)(2,1)}, bf16[1024,512]{1,0:T(8,128)(2,1)}, u32[]{:S(2)}, u32[]{:S(2)}) collective-permute-start(bf16[1024,512]{1,0:T(8,128)(2,1)} %own_ref.1), channel_id=1, source_target_pairs={{0,3},{1,0},{2,1},{3,2},{4,7},{5,4},{6,5},{7,6},{8,11},{9,8},{10,9... | collective-permute-start | bytes 3145736 | tf_op jit(solution)/shard_map/ppermute | solution.py:486
  4.1 1.7 %copy.10.columns_ref.codes_ref = s32[1024,4]{1,0:T(8,128)} copy(s32[1024,4]{0,1:T(4,128)} %param.8) | data formatting | bytes 32768 | tf_op args[2]
  5.8 1.3 reshape.16.codes_ref
  7.2 0.0 copy-start.1
  7.2 4.8 %own_sums.1 = (bf16[32,96,128]{2,1,0:T(8,128)(2,1)}, f32[4,512,128]{2,1,0:T(8,128)}, f32[4,1,512]{2,1,0:T(1,128)}) custom-call(s32[4,1,1024]{2,1,0:T(1,128)} %reshape.16.codes_ref, s32[1024,4]{1,0:T(8,128)} %copy.10.columns_ref.codes_ref, bf16[1024,512]{1,0:T(8,128)(2,1)} %value_ref.3), custom_call_target="tpu_custom_call" | custom-call | flops 1073741824 | bytes 4194304 | tf_op jit(solution)/shard_map/own_sums/pallas_call | solution.py:99
  11.9 9.5 %all-to-all-start = ((bf16[32,96,128]{2,1,0:T(8,128)(2,1)}), bf16[32,96,128]{2,1,0:T(8,128)(2,1)S(1)}, u32[]{:S(2)}, u32[]{:S(2)}) async-start(bf16[32,96,128]{2,1,0:T(8,128)(2,1)} %get-tuple-element.16), calls=%async_computation | async-start | bytes 1572864 | tf_op jit(solution)/shard_map/all_to_all | solution.py:503
  21.4 0.0 copy-done.1
  21.4 1.0 copy.9
  22.4 13.2 %all-to-all-done.in_ref = bf16[32,96,128]{2,1,0:T(8,128)(2,1)S(1)} async-done(((bf16[32,96,128]{2,1,0:T(8,128)(2,1)}), bf16[32,96,128]{2,1,0:T(8,128)(2,1)S(1)}, u32[]{:S(2)}, u32[]{:S(2)}) %all-to-all-start) | async-done | bytes 786464 | tf_op jit(solution)/shard_map/all_to_all | solution.py:503
  35.6 0.0 copy-start
  35.6 0.9 copy-done
  36.5 2.0 %prefix_scan.1 = (bf16[32,64,128]{2,1,0:T(8,128)(2,1)}, f32[2,4,1,512]{3,2,1,0:T(1,128)}) custom-call(s32[1]{0:T(128)} %bitcast.3.me_ref, bf16[32,96,128]{2,1,0:T(8,128)(2,1)} %copy-done, f32[4,1,512]{2,1,0:T(1,128)} %get-tuple-element.17.first_ref), custom_call_target="tpu_custom_call" | custom-call | bytes 1048576 | tf_op jit(solution)/shard_map/prefix_scan/pallas_call | solution.py:140
  38.5 4.1 %all-to-all-start.1 = ((bf16[32,64,128]{2,1,0:T(8,128)(2,1)}), bf16[32,64,128]{2,1,0:T(8,128)(2,1)S(1)}, u32[]{:S(2)}, u32[]{:S(2)}) async-start(bf16[32,64,128]{2,1,0:T(8,128)(2,1)} %get-tuple-element.21), calls=%async_computation.1 | async-start | bytes 1048576 | tf_op jit(solution)/shard_map/all_to_all | solution.py:504
  42.6 0.0 collective-permute-done.left_ref
  42.6 0.0 copy-start.3
  42.7 0.1 collective-permute-start.2
  42.8 0.0 collective-permute-done.1.right_ref
  42.8 1.3 slice.9
  44.1 2.5 %collective-permute-start.3 = (bf16[512,512]{1,0:T(8,128)(2,1)S(1)}, bf16[512,512]{1,0:T(8,128)(2,1)}, u32[]{:S(2)}, u32[]{:S(2)}) collective-permute-start(bf16[512,512]{1,0:T(8,128)(2,1)S(1)} %slice.9), channel_id=1, source_target_pairs={{0,3},{1,0},{2,1},{3,2},{4,7},{5,4},{6,5},{7,6},{8,11},{9,8},{10,9... | collective-permute-start | bytes 1572872 | tf_op jit(solution)/shard_map/ppermute | solution.py:488
  46.6 9.4 %forward.1 = (bf16[2,4,1024,512]{3,2,1,0:T(8,128)(2,1)}, bf16[2,4,128,512]{3,2,1,0:T(8,128)(2,1)}) custom-call(s32[4,1,1024]{2,1,0:T(1,128)} %reshape.16.codes_ref, bf16[1024,512]{1,0:T(8,128)(2,1)} %query_ref.3, bf16[4,512,128]{2,1,0:T(8,128)(2,1)} %book_ref.1, bf16[4,128,512]{2,1,0:T(8,128)(2,1)} %bitcast.4, f32[2,4,1,512]{3,2,1,0:T(1,128)} %get-tuple-element.18.count_ref), custom_call_target="tpu_custom_call" | custom-call | flops 6442450944 | bytes 12582912 | tf_op jit(solution)/shard_map/forward/pallas_call | solution.py:253
  56.0 0.0 copy-done.3
  56.0 0.0 all-to-all-done.1.prefix_ref
  56.0 0.0 copy-start.2
  56.0 1.2 collective-permute-done.2.far0_ref
  57.1 0.0 copy-start.4
  57.1 0.3 collective-permute-done.3.far1_ref
  57.4 0.0 copy-done.2
  57.4 0.5 copy-done.4
  58.0 20.6 %backward.1 = (bf16[1024,512]{1,0:T(8,128)(2,1)}, f32[1024,512]{1,0:T(8,128)}, f32[4,512,128]{2,1,0:T(8,128)}, bf16[32,128,128]{2,1,0:T(8,128)(2,1)}) custom-call(s32[1]{0:T(128)} %bitcast._, bf16[1024,512]{1,0:T(8,128)(2,1)} %own_ref.1, bf16[1024,512]{1,0:T(8,128)(2,1)} %copy-done.3, bf16[1024,512]{1,0:T(8,128)(2,1)} %collective-permute-done.1.right_ref, ...), custom_call_target="tpu_custom_call" | custom-call | flops 21474836480 | bytes 25165824 | tf_op jit(solution)/shard_map/backward/pallas_call | solution.py:424
  78.6 25.6 %all_to_all.20.in_ref = bf16[32,128,128]{2,1,0:T(8,128)(2,1)} all-to-all(bf16[32,128,128]{2,1,0:T(8,128)(2,1)} %get-tuple-element.25), channel_id=1, replica_groups=mesh['seq'=32,'head'=4] {'seq'}, dimensions={0} | all-to-all | bytes 2097152 | tf_op jit(solution)/shard_map/all_to_all | solution.py:510
  104.2 2.4 %suffix_scan.1 = bf16[32,128,128]{2,1,0:T(8,128)(2,1)} custom-call(bf16[32,128,128]{2,1,0:T(8,128)(2,1)} %all_to_all.20.in_ref), custom_call_target="tpu_custom_call" | custom-call | bytes 2097152 | tf_op jit(solution)/shard_map/suffix_scan/pallas_call | solution.py:165
  106.6 22.0 %all_to_all.21.later_ref = bf16[32,128,128]{2,1,0:T(8,128)(2,1)} all-to-all(bf16[32,128,128]{2,1,0:T(8,128)(2,1)} %suffix_scan.1), channel_id=1, replica_groups=mesh['seq'=32,'head'=4] {'seq'}, dimensions={0} | all-to-all | bytes 2097152 | tf_op jit(solution)/shard_map/all_to_all | solution.py:510
  128.5 5.5 %finish_values.1 = (bf16[1024,512]{1,0:T(8,128)(2,1)}, f32[4,512,128]{2,1,0:T(8,128)}) custom-call(s32[1024,4]{1,0:T(8,128)} %copy.10.columns_ref.codes_ref, f32[1024,512]{1,0:T(8,128)} %get-tuple-element.24.local_ref, bf16[32,128,128]{2,1,0:T(8,128)(2,1)} %all_to_all.21.later_ref, f32[4,512,128]{2,1,0:T(8,128)} %get-tuple-element.26.part_ref), custom_call_target="tpu_custom_call" | custom-call | flops 1073741824 | bytes 4194304 | tf_op jit(solution)/shard_map/finish_values/pallas_call | solution.py:467
  (1 shorter events, 0.0 us)
Async XLA Ops:
  0.6 42.0 %collective-permute-start = (bf16[1024,512]{1,0:T(8,128)(2,1)}, bf16[1024,512]{1,0:T(8,128)(2,1)S(1)}, u32[]{:S(2)}, u32[]{:S(2)}) collective-permute-start(bf16[1024,512]{1,0:T(8,128)(2,1)} %own_ref.1), channel_id=1, source_target_pairs={{0,1},{1,2},{2,3},{3,0},{4,5},{5,6},{6,7},{7,4},{8,9},{9,10},{10,1... | collective-permute-start | bytes 3145736 | tf_op jit(solution)/shard_map/ppermute | solution.py:485
  2.7 40.0 %collective-permute-start.1 = (bf16[1024,512]{1,0:T(8,128)(2,1)}, bf16[1024,512]{1,0:T(8,128)(2,1)}, u32[]{:S(2)}, u32[]{:S(2)}) collective-permute-start(bf16[1024,512]{1,0:T(8,128)(2,1)} %own_ref.1), channel_id=1, source_target_pairs={{0,3},{1,0},{2,1},{3,2},{4,7},{5,4},{6,5},{7,6},{8,11},{9,8},{10,9... | collective-permute-start | bytes 3145736 | tf_op jit(solution)/shard_map/ppermute | solution.py:486
  7.2 14.2 %copy-start.1 = (bf16[4,512,128]{2,1,0:T(8,128)(2,1)S(1)}, bf16[4,512,128]{2,1,0:T(8,128)(2,1)}, u32[]{:S(2)}) copy-start(bf16[4,512,128]{2,1,0:T(8,128)(2,1)} %book_ref.1) | copy-start | bytes 1572868
  11.9 23.7 %all-to-all-start = ((bf16[32,96,128]{2,1,0:T(8,128)(2,1)}), bf16[32,96,128]{2,1,0:T(8,128)(2,1)S(1)}, u32[]{:S(2)}, u32[]{:S(2)}) async-start(bf16[32,96,128]{2,1,0:T(8,128)(2,1)} %get-tuple-element.16), calls=%async_computation | async-start | bytes 1572864 | tf_op jit(solution)/shard_map/all_to_all | solution.py:503
  35.6 0.9 copy-start
  38.5 17.4 %all-to-all-start.1 = ((bf16[32,64,128]{2,1,0:T(8,128)(2,1)}), bf16[32,64,128]{2,1,0:T(8,128)(2,1)S(1)}, u32[]{:S(2)}, u32[]{:S(2)}) async-start(bf16[32,64,128]{2,1,0:T(8,128)(2,1)} %get-tuple-element.21), calls=%async_computation.1 | async-start | bytes 1048576 | tf_op jit(solution)/shard_map/all_to_all | solution.py:504
  42.6 13.3 %copy-start.3 = (bf16[1024,512]{1,0:T(8,128)(2,1)}, bf16[1024,512]{1,0:T(8,128)(2,1)S(1)}, u32[]{:S(2)}) copy-start(bf16[1024,512]{1,0:T(8,128)(2,1)S(1)} %collective-permute-done.left_ref) | copy-start | bytes 3145732
  42.7 14.4 %collective-permute-start.2 = (bf16[512,512]{1,0:T(8,128)(2,1)S(1)}, bf16[512,512]{1,0:T(8,128)(2,1)S(1)}, u32[]{:S(2)}, u32[]{:S(2)}) collective-permute-start(bf16[512,512]{1,0:T(8,128)(2,1)S(1)} %slice.8), channel_id=1, source_target_pairs={{0,1},{1,2},{2,3},{3,0},{4,5},{5,6},{6,7},{7,4},{8,9},{9,10},{10,1... | collective-permute-start | bytes 1572872 | tf_op jit(solution)/shard_map/ppermute | solution.py:488
  44.1 13.3 %collective-permute-start.3 = (bf16[512,512]{1,0:T(8,128)(2,1)S(1)}, bf16[512,512]{1,0:T(8,128)(2,1)}, u32[]{:S(2)}, u32[]{:S(2)}) collective-permute-start(bf16[512,512]{1,0:T(8,128)(2,1)S(1)} %slice.9), channel_id=1, source_target_pairs={{0,3},{1,0},{2,1},{3,2},{4,7},{5,4},{6,5},{7,6},{8,11},{9,8},{10,9... | collective-permute-start | bytes 1572872 | tf_op jit(solution)/shard_map/ppermute | solution.py:488
  56.0 1.5 %copy-start.2 = (bf16[32,64,128]{2,1,0:T(8,128)(2,1)}, bf16[32,64,128]{2,1,0:T(8,128)(2,1)S(1)}, u32[]{:S(2)}) copy-start(bf16[32,64,128]{2,1,0:T(8,128)(2,1)S(1)} %all-to-all-done.1.prefix_ref) | copy-start | bytes 1572868
  57.1 0.8 copy-start.4

commit v4 on v3

v4 whole, which is shorter than its diff:
```python
import functools
import math

import jax
import jax.numpy as jnp
from jax import lax
from jax.experimental import pallas as pl
from jax.experimental.pallas import tpu as pltpu
from jax.sharding import PartitionSpec as P

BLOCK = 512
PART = 256
TILE = 128
HALF = 64
ROWS = 96
F32 = jnp.float32
BF16 = jnp.bfloat16
VMEM_LIMIT = 60 << 20


def dot(left, right):
    return lax.dot_general(left, right, (((1,), (0,)), ((), ())), preferred_element_type=F32)


def dot_nt(left, right):
    return lax.dot_general(left, right, (((1,), (1,)), ((), ())), preferred_element_type=F32)


def call(kernel, name, grid, in_specs, outs, scratch=(), aliases=None, prefetch=0, flops=0, size=0,
         limit=VMEM_LIMIT):
    return pl.pallas_call(
        kernel,
        grid_spec=pltpu.PrefetchScalarGridSpec(
            num_scalar_prefetch=prefetch,
            grid=grid,
            in_specs=in_specs,
            out_specs=[spec for _, _, spec in outs],
            scratch_shapes=list(scratch),
        ),
        out_shape=[jax.ShapeDtypeStruct(shape, dtype) for shape, dtype, _ in outs],
        input_output_aliases=aliases or {},
        compiler_params=pltpu.CompilerParams(
            dimension_semantics=("arbitrary",) * len(grid), vmem_limit_bytes=limit
        ),
        cost_estimate=pl.CostEstimate(flops=flops, bytes_accessed=size, transcendentals=0),
        name=name,
    )


def onehot_rows(codes_row, entries):
    entry = lax.broadcasted_iota(jnp.int32, (entries, codes_row.shape[1]), 0)
    return jnp.where(entry == codes_row, 1.0, 0.0).astype(BF16)


def row_at(ref, index):
    place = lax.broadcasted_iota(jnp.int32, ref.shape, 0)
    return jnp.sum(jnp.where(place == index, ref[...], 0), axis=0, keepdims=True)


def fold(array):
    rows, lanes = array.shape
    return jnp.sum(array.reshape(rows // 8, 8, lanes), axis=0)


def fold_max(array):
    rows, lanes = array.shape
    return jnp.max(array.reshape(rows // 8, 8, lanes), axis=0)


def sum_kernel(codes_ref, value_ref, send_ref, first_ref, first_count_ref):
    heads, entries, width = first_ref.shape
    slices = entries // HALF
    blocks = value_ref.shape[0] // BLOCK
    ones = jnp.ones((BLOCK, TILE), BF16)
    lines = []
    for h in range(heads):
        total = None
        for b in range(blocks):
            span = slice(b * BLOCK, (b + 1) * BLOCK)
            hot = onehot_rows(codes_ref[h : h + 1, span], entries)
            columns = value_ref[span, h * width : (h + 1) * width]
            part = dot(hot, jnp.concatenate([columns, ones], axis=1))
            if b == 0:
                first_ref[h] = part[:, :width]
                for i in range(entries // TILE):
                    rows = slice(i * TILE, (i + 1) * TILE)
                    first_count_ref[h, :, rows] = part[rows, width:].T[:1]
            total = part if b == 0 else total + part
        for k in range(slices):
            rows = slice(k * HALF, (k + 1) * HALF)
            send_ref[h * slices + k, :HALF, :] = total[rows, :width].astype(BF16)
        for i in range(entries // TILE):
            lines.append(total[i * TILE : (i + 1) * TILE, width:].T[:1])
    lines = jnp.concatenate(lines, axis=0)
    high = jnp.floor(lines * (1.0 / 256.0))
    digits = jnp.concatenate([high, lines - high * 256.0], axis=0).astype(BF16)
    for k in range(heads * slices):
        send_ref[k, HALF:, :] = digits


def own_sums(codes, values, heads, entries):
    width = values.shape[1] // heads
    slices = entries // HALF
    whole = lambda i: (0, 0, 0)
    return call(
        sum_kernel, "own_sums", (1,),
        [
            pl.BlockSpec(codes.shape, lambda i: (0, 0)),
            pl.BlockSpec(values.shape, lambda i: (0, 0)),
        ],
        [
            ((heads * slices, ROWS, TILE), BF16, pl.BlockSpec((heads * slices, ROWS, TILE), whole)),
            ((heads, entries, width), F32, pl.BlockSpec((heads, entries, width), whole)),
            ((heads, 1, entries), F32, pl.BlockSpec((heads, 1, entries), whole)),
        ],

    )(codes, values)


def prefix_kernel(me_ref, in_ref, first_ref, out_ref, count_ref):
    running = jnp.zeros(out_ref.shape[1:], F32)
    lines = (ROWS - HALF) // 2
    number = jnp.zeros((lines, TILE), F32)
    for d in range(in_ref.shape[0]):
        out_ref[d] = running.astype(BF16)
        running = running + in_ref[d, :HALF, :].astype(F32)
        digits = in_ref[d, HALF:, :].astype(F32)
        digits = digits[:lines] * 256.0 + digits[lines:]
        number = number + jnp.where(d < me_ref[0], digits, 0.0)
    heads = first_ref.shape[0]
    per = lines // heads
    for h in range(heads):
        for i in range(per):
            line = number[h * per + i : h * per + i + 1]
            columns = slice(i * TILE, (i + 1) * TILE)
            count_ref[0, h, :, columns] = line
            count_ref[1, h, :, columns] = line + first_ref[h, :, columns]


def prefix_scan(me, pieces, first):
    count = pieces.shape[0]
    heads, _, entries = first.shape
    whole = lambda i, *_: (0, 0, 0)
    shape = (2, heads, 1, entries)
    return call(
        prefix_kernel, "prefix_scan", (1,),
        [pl.BlockSpec(pieces.shape, whole), pl.BlockSpec(first.shape, whole)],
        [
            ((count, HALF, TILE), BF16, pl.BlockSpec((count, HALF, TILE), whole)),
            (shape, F32, pl.BlockSpec(shape, lambda i, *_: (0, 0, 0, 0))),
        ],
        prefetch=1
    )(me, pieces, first)


def suffix_kernel(in_ref, out_ref):
    running = jnp.zeros((HALF, TILE), F32)
    total = jnp.zeros((HALF, TILE), F32)
    for d in reversed(range(in_ref.shape[0])):
        out_ref[d, :HALF, :] = running.astype(BF16)
        running = running + in_ref[d, :HALF, :].astype(F32)
        total = total + in_ref[d, HALF:, :].astype(F32)
    low = total.astype(BF16)
    for d in range(in_ref.shape[0]):
        out_ref[d, HALF:, :] = low


def suffix_scan(pieces):
    spec = pl.BlockSpec(pieces.shape, lambda i: (0, 0, 0))
    return call(
        suffix_kernel, "suffix_scan", (1,), [spec], [(pieces.shape, BF16, spec)], size=2 << 20
    )(pieces)[0]


def count_columns(number):
    tiles = [
        jnp.broadcast_to(number[:, i * TILE : (i + 1) * TILE], (TILE, TILE)).T
        for i in range(number.shape[1] // TILE)
    ]
    return jnp.concatenate(tiles, axis=0)


def forward_kernel(codes_ref, query_ref, book_ref, book_t_ref, count_ref,
                   low_ref, keys_ref, rows_k, counts, scores):
    entries, width = book_ref.shape[1:]
    head = pl.program_id(0)
    entry_tiles = entries // TILE
    factor = width ** -0.5 * math.log2(math.e)
    causal = lax.broadcasted_iota(jnp.int32, (TILE, TILE), 1) >= lax.broadcasted_iota(
        jnp.int32, (TILE, TILE), 0
    )
    parts = BLOCK // PART
    blocks = low_ref.shape[0]

    codes_row = row_at(codes_ref, head)

    def prepare(b):
        keys_t = dot(
            book_t_ref[0], onehot_rows(codes_row[:, b * BLOCK : (b + 1) * BLOCK], entries)
        )
        keys_ref[b, 0] = keys_t.astype(BF16)
        rows_k[b, :entries, :] = book_ref[0]
        rows_k[b, entries:, :] = keys_t.T.astype(BF16)
        counts[b] = count_columns(count_ref[b, 0])

    def multiply(b, n):
        used = entries + PART * (n + 1)
        at = b * BLOCK + n * PART
        scores[b, n, :used, :] = dot_nt(rows_k[b, :used, :], query_ref[at : at + PART, :])

    def soften(b, n):
        used = entries + PART * (n + 1)
        for j in range(PART // TILE):
            columns = slice(j * TILE, (j + 1) * TILE)
            target = slice(n * PART + j * TILE, n * PART + (j + 1) * TILE)
            pieces = range(entry_tiles + 2 * n + j + 1)
            top = jnp.full((8, TILE), -jnp.inf, F32)
            for i in pieces:
                rows = slice(i * TILE, (i + 1) * TILE)
                piece = scores[b, n, rows, columns]
                if i < entry_tiles:
                    piece = jnp.where(counts[b, rows, :] > 0.0, piece, -jnp.inf)
                    scores[b, n, rows, columns] = piece
                elif i == pieces[-1]:
                    piece = jnp.where(causal, piece, -jnp.inf)
                    scores[b, n, rows, columns] = piece
                top = jnp.maximum(top, fold_max(piece))
            top = jnp.max(top, axis=0, keepdims=True)
            total = jnp.zeros((8, TILE), F32)
            for i in pieces:
                rows = slice(i * TILE, (i + 1) * TILE)
                piece = jnp.exp2((scores[b, n, rows, columns] - top) * factor)
                scores[b, n, rows, columns] = piece
                if i < entry_tiles:
                    piece = piece * counts[b, rows, :]
                total = total + fold(piece)
            inverse = 1.0 / jnp.sum(total, axis=0, keepdims=True)
            for i in pieces:
                rows = slice(i * TILE, (i + 1) * TILE)
                low_ref[b, 0, rows, target] = (scores[b, n, rows, columns] * inverse).astype(BF16)
            if j == 0:
                low_ref[b, 0, used - TILE : used, target] = jnp.zeros((TILE, TILE), BF16)

    order = [(b, n) for b in range(blocks) for n in range(parts)]
    for b in range(blocks):
        prepare(b)
    multiply(*order[0])
    for k, item in enumerate(order):
        if k + 1 < len(order):
            multiply(*order[k + 1])
        soften(*item)


def forward(codes, queries, book, book_t, counts):
    heads, entries, width = book.shape
    tokens = queries.shape[0]
    blocks = tokens // BLOCK
    both = entries + BLOCK
    by_head = lambda h: (h, 0, 0)
    in_blocks = lambda h: (0, h, 0, 0)
    return call(
        forward_kernel, "forward", (heads,),
        [
            pl.BlockSpec(codes.shape, lambda h: (0, 0)),
            pl.BlockSpec((tokens, width), lambda h: (0, h)),
            pl.BlockSpec((1, entries, width), by_head),
            pl.BlockSpec((1, width, entries), by_head),
            pl.BlockSpec((blocks, 1, 1, entries), in_blocks),
        ],
        [
            ((blocks, heads, both, BLOCK), BF16, pl.BlockSpec((blocks, 1, both, BLOCK), in_blocks)),
            ((blocks, heads, width, BLOCK), BF16, pl.BlockSpec((blocks, 1, width, BLOCK), in_blocks)),
        ],
        [
            pltpu.VMEM((blocks, both, width), BF16),
            pltpu.VMEM((blocks, entries, TILE), F32),
            pltpu.VMEM((blocks, 2, both, PART), F32),
        ],

    )(codes, queries, book, book_t, counts)


def cotangent_kernel(_, own_ref, left_ref, right_ref, far_ref, own_w, left_w, right_w, far_w,
                     out_ref):
    heads, rows, width = out_ref.shape
    total = dot_nt(own_ref[...], own_w[...]) + dot_nt(left_ref[...], left_w[...])
    total = total + dot_nt(right_ref[...], right_w[...]) + dot_nt(far_ref[...], far_w[...])
    for h in range(heads):
        out_ref[h] = total[:, h * width : (h + 1) * width].astype(BF16)


def cotangent(me, block, pieces, weight, heads):
    width = weight.shape[0] // heads
    columns = weight.shape[1] // 4

    def chunk(offset):
        return pl.BlockSpec(
            (weight.shape[0], columns), lambda n, me: (0, lax.rem(me[0] + offset, 4))
        )

    rows = pl.BlockSpec((PART, columns), lambda n, *_: (2 * block + n, 0))
    return call(
        cotangent_kernel, f"cotangent_{block}", (2,),
        [
            rows, rows, rows, pl.BlockSpec((PART, columns), lambda n, *_: (n, 0)), chunk(0), chunk(3), chunk(1), chunk(2),
        ],
        [((heads, BLOCK, width), BF16, pl.BlockSpec((heads, PART, width), lambda n, *_: (0, n, 0)))],
        prefetch=1, flops=1 << 30, size=5 << 20,
    )(me, *pieces, *[weight] * 4)[0]


def backward_kernel(block, refs):
    (codes_ref, query_ref, value_ref, dout_ref, probs_ref, keys_ref, book_t_ref, prefix_ref,
     count_ref) = refs[:9]
    if block == 0:
        grad_query_ref, local_ref, part_ref, code_ref = refs[9:13]
    else:
        first_ref, part0_ref, code0_ref = refs[9:12]
        grad_query_ref, local_ref, part_ref, send_ref = refs[14:18]
    hot, rows_v, counts, grads, score_grad, key_grad, wide_t = refs[-7:]
    width, entries = book_t_ref.shape[1:]
    entry_tiles = entries // TILE
    parts = BLOCK // PART
    scale = width ** -0.5
    codes_row = row_at(codes_ref, pl.program_id(0))
    hot[...] = onehot_rows(codes_row[:, block * BLOCK : (block + 1) * BLOCK], entries)
    wide_t[:, :entries] = book_t_ref[0]
    wide_t[:, entries:] = keys_ref[0, 0]
    sums = prefix_ref[...].reshape(entries, width)
    if block > 0:
        sums = (sums.astype(F32) + first_ref[0]).astype(BF16)
    rows_v[:entries, :] = sums
    rows_v[entries:, :] = value_ref[...]
    counts[...] = count_columns(count_ref[0, 0])

    def multiply(n):
        used = entries + PART * (n + 1)
        grads[n, :used, :] = dot_nt(rows_v[:used, :], dout_ref[0, n * PART : (n + 1) * PART, :])

    def combine(n):
        used = entries + PART * (n + 1)
        for j in range(PART // TILE):
            columns = slice(j * TILE, (j + 1) * TILE)
            source = slice(n * PART + j * TILE, n * PART + (j + 1) * TILE)
            pieces = range(entry_tiles + 2 * n + j + 1)
            delta = jnp.zeros((8, TILE), F32)
            for i in pieces:
                rows = slice(i * TILE, (i + 1) * TILE)
                delta = delta + fold(
                    probs_ref[0, 0, rows, source].astype(F32) * grads[n, rows, columns]
                )
            delta = jnp.sum(delta, axis=0, keepdims=True) * scale
            for i in pieces:
                rows = slice(i * TILE, (i + 1) * TILE)
                shift = delta
                if i < entry_tiles:
                    shift = delta * counts[rows, :]
                piece = grads[n, rows, columns] * scale - shift
                piece = probs_ref[0, 0, rows, source].astype(F32) * piece
                score_grad[n, rows, columns] = piece.astype(BF16)
            if j == 0:
                score_grad[n, used - TILE : used, columns] = jnp.zeros((TILE, TILE), BF16)

    sums_k = []
    sums_v = []

    def outputs(n):
        used = entries + PART * (n + 1)
        span = slice(n * PART, (n + 1) * PART)
        sums_k.append(dot(score_grad[n, :used, :], query_ref[span, :]))
        grad_t = dot(wide_t[:, :used], score_grad[n, :used, :])
        grad_query_ref[span, :] = grad_t.T.astype(BF16)

    def shares(n):
        used = entries + PART * (n + 1)
        span = slice(n * PART, (n + 1) * PART)
        sums_v.append(dot(probs_ref[0, 0, :used, span], dout_ref[0, span, :]))

    middle = entries + PART
    multiply(0)
    multiply(1)
    combine(0)
    shares(0)
    shares(1)
    outputs(0)
    combine(1)
    outputs(1)
    first, last = sums_v
    local_ref[:PART, :] = first[entries:] + last[entries:middle]
    local_ref[PART:, :] = last[middle:]
    part = first[:entries] + last[:entries]
    part_ref[0] = part
    first, last = sums_k
    key_grad[:PART, :] = (first[entries:] + last[entries:middle]).astype(BF16)
    key_grad[PART:, :] = last[middle:].astype(BF16)
    code = first[:entries] + last[:entries] + dot(hot[...], key_grad[...])
    if block == 0:
        code_ref[0] = code
    else:
        part = part + part0_ref[0]
        code = code + code0_ref[0]
        for k in range(entries // HALF):
            rows = slice(k * HALF, (k + 1) * HALF)
            send_ref[k, :HALF, :] = part[rows].astype(BF16)
            send_ref[k, HALF:, :] = code[rows].astype(BF16)


def backward(block, codes, queries, values, dout, probs, keys, book_t, prefix, counts, extra=()):
    heads, width, entries = book_t.shape
    tokens = queries.shape[0]
    both = entries + BLOCK
    slices = entries // HALF
    by_head = lambda h: (h, 0, 0)
    in_blocks = lambda h: (block, h, 0, 0)
    rows_of = pl.BlockSpec((BLOCK, width), lambda h: (block, h))
    per_head = pl.BlockSpec((1, entries, width), by_head)
    in_specs = [
        pl.BlockSpec(codes.shape, lambda h: (0, 0)),
        rows_of,
        rows_of,
        pl.BlockSpec((1, BLOCK, width), by_head),
        pl.BlockSpec((1, 1, both, BLOCK), in_blocks),
        pl.BlockSpec((1, 1, width, BLOCK), in_blocks),
        pl.BlockSpec((1, width, entries), by_head),
        pl.BlockSpec((slices, HALF, width), by_head),
        pl.BlockSpec((1, 1, 1, entries), in_blocks),
    ]
    outs = [
        (queries.shape, BF16, rows_of),
        (queries.shape, F32, rows_of),
        ((heads, entries, width), F32, per_head),
    ]
    aliases = None
    if block == 0:
        outs.append(((heads, entries, width), F32, per_head))
    else:
        in_specs += [per_head] * 3 + [pl.BlockSpec(memory_space=pl.ANY)] * 2
        aliases = {12: 0, 13: 1}
        outs.append(
            ((heads * slices, 2 * HALF, width), BF16,
             pl.BlockSpec((slices, 2 * HALF, width), by_head))
        )
    return call(
        lambda *refs: backward_kernel(block, refs), f"backward_{block}", (heads,), in_specs, outs,
        [
            pltpu.VMEM((entries, BLOCK), BF16),
            pltpu.VMEM((both, width), BF16),
            pltpu.VMEM((entries, TILE), F32),
            pltpu.VMEM((2, both, PART), F32),
            pltpu.VMEM((2, both, PART), BF16),
            pltpu.VMEM((BLOCK, width), BF16),
            pltpu.VMEM((width, both), BF16),
        ],
        aliases=aliases, flops=10 << 30, size=12 << 20,
    )(codes, queries, values, dout, probs, keys, book_t, prefix, counts, *extra)


def finish_kernel(codes_ref, local_ref, later_ref, part_ref, out_ref, book_ref):
    entries, width = part_ref.shape[1:]
    head = pl.program_id(0)
    codes_row = row_at(codes_ref, head)
    pieces = later_ref[...]
    later = pieces[:, :HALF, :].reshape(entries, width)
    book_ref[0] = pieces[:, HALF:, :].reshape(entries, width).astype(F32)
    tokens = local_ref.shape[0]
    tables = [later] * (tokens // BLOCK)
    tables[0] = (later.astype(F32) + part_ref[0]).astype(BF16)
    levels = lax.broadcasted_iota(jnp.int32, (TILE, TILE), 1)
    for i in range(tokens // TILE):
        rows = slice(i * TILE, (i + 1) * TILE)
        column = jnp.broadcast_to(codes_row[:, rows], (TILE, TILE)).T
        hot = jnp.concatenate(
            [
                jnp.where(levels + k * TILE == column, 1.0, 0.0).astype(BF16)
                for k in range(entries // TILE)
            ],
            axis=1,
        )
        out_ref[rows, :] = (local_ref[rows, :] + dot(hot, tables[i * TILE // BLOCK])).astype(BF16)


def finish(codes, local, later, part):
    heads, entries, width = part.shape
    tokens = local.shape[0]
    by_head = lambda h: (h, 0, 0)
    rows_of = pl.BlockSpec((tokens, width), lambda h: (0, h))
    per_head = pl.BlockSpec((1, entries, width), by_head)
    return call(
        finish_kernel, "finish_values", (heads,),
        [
            pl.BlockSpec(codes.shape, lambda h: (0, 0)),
            rows_of,
            pl.BlockSpec((entries // HALF, 2 * HALF, width), by_head),
            per_head,
        ],
        [(local.shape, BF16, rows_of), (part.shape, F32, per_head)],
        flops=1 << 30, size=8 << 20,
    )(codes, local, later, part)


def moved(array, step):
    count = lax.axis_size("head")
    return lax.ppermute(array, "head", [(i, (i + step) % count) for i in range(count)])


def per_device(queries, values, codes, codebook, out_weight, grad_out):
    heads, entries, width = codebook.shape
    exchange = functools.partial(
        lax.all_to_all, axis_name="seq", split_axis=0, concat_axis=0, tiled=True
    )
    me_seq = lax.axis_index("seq").astype(jnp.int32).reshape(1)
    me_head = lax.axis_index("head").astype(jnp.int32).reshape(1)
    left, right = moved(grad_out, 1), moved(grad_out, -1)
    far = [moved(grad_out[b * BLOCK : (b + 1) * BLOCK], 2) for b in range(2)]
    codes = codes.T
    book_t = jnp.swapaxes(codebook, 1, 2)
    send, first, first_count = own_sums(codes, values, heads, entries)
    prefix, counts = prefix_scan(me_seq, exchange(send), first_count)
    prefix, left, right = lax.optimization_barrier((prefix, left, right))
    prefix = exchange(prefix)
    probs, keys = forward(codes, queries, codebook, book_t, counts)
    extra = ()
    for b in range(2):
        if extra:
            far[b], part = lax.optimization_barrier((far[b], part))
            extra = (first, part, *extra[2:])
        dout = cotangent(me_head, b, (grad_out, left, right, far[b]), out_weight, heads)
        grad_query, local, part, last = backward(
            b, codes, queries, values, dout, probs, keys, book_t, prefix, counts, extra
        )
        extra = (first, part, last, grad_query, local)
    later = exchange(suffix_scan(exchange(last)))
    grad_values, grad_book = finish(codes, local, later, part)
    return grad_query, grad_values, grad_book


def solution(mesh):
    rows = P("seq", "head")
    return jax.shard_map(
        per_device,
        mesh=mesh,
        in_specs=(rows, rows, rows, P("head", None, None), P("head", None), rows),
        out_specs=(rows, rows, P("head", None, None)),
        check_vma=False,
    )
```

time: 135 us -> 145 us (1.074)
  starting transfers between devices: 19.6 us -> 31.7 us
  Pallas kernels: 44.7 us -> 51.4 us
  local copies, waits for them, and re-layouts: 6.9 us -> 2.87 us
  waiting for transfers between devices: 14.6 us -> 11.2 us
    all_to_all x1, starting transfers between devices: 4.11 us -> 17.2 us  [per_device(): prefix = exchange(prefix)]
    pallas_call x4 -> x7, Pallas kernels: 40.2 us -> 46.9 us  [the longest x2 20.5 us: backward(): call(lambda *refs: backward_kernel(block, refs), f'backward_{block}', (he...]
    unnamed x12 -> x11, local copies, waits for them, and re-layouts: 4.22 us -> 1.83 us
    all_to_all x1, waiting for transfers between devices: 13.2 us -> 11.2 us  [per_device(): prefix, counts = prefix_scan(me_seq, exchange(send), first_count)]
    ppermute x4, waiting for transfers between devices: 1.46 us -> 0.01 us  [moved(): lax.ppermute(array, 'head', [(i, (i + step) % count) for i in range(count)])]
  transfers between devices with their start and end apart: 6 -> 6, of which waited for: 3 -> 1; matrix products, arithmetic and copies ran while one was open for 4% -> 1% of each run, Pallas kernels for 12% -> 20%
where the time goes in v4:
time: 145 us
  Pallas kernels  51.4 us (35%)
  blocking collectives  46.6 us (32%)
  starting transfers between devices  31.7 us (22%)
  waiting for transfers between devices  11.2 us (8%)
  local copies, waits for them, and re-layouts  2.87 us (2%)
    all_to_all x2, blocking collectives, per_device(): later = exchange(suffix_scan(exchange(last)))  46.6 us
    pallas_call x2, Pallas kernels, backward(): call(lambda *refs: backward_kernel(block, refs), f'backward_{block}', (he...  20.5 us
    all_to_all x1, starting transfers between devices, per_device(): prefix = exchange(prefix)  17.2 us
    all_to_all x1, waiting for transfers between devices, per_device(): prefix, counts = prefix_scan(me_seq, exchange(send), first_count)  11.2 us
    pallas_call x1, Pallas kernels, forward(): call(forward_kernel, 'forward', (heads,), [pl.BlockSpec(codes.shape, lamb...  9.35 us
    all_to_all x1, starting transfers between devices, per_device(): prefix, counts = prefix_scan(me_seq, exchange(send), first_count)  9.1 us
    pallas_call x2, Pallas kernels, cotangent(): call(cotangent_kernel, f'cotangent_{block}', (2,), [rows, rows, rows, pl....  8.43 us
    ppermute x4, starting transfers between devices, moved(): lax.ppermute(array, 'head', [(i, (i + step) % count) for i in range(count)])  5.47 us
  transfers between devices with their start and end apart: 6, of which 1 were waited for; matrix products, arithmetic and copies ran while one was open for 1% of the time, Pallas kernels for 20%

profile of v4, /device:TPU:1, one launch (start us, length us, event | category | flops | bytes accessed | tf_op | source)
XLA Modules:
  0.0 144.6 jit_solution(14625209329179152551)
XLA Ops:
  0.6 0.0 copy-start
  0.6 3.4 %collective-permute-start.1 = (bf16[1024,512]{1,0:T(8,128)(2,1)}, bf16[1024,512]{1,0:T(8,128)(2,1)S(1)}, u32[]{:S(2)}, u32[]{:S(2)}) collective-permute-start(bf16[1024,512]{1,0:T(8,128)(2,1)} %own_ref.3), channel_id=1, source_target_pairs={{0,3},{1,0},{2,1},{3,2},{4,7},{5,4},{6,5},{7,6},{8,11},{9,8},{10,9... | collective-permute-start | bytes 3145736 | tf_op jit(solution)/shard_map/ppermute | solution.py:503
  4.0 0.0 collective-permute-start
  4.0 3.7 %own_sums.1 = (bf16[32,96,128]{2,1,0:T(8,128)(2,1)}, f32[4,512,128]{2,1,0:T(8,128)}, f32[4,1,512]{2,1,0:T(1,128)}) custom-call(s32[4,1024]{1,0:T(4,128)} %bitcast.7, bf16[1024,512]{1,0:T(8,128)(2,1)} %refs_2_.3), custom_call_target="tpu_custom_call" | custom-call | tf_op jit(solution)/shard_map/own_sums/pallas_call | solution.py:105
  7.8 9.1 %all-to-all-start = ((bf16[32,96,128]{2,1,0:T(8,128)(2,1)}), bf16[32,96,128]{2,1,0:T(8,128)(2,1)}, u32[]{:S(2)}, u32[]{:S(2)}) async-start(bf16[32,96,128]{2,1,0:T(8,128)(2,1)} %get-tuple-element.25), calls=%async_computation | async-start | bytes 1572864 | tf_op jit(solution)/shard_map/all_to_all | solution.py:518
  16.9 0.0 copy-done
  16.9 1.0 fusion
  17.9 0.0 copy-start.3
  17.9 2.0 %collective-permute-start.3 = (bf16[512,512]{1,0:T(8,128)(2,1)}, bf16[512,512]{1,0:T(8,128)(2,1)S(1)}, u32[]{:S(2)}, u32[]{:S(2)}) collective-permute-start(bf16[512,512]{1,0:T(8,128)(2,1)} %get-tuple-element.47), channel_id=1, source_target_pairs={{0,2},{1,3},{2,0},{3,1},{4,6},{5,7},{6,4},{7,5},{8,10},{9,11},{10,... | collective-permute-start | bytes 1572872 | tf_op jit(solution)/shard_map/ppermute | solution.py:503
  19.9 11.2 %all-to-all-done.in_ref = bf16[32,96,128]{2,1,0:T(8,128)(2,1)} async-done(((bf16[32,96,128]{2,1,0:T(8,128)(2,1)}), bf16[32,96,128]{2,1,0:T(8,128)(2,1)}, u32[]{:S(2)}, u32[]{:S(2)}) %all-to-all-start) | async-done | bytes 786464 | tf_op jit(solution)/shard_map/all_to_all | solution.py:518
  31.1 2.1 %prefix_scan.1 = (bf16[32,64,128]{2,1,0:T(8,128)(2,1)}, f32[2,4,1,512]{3,2,1,0:T(1,128)}) custom-call(s32[1]{0:T(128)} %bitcast.2.me_ref, bf16[32,96,128]{2,1,0:T(8,128)(2,1)} %all-to-all-done.in_ref, f32[4,1,512]{2,1,0:T(1,128)} %get-tuple-element.26.first_ref), custom_call_target="tpu_custom_call" | custom-call | tf_op jit(solution)/shard_map/prefix_scan/pallas_call | solution.py:145
  33.2 0.0 collective-permute-done.1.right_ref
  33.2 0.0 copy-start.1
  33.2 0.0 collective-permute-done.left_ref
  33.2 0.0 copy-start.2
  33.2 17.2 %all-to-all-start.1 = ((bf16[32,64,128]{2,1,0:T(8,128)(2,1)}), bf16[32,64,128]{2,1,0:T(8,128)(2,1)}, u32[]{:S(2)}, u32[]{:S(2)}) async-start(bf16[32,64,128]{2,1,0:T(8,128)(2,1)} %get-tuple-element.33), calls=%async_computation.1 | async-start | bytes 1048576 | tf_op jit(solution)/shard_map/all_to_all | solution.py:520
  50.4 0.1 collective-permute-start.2
  50.5 0.0 copy-done.3
  50.5 1.0 copy.11
  51.5 9.4 %forward.1 = (bf16[2,4,1024,512]{3,2,1,0:T(8,128)(2,1)}, bf16[2,4,128,512]{3,2,1,0:T(8,128)(2,1)}) custom-call(s32[4,1024]{1,0:T(4,128)} %bitcast.8, bf16[1024,512]{1,0:T(8,128)(2,1)} %refs_1_.3, bf16[4,512,128]{2,1,0:T(8,128)(2,1)} %book_ref.1, bf16[4,128,512]{2,1,0:T(8,128)(2,1)} %bitcast.4, f32[2,4,1,512]{3,2,1,0:T(1,128)} %get-tuple-element.30.count_ref.refs_8_), custom_call_target="tpu_custom_call" | custom-call | tf_op jit(solution)/shard_map/forward/pallas_call | solution.py:261
  60.9 0.0 copy-done.1
  60.9 0.0 copy-done.2
  60.9 0.0 collective-permute-done.3.far_ref
  60.9 0.0 copy-start.4
  60.9 0.8 copy-done.4
  61.7 4.2 %cotangent_0.1.refs_3_ = bf16[4,512,128]{2,1,0:T(8,128)(2,1)} custom-call(s32[1]{0:T(128)} %bitcast.1._, bf16[1024,512]{1,0:T(8,128)(2,1)} %own_ref.3, bf16[1024,512]{1,0:T(8,128)(2,1)} %copy-done.2, bf16[1024,512]{1,0:T(8,128)(2,1)} %copy-done.1, bf16[512,512]{1,0:T(8,128)(2,1)} %copy-done.4, bf16[512,2048]{1,0:T(8,128)(2,1)} %far_w.3, ...), custom_call_target="tpu_custom_call" | custom-call | flops 1073741824 | bytes 5242880 | tf_op jit(solution)/shard_map/cotangent_0/pallas_call | solution.py:302
  65.9 0.0 all-to-all-done.1.refs_7_
  65.9 10.2 %backward_0.1 = (bf16[1024,512]{1,0:T(8,128)(2,1)}, f32[1024,512]{1,0:T(8,128)}, f32[4,512,128]{2,1,0:T(8,128)}, f32[4,512,128]{2,1,0:T(8,128)}) custom-call(s32[4,1024]{1,0:T(4,128)} %bitcast.9, bf16[1024,512]{1,0:T(8,128)(2,1)} %refs_1_.3, bf16[1024,512]{1,0:T(8,128)(2,1)} %refs_2_.3, bf16[4,512,128]{2,1,0:T(8,128)(2,1)} %cotangent_0.1.refs_3_, ...), custom_call_target="tpu_custom_call" | custom-call | flops 10737418240 | bytes 12582912 | tf_op jit(solution)/shard_map/backward_0/pallas_call | solution.py:443
  76.1 0.0 collective-permute-done.2.far_ref
  76.1 4.2 %cotangent_1.1.refs_3_ = bf16[4,512,128]{2,1,0:T(8,128)(2,1)} custom-call(s32[1]{0:T(128)} %bitcast.1._, bf16[1024,512]{1,0:T(8,128)(2,1)} %own_ref.3, bf16[1024,512]{1,0:T(8,128)(2,1)} %copy-done.2, bf16[1024,512]{1,0:T(8,128)(2,1)} %copy-done.1, bf16[512,512]{1,0:T(8,128)(2,1)} %collective-permute-done.2.far_ref, bf16[512,2048]{1,0:T(8,128)(2,1)} %far_w.3, ...), custom_call_target="tpu_custom_call" | custom-call | flops 1073741824 | bytes 5242880 | tf_op jit(solution)/shard_map/cotangent_1/pallas_call | solution.py:302
  80.3 10.3 %backward_1.1 = (bf16[1024,512]{1,0:T(8,128)(2,1)}, f32[1024,512]{1,0:T(8,128)}, f32[4,512,128]{2,1,0:T(8,128)}, bf16[32,128,128]{2,1,0:T(8,128)(2,1)}) custom-call(s32[4,1024]{1,0:T(4,128)} %bitcast.10, bf16[1024,512]{1,0:T(8,128)(2,1)} %refs_1_.3, bf16[1024,512]{1,0:T(8,128)(2,1)} %refs_2_.3, ...), custom_call_target="tpu_custom_call", output_to_operand_aliasing={{0}: (12, {}), {1}: (13, {})} | custom-call | flops 10737418240 | bytes 12582912 | tf_op jit(solution)/shard_map/backward_1/pallas_call | solution.py:443
  90.6 24.7 %all_to_all.20.in_ref = bf16[32,128,128]{2,1,0:T(8,128)(2,1)} all-to-all(bf16[32,128,128]{2,1,0:T(8,128)(2,1)} %get-tuple-element.43), channel_id=1, replica_groups=mesh['seq'=32,'head'=4] {'seq'}, dimensions={0} | all-to-all | bytes 2097152 | tf_op jit(solution)/shard_map/all_to_all | solution.py:532
  115.3 2.4 %suffix_scan.1 = bf16[32,128,128]{2,1,0:T(8,128)(2,1)} custom-call(bf16[32,128,128]{2,1,0:T(8,128)(2,1)} %all_to_all.20.in_ref), custom_call_target="tpu_custom_call" | custom-call | bytes 2097152 | tf_op jit(solution)/shard_map/suffix_scan/pallas_call | solution.py:170
  117.7 22.0 %all_to_all.21.later_ref = bf16[32,128,128]{2,1,0:T(8,128)(2,1)} all-to-all(bf16[32,128,128]{2,1,0:T(8,128)(2,1)} %suffix_scan.1), channel_id=1, replica_groups=mesh['seq'=32,'head'=4] {'seq'}, dimensions={0} | all-to-all | bytes 2097152 | tf_op jit(solution)/shard_map/all_to_all | solution.py:532
  139.7 4.9 %finish_values.1 = (bf16[1024,512]{1,0:T(8,128)(2,1)}, f32[4,512,128]{2,1,0:T(8,128)}) custom-call(s32[4,1024]{1,0:T(4,128)} %bitcast.11, f32[1024,512]{1,0:T(8,128)} %get-tuple-element.42.local_ref, bf16[32,128,128]{2,1,0:T(8,128)(2,1)} %all_to_all.21.later_ref, f32[4,512,128]{2,1,0:T(8,128)} %get-tuple-element.44.part_ref), custom_call_target="tpu_custom_call" | custom-call | flops 1073741824 | bytes 8388608 | tf_op jit(solution)/shard_map/finish_values/pallas_call | solution.py:488
Async XLA Ops:
  0.6 16.2 %copy-start = (bf16[1024,512]{1,0:T(8,128)(2,1)S(1)}, bf16[1024,512]{1,0:T(8,128)(2,1)}, u32[]{:S(2)}) copy-start(bf16[1024,512]{1,0:T(8,128)(2,1)} %own_ref.3) | copy-start | bytes 3145732
  0.6 32.6 %collective-permute-start.1 = (bf16[1024,512]{1,0:T(8,128)(2,1)}, bf16[1024,512]{1,0:T(8,128)(2,1)S(1)}, u32[]{:S(2)}, u32[]{:S(2)}) collective-permute-start(bf16[1024,512]{1,0:T(8,128)(2,1)} %own_ref.3), channel_id=1, source_target_pairs={{0,3},{1,0},{2,1},{3,2},{4,7},{5,4},{6,5},{7,6},{8,11},{9,8},{10,9... | collective-permute-start | bytes 3145736 | tf_op jit(solution)/shard_map/ppermute | solution.py:503
  4.0 29.2 %collective-permute-start = (bf16[1024,512]{1,0:T(8,128)(2,1)}, bf16[1024,512]{1,0:T(8,128)(2,1)S(1)}, u32[]{:S(2)}, u32[]{:S(2)}) collective-permute-start(bf16[1024,512]{1,0:T(8,128)(2,1)} %own_ref.3), channel_id=1, source_target_pairs={{0,1},{1,2},{2,3},{3,0},{4,5},{5,6},{6,7},{7,4},{8,9},{9,10},{10,1... | collective-permute-start | bytes 3145736 | tf_op jit(solution)/shard_map/ppermute | solution.py:503
  7.8 23.4 %all-to-all-start = ((bf16[32,96,128]{2,1,0:T(8,128)(2,1)}), bf16[32,96,128]{2,1,0:T(8,128)(2,1)}, u32[]{:S(2)}, u32[]{:S(2)}) async-start(bf16[32,96,128]{2,1,0:T(8,128)(2,1)} %get-tuple-element.25), calls=%async_computation | async-start | bytes 1572864 | tf_op jit(solution)/shard_map/all_to_all | solution.py:518
  17.9 32.6 %copy-start.3 = (bf16[4,512,128]{2,1,0:T(8,128)(2,1)S(1)}, bf16[4,512,128]{2,1,0:T(8,128)(2,1)}, u32[]{:S(2)}) copy-start(bf16[4,512,128]{2,1,0:T(8,128)(2,1)} %book_ref.1) | copy-start | bytes 1572868
  17.9 43.0 %collective-permute-start.3 = (bf16[512,512]{1,0:T(8,128)(2,1)}, bf16[512,512]{1,0:T(8,128)(2,1)S(1)}, u32[]{:S(2)}, u32[]{:S(2)}) collective-permute-start(bf16[512,512]{1,0:T(8,128)(2,1)} %get-tuple-element.47), channel_id=1, source_target_pairs={{0,2},{1,3},{2,0},{3,1},{4,6},{5,7},{6,4},{7,5},{8,10},{9,11},{10,... | collective-permute-start | bytes 1572872 | tf_op jit(solution)/shard_map/ppermute | solution.py:503
  33.2 27.7 %copy-start.1 = (bf16[1024,512]{1,0:T(8,128)(2,1)}, bf16[1024,512]{1,0:T(8,128)(2,1)S(1)}, u32[]{:S(2)}) copy-start(bf16[1024,512]{1,0:T(8,128)(2,1)S(1)} %collective-permute-done.1.right_ref) | copy-start | bytes 3145732
  33.2 27.7 %copy-start.2 = (bf16[1024,512]{1,0:T(8,128)(2,1)}, bf16[1024,512]{1,0:T(8,128)(2,1)S(1)}, u32[]{:S(2)}) copy-start(bf16[1024,512]{1,0:T(8,128)(2,1)S(1)} %collective-permute-done.left_ref) | copy-start | bytes 3145732
  33.2 32.7 %all-to-all-start.1 = ((bf16[32,64,128]{2,1,0:T(8,128)(2,1)}), bf16[32,64,128]{2,1,0:T(8,128)(2,1)}, u32[]{:S(2)}, u32[]{:S(2)}) async-start(bf16[32,64,128]{2,1,0:T(8,128)(2,1)} %get-tuple-element.33), calls=%async_computation.1 | async-start | bytes 1048576 | tf_op jit(solution)/shard_map/all_to_all | solution.py:520
  50.4 25.7 %collective-permute-start.2 = (bf16[512,512]{1,0:T(8,128)(2,1)}, bf16[512,512]{1,0:T(8,128)(2,1)}, u32[]{:S(2)}, u32[]{:S(2)}) collective-permute-start(bf16[512,512]{1,0:T(8,128)(2,1)} %get-tuple-element.48), channel_id=1, source_target_pairs={{0,2},{1,3},{2,0},{3,1},{4,6},{5,7},{6,4},{7,5},{8,10},{9,11},{10,... | collective-permute-start | bytes 1572872 | tf_op jit(solution)/shard_map/ppermute | solution.py:503
  60.9 0.8 copy-start.4

commit v5 on v3

--- a/solution.py
+++ b/solution.py
@@ -26,7 +26,8 @@
     return lax.dot_general(left, right, (((1,), (1,)), ((), ())), preferred_element_type=F32)
 
 
-def call(kernel, name, grid, in_specs, outs, scratch=(), aliases=None, prefetch=0, flops=0, size=0):
+def call(kernel, name, grid, in_specs, outs, scratch=(), aliases=None, prefetch=0, flops=0, size=0,
+         limit=VMEM_LIMIT):
     return pl.pallas_call(
         kernel,
         grid_spec=pltpu.PrefetchScalarGridSpec(
@@ -39,7 +40,7 @@
         out_shape=[jax.ShapeDtypeStruct(shape, dtype) for shape, dtype, _ in outs],
         input_output_aliases=aliases or {},
         compiler_params=pltpu.CompilerParams(
-            dimension_semantics=("arbitrary",) * len(grid), vmem_limit_bytes=VMEM_LIMIT
+            dimension_semantics=("arbitrary",) * len(grid), vmem_limit_bytes=limit
         ),
         cost_estimate=pl.CostEstimate(flops=flops, bytes_accessed=size, transcendentals=0),
         name=name,
@@ -51,6 +52,11 @@
     return jnp.where(entry == codes_row, 1.0, 0.0).astype(BF16)
 
 
+def row_at(ref, index):
+    place = lax.broadcasted_iota(jnp.int32, ref.shape, 0)
+    return jnp.sum(jnp.where(place == index, ref[...], 0), axis=0, keepdims=True)
+
+
 def fold(array):
     rows, lanes = array.shape
     return jnp.sum(array.reshape(rows // 8, 8, lanes), axis=0)
@@ -61,29 +67,30 @@
     return jnp.max(array.reshape(rows // 8, 8, lanes), axis=0)
 
 
-def sum_kernel(codes_ref, columns_ref, value_ref, send_ref, first_ref, first_count_ref):
+def sum_kernel(codes_ref, value_ref, send_ref, first_ref, first_count_ref):
     heads, entries, width = first_ref.shape
     slices = entries // HALF
     blocks = value_ref.shape[0] // BLOCK
-    levels = lax.broadcasted_iota(jnp.int32, (BLOCK, entries), 1)
+    ones = jnp.ones((BLOCK, TILE), BF16)
     lines = []
     for h in range(heads):
         total = None
-        number = None
         for b in range(blocks):
             span = slice(b * BLOCK, (b + 1) * BLOCK)
-            hot = onehot_rows(codes_ref[h, :, span], entries)
-            part = dot(hot, value_ref[span, h * width : (h + 1) * width])
-            same = jnp.where(levels == columns_ref[span, h : h + 1], 1.0, 0.0)
-            amount = jnp.sum(fold(same), axis=0, keepdims=True)
+            hot = onehot_rows(codes_ref[h : h + 1, span], entries)
+            columns = value_ref[span, h * width : (h + 1) * width]
+            part = dot(hot, jnp.concatenate([columns, ones], axis=1))
             if b == 0:
-                first_ref[h] = part
-                first_count_ref[h] = amount
+                first_ref[h] = part[:, :width]
+                for i in range(entries // TILE):
+                    rows = slice(i * TILE, (i + 1) * TILE)
+                    first_count_ref[h, :, rows] = part[rows, width:].T[:1]
             total = part if b == 0 else total + part
-            number = amount if b == 0 else number + amount
         for k in range(slices):
-            send_ref[h * slices + k, :HALF, :] = total[k * HALF : (k + 1) * HALF].astype(BF16)
-        lines += [number[:, i * TILE : (i + 1) * TILE] for i in range(entries // TILE)]
+            rows = slice(k * HALF, (k + 1) * HALF)
+            send_ref[h * slices + k, :HALF, :] = total[rows, :width].astype(BF16)
+        for i in range(entries // TILE):
+            lines.append(total[i * TILE : (i + 1) * TILE, width:].T[:1])
     lines = jnp.concatenate(lines, axis=0)
     high = jnp.floor(lines * (1.0 / 256.0))
     digits = jnp.concatenate([high, lines - high * 256.0], axis=0).astype(BF16)
@@ -91,15 +98,13 @@
         send_ref[k, HALF:, :] = digits
 
 
-def own_sums(codes_rows, codes, values, heads, entries):
-    tokens = values.shape[0]
+def own_sums(codes, values, heads, entries):
     width = values.shape[1] // heads
     slices = entries // HALF
     whole = lambda i: (0, 0, 0)
     return call(
         sum_kernel, "own_sums", (1,),
         [
-            pl.BlockSpec(codes_rows.shape, whole),
             pl.BlockSpec(codes.shape, lambda i: (0, 0)),
             pl.BlockSpec(values.shape, lambda i: (0, 0)),
         ],
@@ -108,8 +113,8 @@
             ((heads, entries, width), F32, pl.BlockSpec((heads, entries, width), whole)),
             ((heads, 1, entries), F32, pl.BlockSpec((heads, 1, entries), whole)),
         ],
-        flops=1 << 30, size=4 << 20,
-    )(codes_rows, codes, values)
+
+    )(codes, values)
 
 
 def prefix_kernel(me_ref, in_ref, first_ref, out_ref, count_ref):
@@ -144,7 +149,7 @@
             ((count, HALF, TILE), BF16, pl.BlockSpec((count, HALF, TILE), whole)),
             (shape, F32, pl.BlockSpec(shape, lambda i, *_: (0, 0, 0, 0))),
         ],
-        prefetch=1, size=1 << 20,
+        prefetch=1
     )(me, pieces, first)
 
 
@@ -178,6 +183,7 @@
 def forward_kernel(codes_ref, query_ref, book_ref, book_t_ref, count_ref,
                    low_ref, keys_ref, rows_k, counts, scores):
     entries, width = book_ref.shape[1:]
+    head = pl.program_id(0)
     entry_tiles = entries // TILE
     factor = width ** -0.5 * math.log2(math.e)
     causal = lax.broadcasted_iota(jnp.int32, (TILE, TILE), 1) >= lax.broadcasted_iota(
@@ -186,9 +192,11 @@
     parts = BLOCK // PART
     blocks = low_ref.shape[0]
 
+    codes_row = row_at(codes_ref, head)
+
     def prepare(b):
         keys_t = dot(
-            book_t_ref[0], onehot_rows(codes_ref[0, :, b * BLOCK : (b + 1) * BLOCK], entries)
+            book_t_ref[0], onehot_rows(codes_row[:, b * BLOCK : (b + 1) * BLOCK], entries)
         )
         keys_ref[b, 0] = keys_t.astype(BF16)
         rows_k[b, :entries, :] = book_ref[0]
@@ -243,7 +251,7 @@
         soften(*item)
 
 
-def forward(codes_rows, queries, book, book_t, counts):
+def forward(codes, queries, book, book_t, counts):
     heads, entries, width = book.shape
     tokens = queries.shape[0]
     blocks = tokens // BLOCK
@@ -253,7 +261,7 @@
     return call(
         forward_kernel, "forward", (heads,),
         [
-            pl.BlockSpec((1, 1, tokens), by_head),
+            pl.BlockSpec(codes.shape, lambda h: (0, 0)),
             pl.BlockSpec((tokens, width), lambda h: (0, h)),
             pl.BlockSpec((1, entries, width), by_head),
             pl.BlockSpec((1, width, entries), by_head),
@@ -268,8 +276,8 @@
             pltpu.VMEM((blocks, entries, TILE), F32),
             pltpu.VMEM((blocks, 2, both, PART), F32),
         ],
-        flops=6 << 30, size=12 << 20,
-    )(codes_rows, queries, book, book_t, counts)
+
+    )(codes, queries, book, book_t, counts)
 
 
 def backward_kernel(_, own_ref, left_ref, right_ref, far0_ref, far1_ref, own_w, left_w, right_w,
@@ -299,8 +307,10 @@
             for h in range(dout.shape[0]):
                 dout[h, span, :] = total[:, h * width : (h + 1) * width].astype(BF16)
 
+    codes_row = row_at(codes_ref, head)
+
     def prepare(b):
-        hot[b] = onehot_rows(codes_ref[0, :, b * BLOCK : (b + 1) * BLOCK], entries)
+        hot[b] = onehot_rows(codes_row[:, b * BLOCK : (b + 1) * BLOCK], entries)
         wide_t[b, :, :entries] = book_t_ref[0]
         wide_t[b, :, entries:] = keys_ref[b, 0]
         sums = prefix_ref[...].reshape(entries, width)
@@ -384,7 +394,7 @@
         send_ref[k, HALF:, :] = code[rows].astype(BF16)
 
 
-def backward(me, pieces, weight, codes_rows, queries, values, probs, keys, book_t, prefix, counts,
+def backward(me, pieces, weight, codes, queries, values, probs, keys, book_t, prefix, counts,
              first):
     heads, width, entries = book_t.shape
     tokens = queries.shape[0]
@@ -405,7 +415,7 @@
     in_specs = [pl.BlockSpec(piece.shape, lambda h, *_: (0, 0)) for piece in pieces]
     in_specs += [chunk(0), chunk(3), chunk(1), chunk(2)]
     in_specs += [
-        pl.BlockSpec((1, 1, tokens), by_head),
+        pl.BlockSpec(codes.shape, lambda h, *_: (0, 0)),
         rows_of,
         rows_of,
         pl.BlockSpec((blocks, 1, both, BLOCK), in_blocks),
@@ -434,47 +444,50 @@
             pltpu.VMEM((blocks, width, both), BF16),
         ],
         prefetch=1, flops=20 << 30, size=24 << 20,
-    )(me, *pieces, *[weight] * 4, codes_rows, queries, values, probs, keys, book_t, prefix, counts,
+    )(me, *pieces, *[weight] * 4, codes, queries, values, probs, keys, book_t, prefix, counts,
       first)
 
 
-def finish_kernel(codes_ref, local_ref, later_ref, part_ref, out_ref, book_ref, tables):
-    heads, entries, width = part_ref.shape
-    slices = entries // HALF
-    step = pl.program_id(0)
-
-    @pl.when(step == 0)
-    def _():
-        for h in range(heads):
-            pieces = later_ref[h * slices : (h + 1) * slices]
-            later = pieces[:, :HALF, :].reshape(entries, width)
-            tables[1, h] = later
-            tables[0, h] = (later.astype(F32) + part_ref[h]).astype(BF16)
-            book_ref[h] = pieces[:, HALF:, :].reshape(entries, width).astype(F32)
-
-    block = step // (pl.num_programs(0) // 2)
-    levels = lax.broadcasted_iota(jnp.int32, (codes_ref.shape[0], entries), 1)
-    for h in range(heads):
-        hot = jnp.where(levels == codes_ref[:, h : h + 1], 1.0, 0.0).astype(BF16)
-        columns = slice(h * width, (h + 1) * width)
-        out_ref[:, columns] = (local_ref[:, columns] + dot(hot, tables[block, h])).astype(BF16)
+def finish_kernel(codes_ref, local_ref, later_ref, part_ref, out_ref, book_ref):
+    entries, width = part_ref.shape[1:]
+    head = pl.program_id(0)
+    codes_row = row_at(codes_ref, head)
+    pieces = later_ref[...]
+    later = pieces[:, :HALF, :].reshape(entries, width)
+    book_ref[0] = pieces[:, HALF:, :].reshape(entries, width).astype(F32)
+    tokens = local_ref.shape[0]
+    tables = [later] * (tokens // BLOCK)
+    tables[0] = (later.astype(F32) + part_ref[0]).astype(BF16)
+    levels = lax.broadcasted_iota(jnp.int32, (TILE, TILE), 1)
+    for i in range(tokens // TILE):
+        rows = slice(i * TILE, (i + 1) * TILE)
+        column = jnp.broadcast_to(codes_row[:, rows], (TILE, TILE)).T
+        hot = jnp.concatenate(
+            [
+                jnp.where(levels + k * TILE == column, 1.0, 0.0).astype(BF16)
+                for k in range(entries // TILE)
+            ],
+            axis=1,
+        )
+        out_ref[rows, :] = (local_ref[rows, :] + dot(hot, tables[i * TILE // BLOCK])).astype(BF16)
 
 
 def finish(codes, local, later, part):
     heads, entries, width = part.shape
-    whole = lambda b: (0, 0, 0)
-    rows = pl.BlockSpec((PART, heads * width), lambda b: (b, 0))
+    tokens = local.shape[0]
+    by_head = lambda h: (h, 0, 0)
+    rows_of = pl.BlockSpec((tokens, width), lambda h: (0, h))
+    per_head = pl.BlockSpec((1, entries, width), by_head)
     return call(
-        finish_kernel, "finish_values", (local.shape[0] // PART,),
-        [
-            pl.BlockSpec((PART, heads), lambda b: (b, 0)),
-            rows,
-            pl.BlockSpec(later.shape, whole),
-            pl.BlockSpec(part.shape, whole),
-        ],
-        [(local.shape, BF16, rows), (part.shape, F32, pl.BlockSpec(part.shape, whole))],
-        [pltpu.VMEM((2, heads, entries, width), BF16)],
-        flops=1 << 30, size=4 << 20,
+        finish_kernel, "finish_values", (heads,),
+        [
+            pl.BlockSpec(codes.shape, lambda h: (0, 0)),
+            rows_of,
+            pl.BlockSpec((entries // HALF, 2 * HALF, width), by_head),
+            per_head,
+        ],
+        [(local.shape, BF16, rows_of), (part.shape, F32, per_head)],
+        flops=1 << 30, size=8 << 20,
     )(codes, local, later, part)
 
 
@@ -497,17 +510,17 @@
     me_seq = lax.axis_index("seq").astype(jnp.int32).reshape(1)
     me_head = lax.axis_index("head").astype(jnp.int32).reshape(1)
     pieces = ring_pieces(grad_out)
-    codes_rows = codes.T.reshape(heads, 1, -1)
+    codes = codes.T
     book_t = jnp.swapaxes(codebook, 1, 2)
-    send, first, first_count = own_sums(codes_rows, codes, values, heads, entries)
+    send, first, first_count = own_sums(codes, values, heads, entries)
     prefix, counts = prefix_scan(me_seq, exchange(send), first_count)
     prefix = exchange(prefix)
-    probs, keys = forward(codes_rows, queries, codebook, book_t, counts)
-    grad_query, local, part, send = backward(
-        me_head, pieces, out_weight, codes_rows, queries, values, probs, keys, book_t, prefix,
-        counts, first,
+    probs, keys = forward(codes, queries, codebook, book_t, counts)
+    grad_query, local, part, last = backward(
+        me_head, pieces, out_weight, codes, queries, values, probs, keys, book_t, prefix, counts,
+        first,
     )
-    later = exchange(suffix_scan(exchange(send)))
+    later = exchange(suffix_scan(exchange(last)))
     grad_values, grad_book = finish(codes, local, later, part)
     return grad_query, grad_values, grad_book
 

time: 135 us -> 131 us (0.970)
  starting transfers between devices: 19.6 us -> 25.3 us
  waiting for transfers between devices: 14.6 us -> 11.5 us
  local copies, waits for them, and re-layouts: 6.9 us -> 3.85 us
  blocking collectives: 47.6 us -> 45.5 us
  Pallas kernels: 44.7 us -> 43.1 us
    all_to_all x1, waiting for transfers between devices: 13.2 us -> 0.9 us  [per_device(): prefix, counts = prefix_scan(me_seq, exchange(send), first_count)]
    ppermute x1, waiting for transfers between devices: 0.01 us -> 9.37 us  [ring_pieces(): left = lax.ppermute(array, 'head', up)]
    all_to_all x1, starting transfers between devices: 4.11 us -> 9.62 us  [per_device(): prefix = exchange(prefix)]
    all_to_all x2, blocking collectives: 47.6 us -> 45.5 us  [per_device(): later = exchange(suffix_scan(exchange(last)))]
    pallas_call x3, Pallas kernels: 19.6 us -> 18 us  [the longest x1 9.32 us: forward(): call(forward_kernel, 'forward', (heads,), [pl.BlockSpec(codes.shape, lamb...]
    unnamed x12 -> x9, local copies, waits for them, and re-layouts: 4.22 us -> 2.74 us
  transfers between devices with their start and end apart: 6 -> 6, of which waited for: 3 -> 3; matrix products, arithmetic and copies ran while one was open for 4% -> 2% of each run, Pallas kernels for 12% -> 12%
where the time goes in v5:
time: 131 us; the launch traced here: 130 us
  blocking collectives  45.5 us (35%)
  Pallas kernels  43.1 us (33%)
  starting transfers between devices  25.3 us (19%)
  waiting for transfers between devices  11.5 us (9%)
  local copies, waits for them, and re-layouts  3.85 us (3%)
    all_to_all x2, blocking collectives, per_device(): later = exchange(suffix_scan(exchange(last)))  45.5 us
    pallas_call x1, Pallas kernels, backward(): call(backward_kernel, 'backward', (heads,), in_specs, outs, [pltpu.VMEM((...  20.7 us
    all_to_all x1, starting transfers between devices, per_device(): prefix = exchange(prefix)  9.62 us
    all_to_all x1, starting transfers between devices, per_device(): prefix, counts = prefix_scan(me_seq, exchange(send), first_count)  9.45 us
    ppermute x1, waiting for transfers between devices, ring_pieces(): left = lax.ppermute(array, 'head', up)  9.37 us
    pallas_call x1, Pallas kernels, forward(): call(forward_kernel, 'forward', (heads,), [pl.BlockSpec(codes.shape, lamb...  9.32 us
    pallas_call x1, Pallas kernels, finish(): call(finish_kernel, 'finish_values', (heads,), [pl.BlockSpec(codes.shape,...  4.93 us
    pallas_call x1, Pallas kernels, own_sums(): call(sum_kernel, 'own_sums', (1,), [pl.BlockSpec(codes.shape, lambda i: (...  3.73 us
  transfers between devices with their start and end apart: 6, of which 3 were waited for; matrix products, arithmetic and copies ran while one was open for 2% of the time, Pallas kernels for 12%

profile of v5, /device:TPU:1, one launch (start us, length us, event | category | flops | bytes accessed | tf_op | source)
XLA Modules:
  0.0 129.9 jit_solution(6215503273471069027)
XLA Ops:
  0.6 2.1 %collective-permute-start = (bf16[1024,512]{1,0:T(8,128)(2,1)}, bf16[1024,512]{1,0:T(8,128)(2,1)S(1)}, u32[]{:S(2)}, u32[]{:S(2)}) collective-permute-start(bf16[1024,512]{1,0:T(8,128)(2,1)} %own_ref.1), channel_id=1, source_target_pairs={{0,1},{1,2},{2,3},{3,0},{4,5},{5,6},{6,7},{7,4},{8,9},{9,10},{10,1... | collective-permute-start | bytes 3145736 | tf_op jit(solution)/shard_map/ppermute | solution.py:498
  2.7 1.4 %collective-permute-start.1 = (bf16[1024,512]{1,0:T(8,128)(2,1)}, bf16[1024,512]{1,0:T(8,128)(2,1)}, u32[]{:S(2)}, u32[]{:S(2)}) collective-permute-start(bf16[1024,512]{1,0:T(8,128)(2,1)} %own_ref.1), channel_id=1, source_target_pairs={{0,3},{1,0},{2,1},{3,2},{4,7},{5,4},{6,5},{7,6},{8,11},{9,8},{10,9... | collective-permute-start | bytes 3145736 | tf_op jit(solution)/shard_map/ppermute | solution.py:499
  4.1 3.7 %own_sums.1 = (bf16[32,96,128]{2,1,0:T(8,128)(2,1)}, f32[4,512,128]{2,1,0:T(8,128)}, f32[4,1,512]{2,1,0:T(1,128)}) custom-call(s32[4,1024]{1,0:T(4,128)} %bitcast.6, bf16[1024,512]{1,0:T(8,128)(2,1)} %value_ref.3), custom_call_target="tpu_custom_call" | custom-call | tf_op jit(solution)/shard_map/own_sums/pallas_call | solution.py:105
  7.8 9.4 %all-to-all-start = ((bf16[32,96,128]{2,1,0:T(8,128)(2,1)}), bf16[32,96,128]{2,1,0:T(8,128)(2,1)S(1)}, u32[]{:S(2)}, u32[]{:S(2)}) async-start(bf16[32,96,128]{2,1,0:T(8,128)(2,1)} %get-tuple-element.16), calls=%async_computation | async-start | bytes 1572864 | tf_op jit(solution)/shard_map/all_to_all | solution.py:516
  17.3 0.0 copy-start.1
  17.3 9.4 %collective-permute-done.left_ref = bf16[1024,512]{1,0:T(8,128)(2,1)S(1)} collective-permute-done((bf16[1024,512]{1,0:T(8,128)(2,1)}, bf16[1024,512]{1,0:T(8,128)(2,1)S(1)}, u32[]{:S(2)}, u32[]{:S(2)}) %collective-permute-start) | collective-permute-done | bytes 1048608 | tf_op jit(solution)/shard_map/ppermute | solution.py:498
  26.7 0.0 copy-start.3
  26.7 0.5 collective-permute-start.2
  27.2 0.0 collective-permute-done.1.right_ref
  27.2 1.1 slice.9
  28.3 2.3 %collective-permute-start.3 = (bf16[512,512]{1,0:T(8,128)(2,1)S(1)}, bf16[512,512]{1,0:T(8,128)(2,1)}, u32[]{:S(2)}, u32[]{:S(2)}) collective-permute-start(bf16[512,512]{1,0:T(8,128)(2,1)S(1)} %slice.9), channel_id=1, source_target_pairs={{0,3},{1,0},{2,1},{3,2},{4,7},{5,4},{6,5},{7,6},{8,11},{9,8},{10,9... | collective-permute-start | bytes 1572872 | tf_op jit(solution)/shard_map/ppermute | solution.py:501
  30.6 0.9 all-to-all-done.in_ref
  31.5 0.0 copy-start
  31.5 0.9 copy-done
  32.4 2.1 %prefix_scan.1 = (bf16[32,64,128]{2,1,0:T(8,128)(2,1)}, f32[2,4,1,512]{3,2,1,0:T(1,128)}) custom-call(s32[1]{0:T(128)} %bitcast.3.me_ref, bf16[32,96,128]{2,1,0:T(8,128)(2,1)} %copy-done, f32[4,1,512]{2,1,0:T(1,128)} %get-tuple-element.17.first_ref), custom_call_target="tpu_custom_call" | custom-call | tf_op jit(solution)/shard_map/prefix_scan/pallas_call | solution.py:145
  34.4 9.6 %all-to-all-start.1 = ((bf16[32,64,128]{2,1,0:T(8,128)(2,1)}), bf16[32,64,128]{2,1,0:T(8,128)(2,1)S(1)}, u32[]{:S(2)}, u32[]{:S(2)}) async-start(bf16[32,64,128]{2,1,0:T(8,128)(2,1)} %get-tuple-element.21), calls=%async_computation.1 | async-start | bytes 1048576 | tf_op jit(solution)/shard_map/all_to_all | solution.py:517
  44.1 0.0 copy-done.1
  44.1 1.0 copy.9
  45.1 0.0 copy-done.3
  45.1 9.3 %forward.1 = (bf16[2,4,1024,512]{3,2,1,0:T(8,128)(2,1)}, bf16[2,4,128,512]{3,2,1,0:T(8,128)(2,1)}) custom-call(s32[4,1024]{1,0:T(4,128)} %bitcast.7, bf16[1024,512]{1,0:T(8,128)(2,1)} %query_ref.3, bf16[4,512,128]{2,1,0:T(8,128)(2,1)} %book_ref.1, bf16[4,128,512]{2,1,0:T(8,128)(2,1)} %bitcast.4, f32[2,4,1,512]{3,2,1,0:T(1,128)} %get-tuple-element.18.count_ref), custom_call_target="tpu_custom_call" | custom-call | tf_op jit(solution)/shard_map/forward/pallas_call | solution.py:261
  54.4 1.2 all-to-all-done.1.prefix_ref
  55.6 0.0 copy-start.2
  55.6 0.0 collective-permute-done.2.far0_ref
  55.6 0.0 collective-permute-done.3.far1_ref
  55.6 0.8 copy-done.2
  56.4 20.7 %backward.1 = (bf16[1024,512]{1,0:T(8,128)(2,1)}, f32[1024,512]{1,0:T(8,128)}, f32[4,512,128]{2,1,0:T(8,128)}, bf16[32,128,128]{2,1,0:T(8,128)(2,1)}) custom-call(s32[1]{0:T(128)} %bitcast._, bf16[1024,512]{1,0:T(8,128)(2,1)} %own_ref.1, bf16[1024,512]{1,0:T(8,128)(2,1)} %copy-done.3, bf16[1024,512]{1,0:T(8,128)(2,1)} %collective-permute-done.1.right_ref, ...), custom_call_target="tpu_custom_call" | custom-call | flops 21474836480 | bytes 25165824 | tf_op jit(solution)/shard_map/backward/pallas_call | solution.py:434
  77.1 23.5 %all_to_all.20.in_ref = bf16[32,128,128]{2,1,0:T(8,128)(2,1)} all-to-all(bf16[32,128,128]{2,1,0:T(8,128)(2,1)} %get-tuple-element.25), channel_id=1, replica_groups=mesh['seq'=32,'head'=4] {'seq'}, dimensions={0} | all-to-all | bytes 2097152 | tf_op jit(solution)/shard_map/all_to_all | solution.py:523
  100.6 2.4 %suffix_scan.1 = bf16[32,128,128]{2,1,0:T(8,128)(2,1)} custom-call(bf16[32,128,128]{2,1,0:T(8,128)(2,1)} %all_to_all.20.in_ref), custom_call_target="tpu_custom_call" | custom-call | bytes 2097152 | tf_op jit(solution)/shard_map/suffix_scan/pallas_call | solution.py:170
  103.0 22.0 %all_to_all.21.later_ref = bf16[32,128,128]{2,1,0:T(8,128)(2,1)} all-to-all(bf16[32,128,128]{2,1,0:T(8,128)(2,1)} %suffix_scan.1), channel_id=1, replica_groups=mesh['seq'=32,'head'=4] {'seq'}, dimensions={0} | all-to-all | bytes 2097152 | tf_op jit(solution)/shard_map/all_to_all | solution.py:523
  124.9 4.9 %finish_values.1 = (bf16[1024,512]{1,0:T(8,128)(2,1)}, f32[4,512,128]{2,1,0:T(8,128)}) custom-call(s32[4,1024]{1,0:T(4,128)} %bitcast.9, f32[1024,512]{1,0:T(8,128)} %get-tuple-element.24.local_ref, bf16[32,128,128]{2,1,0:T(8,128)(2,1)} %all_to_all.21.later_ref, f32[4,512,128]{2,1,0:T(8,128)} %get-tuple-element.26.part_ref), custom_call_target="tpu_custom_call" | custom-call | flops 1073741824 | bytes 8388608 | tf_op jit(solution)/shard_map/finish_values/pallas_call | solution.py:481
  (1 shorter events, 0.0 us)
Async XLA Ops:
  0.6 26.0 %collective-permute-start = (bf16[1024,512]{1,0:T(8,128)(2,1)}, bf16[1024,512]{1,0:T(8,128)(2,1)S(1)}, u32[]{:S(2)}, u32[]{:S(2)}) collective-permute-start(bf16[1024,512]{1,0:T(8,128)(2,1)} %own_ref.1), channel_id=1, source_target_pairs={{0,1},{1,2},{2,3},{3,0},{4,5},{5,6},{6,7},{7,4},{8,9},{9,10},{10,1... | collective-permute-start | bytes 3145736 | tf_op jit(solution)/shard_map/ppermute | solution.py:498
  2.7 24.5 %collective-permute-start.1 = (bf16[1024,512]{1,0:T(8,128)(2,1)}, bf16[1024,512]{1,0:T(8,128)(2,1)}, u32[]{:S(2)}, u32[]{:S(2)}) collective-permute-start(bf16[1024,512]{1,0:T(8,128)(2,1)} %own_ref.1), channel_id=1, source_target_pairs={{0,3},{1,0},{2,1},{3,2},{4,7},{5,4},{6,5},{7,6},{8,11},{9,8},{10,9... | collective-permute-start | bytes 3145736 | tf_op jit(solution)/shard_map/ppermute | solution.py:499
  7.8 23.7 %all-to-all-start = ((bf16[32,96,128]{2,1,0:T(8,128)(2,1)}), bf16[32,96,128]{2,1,0:T(8,128)(2,1)S(1)}, u32[]{:S(2)}, u32[]{:S(2)}) async-start(bf16[32,96,128]{2,1,0:T(8,128)(2,1)} %get-tuple-element.16), calls=%async_computation | async-start | bytes 1572864 | tf_op jit(solution)/shard_map/all_to_all | solution.py:516
  17.3 26.8 %copy-start.1 = (bf16[4,512,128]{2,1,0:T(8,128)(2,1)S(1)}, bf16[4,512,128]{2,1,0:T(8,128)(2,1)}, u32[]{:S(2)}) copy-start(bf16[4,512,128]{2,1,0:T(8,128)(2,1)} %book_ref.1) | copy-start | bytes 1572868
  26.7 18.5 %copy-start.3 = (bf16[1024,512]{1,0:T(8,128)(2,1)}, bf16[1024,512]{1,0:T(8,128)(2,1)S(1)}, u32[]{:S(2)}) copy-start(bf16[1024,512]{1,0:T(8,128)(2,1)S(1)} %collective-permute-done.left_ref) | copy-start | bytes 3145732
  26.7 28.9 %collective-permute-start.2 = (bf16[512,512]{1,0:T(8,128)(2,1)S(1)}, bf16[512,512]{1,0:T(8,128)(2,1)}, u32[]{:S(2)}, u32[]{:S(2)}) collective-permute-start(bf16[512,512]{1,0:T(8,128)(2,1)S(1)} %slice.8), channel_id=1, source_target_pairs={{0,1},{1,2},{2,3},{3,0},{4,5},{5,6},{6,7},{7,4},{8,9},{9,10},{10,1... | collective-permute-start | bytes 1572872 | tf_op jit(solution)/shard_map/ppermute | solution.py:501
  28.3 27.3 %collective-permute-start.3 = (bf16[512,512]{1,0:T(8,128)(2,1)S(1)}, bf16[512,512]{1,0:T(8,128)(2,1)}, u32[]{:S(2)}, u32[]{:S(2)}) collective-permute-start(bf16[512,512]{1,0:T(8,128)(2,1)S(1)} %slice.9), channel_id=1, source_target_pairs={{0,3},{1,0},{2,1},{3,2},{4,7},{5,4},{6,5},{7,6},{8,11},{9,8},{10,9... | collective-permute-start | bytes 1572872 | tf_op jit(solution)/shard_map/ppermute | solution.py:501
  31.5 0.9 copy-start
  34.4 21.2 %all-to-all-start.1 = ((bf16[32,64,128]{2,1,0:T(8,128)(2,1)}), bf16[32,64,128]{2,1,0:T(8,128)(2,1)S(1)}, u32[]{:S(2)}, u32[]{:S(2)}) async-start(bf16[32,64,128]{2,1,0:T(8,128)(2,1)} %get-tuple-element.21), calls=%async_computation.1 | async-start | bytes 1048576 | tf_op jit(solution)/shard_map/all_to_all | solution.py:517
  55.6 0.8 copy-start.2

commit v6 on v5

--- a/solution.py
+++ b/solution.py
@@ -6,6 +6,7 @@
 from jax import lax
 from jax.experimental import pallas as pl
 from jax.experimental.pallas import tpu as pltpu
+from jax.sharding import Mesh
 from jax.sharding import PartitionSpec as P
 
 BLOCK = 512
@@ -280,19 +281,20 @@
     )(codes, queries, book, book_t, counts)
 
 
-def backward_kernel(_, own_ref, left_ref, right_ref, far0_ref, far1_ref, own_w, left_w, right_w,
+def backward_kernel(me_ref, own_ref, left_ref, right_ref, far0_ref, far1_ref, own_w, left_w, right_w,
                     far_w, codes_ref, query_ref, value_ref, probs_ref, keys_ref, book_t_ref,
                     prefix_ref, count_ref, first_ref,
-                    grad_query_ref, local_ref, part_ref, send_ref,
+                    grad_query_ref, local_ref, part_ref, give_ref, keep_ref,
                     dout, hot, rows_v, counts, grads, score_grad, key_grad, wide_t):
     width, entries = book_t_ref.shape[1:]
     entry_tiles = entries // TILE
     parts = BLOCK // PART
     blocks = probs_ref.shape[0]
     scale = width ** -0.5
-    head = pl.program_id(0)
-
-    @pl.when(head == 0)
+    step = pl.program_id(0)
+    head = lax.rem(step + 2 - 2 * me_ref[1], 4)
+
+    @pl.when(step == 0)
     def _():
         count = own_ref.shape[0] // PART
         for n in range(count):
@@ -388,10 +390,20 @@
             key_grad[b, PART:, :] = last[middle:].astype(BF16)
             mine = first[:entries] + last[:entries] + dot(hot[b], key_grad[b])
             code = mine if b == 0 else code + mine
-    for k in range(entries // HALF):
-        rows = slice(k * HALF, (k + 1) * HALF)
-        send_ref[k, :HALF, :] = part[rows].astype(BF16)
-        send_ref[k, HALF:, :] = code[rows].astype(BF16)
+
+    def write(ref):
+        for k in range(entries // HALF):
+            rows = slice(k * HALF, (k + 1) * HALF)
+            ref[k, :HALF, :] = part[rows].astype(BF16)
+            ref[k, HALF:, :] = code[rows].astype(BF16)
+
+    @pl.when(step < 2)
+    def _():
+        write(give_ref)
+
+    @pl.when(step >= 2)
+    def _():
+        write(keep_ref)
 
 
 def backward(me, pieces, weight, codes, queries, values, probs, keys, book_t, prefix, counts,
@@ -402,9 +414,12 @@
     both = entries + BLOCK
     columns = weight.shape[1] // 4
     slices = entries // HALF
-    by_head = lambda h, *_: (h, 0, 0)
-    in_blocks = lambda h, *_: (0, h, 0, 0)
-    rows_of = pl.BlockSpec((tokens, width), lambda h, *_: (0, h))
+    at = lambda s, me: lax.rem(s + 2 - 2 * me[1], 4)
+    by_head = lambda s, me: (at(s, me), 0, 0)
+    in_blocks = lambda s, me: (0, at(s, me), 0, 0)
+    rows_of = pl.BlockSpec((tokens, width), lambda s, me: (0, at(s, me)))
+    shape = (slices, 2 * HALF, width)
+    both_heads = (2 * slices, 2 * HALF, width)
     per_head = pl.BlockSpec((1, entries, width), by_head)
 
     def chunk(offset):
@@ -429,7 +444,8 @@
         (queries.shape, BF16, rows_of),
         (queries.shape, F32, rows_of),
         ((heads, entries, width), F32, per_head),
-        ((heads * slices, 2 * HALF, width), BF16, pl.BlockSpec((slices, 2 * HALF, width), by_head)),
+        (both_heads, BF16, pl.BlockSpec(shape, lambda s, *_: (jnp.minimum(s, 1), 0, 0))),
+        (both_heads, BF16, pl.BlockSpec(shape, lambda s, *_: (jnp.maximum(s - 2, 0), 0, 0))),
     ]
     return call(
         backward_kernel, "backward", (heads,), in_specs, outs,
@@ -448,16 +464,25 @@
       first)
 
 
-def finish_kernel(codes_ref, local_ref, later_ref, part_ref, out_ref, book_ref):
+def finish_kernel(own, refs):
+    me_ref, codes_ref, local_ref, later_ref = refs[:4]
+    if own:
+        kept_ref, part_ref = refs[4:6]
+    else:
+        part_ref = refs[4]
+    out_ref, book_ref = refs[-2:]
     entries, width = part_ref.shape[1:]
-    head = pl.program_id(0)
+    step = pl.program_id(0)
+    head = 2 * me_ref[0] + step if own else 2 - 2 * me_ref[0] + step
     codes_row = row_at(codes_ref, head)
-    pieces = later_ref[...]
-    later = pieces[:, :HALF, :].reshape(entries, width)
-    book_ref[0] = pieces[:, HALF:, :].reshape(entries, width).astype(F32)
+    later = later_ref[:, :HALF, :].astype(F32)
+    if own:
+        later = later + jnp.where(me_ref[0] == 0, kept_ref[:, :HALF, :].astype(F32), 0.0)
+    later = later.reshape(entries, width)
+    book_ref[0] = later_ref[:, HALF:, :].reshape(entries, width).astype(F32)
     tokens = local_ref.shape[0]
-    tables = [later] * (tokens // BLOCK)
-    tables[0] = (later.astype(F32) + part_ref[0]).astype(BF16)
+    tables = [later.astype(BF16)] * (tokens // BLOCK)
+    tables[0] = (later + part_ref[0]).astype(BF16)
     levels = lax.broadcasted_iota(jnp.int32, (TILE, TILE), 1)
     for i in range(tokens // TILE):
         rows = slice(i * TILE, (i + 1) * TILE)
@@ -472,23 +497,27 @@
         out_ref[rows, :] = (local_ref[rows, :] + dot(hot, tables[i * TILE // BLOCK])).astype(BF16)
 
 
-def finish(codes, local, later, part):
+def finish(own, core, codes, local, later, part, extra):
     heads, entries, width = part.shape
     tokens = local.shape[0]
-    by_head = lambda h: (h, 0, 0)
-    rows_of = pl.BlockSpec((tokens, width), lambda h: (0, h))
+    at = lambda s, core: (2 * core[0] if own else 2 - 2 * core[0]) + s
+    by_head = lambda s, core: (at(s, core), 0, 0)
+    rows_of = pl.BlockSpec((tokens, width), lambda s, core: (0, at(s, core)))
+    pieces = pl.BlockSpec((entries // HALF, 2 * HALF, width), lambda s, *_: (s, 0, 0))
     per_head = pl.BlockSpec((1, entries, width), by_head)
+    in_specs = [pl.BlockSpec(codes.shape, lambda s, *_: (0, 0)), rows_of, pieces]
+    if own:
+        in_specs += [pieces, per_head]
+        args = (*extra, part)
+    else:
+        in_specs += [per_head] + [pl.BlockSpec(memory_space=pl.ANY)] * 2
+        args = (part, *extra)
     return call(
-        finish_kernel, "finish_values", (heads,),
-        [
-            pl.BlockSpec(codes.shape, lambda h: (0, 0)),
-            rows_of,
-            pl.BlockSpec((entries // HALF, 2 * HALF, width), by_head),
-            per_head,
-        ],
+        lambda *refs: finish_kernel(own, refs), "finish_own" if own else "finish_other", (2,),
+        in_specs,
         [(local.shape, BF16, rows_of), (part.shape, F32, per_head)],
-        flops=1 << 30, size=8 << 20,
-    )(codes, local, later, part)
+        aliases=None if own else {5: 0, 6: 1}, prefetch=1, flops=1 << 30, size=8 << 20,
+    )(core, codes, local, later, *args)
 
 
 def ring_pieces(array):
@@ -505,10 +534,15 @@
 def per_device(queries, values, codes, codebook, out_weight, grad_out):
     heads, entries, width = codebook.shape
     exchange = functools.partial(
-        lax.all_to_all, axis_name="seq", split_axis=0, concat_axis=0, tiled=True
+        lax.all_to_all, axis_name=("chip", "core"), split_axis=0, concat_axis=0, tiled=True
     )
-    me_seq = lax.axis_index("seq").astype(jnp.int32).reshape(1)
-    me_head = lax.axis_index("head").astype(jnp.int32).reshape(1)
+    between_chips = functools.partial(
+        lax.all_to_all, axis_name="chip", split_axis=0, concat_axis=0, tiled=True
+    )
+    other_core = functools.partial(lax.ppermute, axis_name="core", perm=[(0, 1), (1, 0)])
+    core = lax.axis_index("core").astype(jnp.int32)
+    me_seq = lax.axis_index(("chip", "core")).astype(jnp.int32).reshape(1)
+    me = jnp.stack([lax.axis_index("head").astype(jnp.int32), core])
     pieces = ring_pieces(grad_out)
     codes = codes.T
     book_t = jnp.swapaxes(codebook, 1, 2)
@@ -516,20 +550,27 @@
     prefix, counts = prefix_scan(me_seq, exchange(send), first_count)
     prefix = exchange(prefix)
     probs, keys = forward(codes, queries, codebook, book_t, counts)
-    grad_query, local, part, last = backward(
-        me_head, pieces, out_weight, codes, queries, values, probs, keys, book_t, prefix, counts,
-        first,
+    grad_query, local, part, give, keep = backward(
+        me, pieces, out_weight, codes, queries, values, probs, keys, book_t, prefix, counts, first
     )
-    later = exchange(suffix_scan(exchange(last)))
-    grad_values, grad_book = finish(codes, local, later, part)
+    got = other_core(give)
+    chip = (keep.astype(F32) + got.astype(F32)).astype(BF16)
+    later = between_chips(suffix_scan(between_chips(chip)))
+    is_value = lax.broadcasted_iota(jnp.int32, later.shape, 1) < HALF
+    mine = jnp.where(is_value & (core == 1), keep.astype(F32), 0.0)
+    theirs = other_core((later.astype(F32) + mine).astype(BF16))
+    core = core.reshape(1)
+    results = finish(True, core, codes, local, later, part, (got,))
+    grad_values, grad_book = finish(False, core, codes, local, theirs, part, results)
     return grad_query, grad_values, grad_book
 
 
 def solution(mesh):
-    rows = P("seq", "head")
+    finer = Mesh(mesh.devices.reshape(-1, 2, mesh.shape["head"]), ("chip", "core", "head"))
+    rows = P(("chip", "core"), "head")
     return jax.shard_map(
         per_device,
-        mesh=mesh,
+        mesh=finer,
         in_specs=(rows, rows, rows, P("head", None, None), P("head", None), rows),
         out_specs=(rows, rows, P("head", None, None)),
         check_vma=False,

time: 131 us -> 125 us (0.954)
  blocking collectives: 45.5 us -> 16.8 us
  waiting for transfers between devices: 11.5 us -> 22.4 us
  starting transfers between devices: 25.3 us -> 32 us
  other arithmetic: 0 us -> 2.32 us
  Pallas kernels: 43.1 us -> 45.3 us
    all_to_all x2 -> x1, blocking collectives: 45.5 us -> 16.8 us  [per_device(): later = between_chips(suffix_scan(between_chips(chip)))]
    all_to_all x0 -> x1, waiting for transfers between devices: none -> 9.96 us  [per_device(): later = between_chips(suffix_scan(between_chips(chip)))]
    all_to_all x0 -> x1, starting transfers between devices: none -> 3.57 us  [per_device(): later = between_chips(suffix_scan(between_chips(chip)))]
    ppermute x0 -> x2, starting transfers between devices: none -> 3.12 us  [the longest x1 2.6 us: per_device(): theirs = other_core((later.astype(F32) + mine).astype(BF16))]
    ppermute x0 -> x2, waiting for transfers between devices: none -> 1.75 us  [the longest x1 1.75 us: per_device(): got = other_core(give)]
    convert_element_type x0 -> x2, other arithmetic: none -> 1.65 us  [the longest x1 1.4 us: per_device(): chip = (keep.astype(F32) + got.astype(F32)).astype(BF16)]
    pallas_call x1, Pallas kernels: 20.7 us -> 22.2 us  [backward(): call(backward_kernel, 'backward', (heads,), in_specs, outs, [pltpu.VMEM((...]
    pallas_call x1 -> x2, Pallas kernels: 4.93 us -> 6.07 us  [finish(): call(lambda *refs: finish_kernel(own, refs), 'finish_own' if own else 'fi...]
  transfers between devices with their start and end apart: 6 -> 9, of which waited for: 3 -> 5; matrix products, arithmetic and copies ran while one was open for 2% -> 2% of each run, Pallas kernels for 12% -> 15%
where the time goes in v6:
time: 125 us; the launch traced here: 124 us
  Pallas kernels  45.3 us (36%)
  starting transfers between devices  32 us (26%)
  waiting for transfers between devices  22.4 us (18%)
  blocking collectives  16.8 us (13%)
  local copies, waits for them, and re-layouts  4.63 us (4%)
  other arithmetic  2.32 us (2%)
    pallas_call x1, Pallas kernels, backward(): call(backward_kernel, 'backward', (heads,), in_specs, outs, [pltpu.VMEM((...  22.2 us
    all_to_all x1, blocking collectives, per_device(): later = between_chips(suffix_scan(between_chips(chip)))  16.8 us
    all_to_all x1, waiting for transfers between devices, per_device(): later = between_chips(suffix_scan(between_chips(chip)))  9.96 us
    all_to_all x1, starting transfers between devices, per_device(): prefix = exchange(prefix)  9.62 us
    all_to_all x1, starting transfers between devices, per_device(): prefix, counts = prefix_scan(me_seq, exchange(send), first_count)  9.45 us
    pallas_call x1, Pallas kernels, forward(): call(forward_kernel, 'forward', (heads,), [pl.BlockSpec(codes.shape, lamb...  9.4 us
    ppermute x1, waiting for transfers between devices, ring_pieces(): left = lax.ppermute(array, 'head', up)  9.37 us
    pallas_call x2, Pallas kernels, finish(): call(lambda *refs: finish_kernel(own, refs), 'finish_own' if own else 'fi...  6.07 us
  transfers between devices with their start and end apart: 9, of which 5 were waited for; matrix products, arithmetic and copies ran while one was open for 2% of the time, Pallas kernels for 15%

profile of v6, /device:TPU:1, one launch (start us, length us, event | category | flops | bytes accessed | tf_op | source)
XLA Modules:
  0.0 124.3 jit_solution(3918023955659721300)
XLA Ops:
  0.6 2.1 %collective-permute-start = (bf16[1024,512]{1,0:T(8,128)(2,1)}, bf16[1024,512]{1,0:T(8,128)(2,1)S(1)}, u32[]{:S(2)}, u32[]{:S(2)}) collective-permute-start(bf16[1024,512]{1,0:T(8,128)(2,1)} %own_ref.1), channel_id=1, source_target_pairs={{0,1},{1,2},{2,3},{3,0},{4,5},{5,6},{6,7},{7,4},{8,9},{9,10},{10,1... | collective-permute-start | bytes 3145736 | tf_op jit(solution)/shard_map/ppermute | solution.py:527
  2.7 1.4 %collective-permute-start.1 = (bf16[1024,512]{1,0:T(8,128)(2,1)}, bf16[1024,512]{1,0:T(8,128)(2,1)}, u32[]{:S(2)}, u32[]{:S(2)}) collective-permute-start(bf16[1024,512]{1,0:T(8,128)(2,1)} %own_ref.1), channel_id=1, source_target_pairs={{0,3},{1,0},{2,1},{3,2},{4,7},{5,4},{6,5},{7,6},{8,11},{9,8},{10,9... | collective-permute-start | bytes 3145736 | tf_op jit(solution)/shard_map/ppermute | solution.py:528
  4.1 3.7 %own_sums.1 = (bf16[32,96,128]{2,1,0:T(8,128)(2,1)}, f32[4,512,128]{2,1,0:T(8,128)}, f32[4,1,512]{2,1,0:T(1,128)}) custom-call(s32[4,1024]{1,0:T(4,128)} %bitcast.7, bf16[1024,512]{1,0:T(8,128)(2,1)} %value_ref.3), custom_call_target="tpu_custom_call" | custom-call | tf_op jit(solution)/shard_map/own_sums/pallas_call | solution.py:106
  7.8 9.4 %all-to-all-start = ((bf16[32,96,128]{2,1,0:T(8,128)(2,1)}), bf16[32,96,128]{2,1,0:T(8,128)(2,1)S(1)}, u32[]{:S(2)}, u32[]{:S(2)}) async-start(bf16[32,96,128]{2,1,0:T(8,128)(2,1)} %get-tuple-element.19), calls=%async_computation | async-start | bytes 1572864 | tf_op jit(solution)/shard_map/all_to_all | solution.py:550
  17.3 0.0 copy-start.4
  17.3 9.4 %collective-permute-done.left_ref = bf16[1024,512]{1,0:T(8,128)(2,1)S(1)} collective-permute-done((bf16[1024,512]{1,0:T(8,128)(2,1)}, bf16[1024,512]{1,0:T(8,128)(2,1)S(1)}, u32[]{:S(2)}, u32[]{:S(2)}) %collective-permute-start) | collective-permute-done | bytes 1048608 | tf_op jit(solution)/shard_map/ppermute | solution.py:527
  26.7 0.0 copy-start.7
  26.7 0.5 collective-permute-start.2
  27.2 0.0 collective-permute-done.1.right_ref
  27.2 1.1 slice.9
  28.3 2.3 %collective-permute-start.3 = (bf16[512,512]{1,0:T(8,128)(2,1)S(1)}, bf16[512,512]{1,0:T(8,128)(2,1)}, u32[]{:S(2)}, u32[]{:S(2)}) collective-permute-start(bf16[512,512]{1,0:T(8,128)(2,1)S(1)} %slice.9), channel_id=1, source_target_pairs={{0,3},{1,0},{2,1},{3,2},{4,7},{5,4},{6,5},{7,6},{8,11},{9,8},{10,9... | collective-permute-start | bytes 1572872 | tf_op jit(solution)/shard_map/ppermute | solution.py:530
  30.6 0.9 all-to-all-done.in_ref
  31.5 0.0 copy-start.1
  31.5 0.9 copy-done.1
  32.4 2.0 %prefix_scan.1 = (bf16[32,64,128]{2,1,0:T(8,128)(2,1)}, f32[2,4,1,512]{3,2,1,0:T(1,128)}) custom-call(s32[1]{0:T(128)} %bitcast.4.me_ref, bf16[32,96,128]{2,1,0:T(8,128)(2,1)} %copy-done.1, f32[4,1,512]{2,1,0:T(1,128)} %get-tuple-element.20.first_ref), custom_call_target="tpu_custom_call" | custom-call | tf_op jit(solution)/shard_map/prefix_scan/pallas_call | solution.py:146
  34.4 9.6 %all-to-all-start.1 = ((bf16[32,64,128]{2,1,0:T(8,128)(2,1)}), bf16[32,64,128]{2,1,0:T(8,128)(2,1)S(1)}, u32[]{:S(2)}, u32[]{:S(2)}) async-start(bf16[32,64,128]{2,1,0:T(8,128)(2,1)} %get-tuple-element.24), calls=%async_computation.1 | async-start | bytes 1048576 | tf_op jit(solution)/shard_map/all_to_all | solution.py:551
  44.0 0.0 copy-done.4
  44.1 1.0 copy.11
  45.1 0.0 copy-done.7
  45.1 0.7 pad_add_fusion.me_ref
  45.8 9.4 %forward.1 = (bf16[2,4,1024,512]{3,2,1,0:T(8,128)(2,1)}, bf16[2,4,128,512]{3,2,1,0:T(8,128)(2,1)}) custom-call(s32[4,1024]{1,0:T(4,128)} %bitcast.8, bf16[1024,512]{1,0:T(8,128)(2,1)} %query_ref.3, bf16[4,512,128]{2,1,0:T(8,128)(2,1)} %book_ref.1, bf16[4,128,512]{2,1,0:T(8,128)(2,1)} %bitcast.5, f32[2,4,1,512]{3,2,1,0:T(1,128)} %get-tuple-element.21.count_ref), custom_call_target="tpu_custom_call" | custom-call | tf_op jit(solution)/shard_map/forward/pallas_call | solution.py:262
  55.2 0.4 all-to-all-done.1.prefix_ref
  55.6 0.0 copy-start.6
  55.6 0.0 collective-permute-done.2.far0_ref
  55.6 0.0 collective-permute-done.3.far1_ref
  55.6 0.8 copy-done.6
  56.4 22.2 %backward.1 = (bf16[1024,512]{1,0:T(8,128)(2,1)}, f32[1024,512]{1,0:T(8,128)}, f32[4,512,128]{2,1,0:T(8,128)}, bf16[16,128,128]{2,1,0:T(8,128)(2,1)}, bf16[16,128,128]{2,1,0:T(8,128)(2,1)}) custom-call(s32[2]{0:T(128)} %pad_add_fusion.me_ref, bf16[1024,512]{1,0:T(8,128)(2,1)} %own_ref.1, bf16[1024,512]{1,0:T(8,128)(2,1)} %copy-done.7, ...), custom_call_target="tpu_custom_call" | custom-call | flops 21474836480 | bytes 25165824 | tf_op jit(solution)/shard_map/backward/pallas_call | solution.py:450
  78.6 0.5 collective-permute-start.4
  79.1 1.7 %collective-permute-done.4.refs_4_ = bf16[16,128,128]{2,1,0:T(8,128)(2,1)S(1)} collective-permute-done((bf16[16,128,128]{2,1,0:T(8,128)(2,1)}, bf16[16,128,128]{2,1,0:T(8,128)(2,1)S(1)}, u32[]{:S(2)}, u32[]{:S(2)}) %collective-permute-start.4) | collective-permute-done | bytes 524320 | tf_op jit(solution)/shard_map/ppermute | solution.py:556
  80.9 0.0 copy-start.2
  80.9 0.0 copy-start.3
  80.9 1.4 %fusion = bf16[16,128,128]{2,1,0:T(8,128)(2,1)S(1)} fusion(bf16[16,128,128]{2,1,0:T(8,128)(2,1)} %get-tuple-element.28, bf16[16,128,128]{2,1,0:T(8,128)(2,1)S(1)} %collective-permute-done.4.refs_4_), kind=kLoop, calls=%fused_computation.2 | loop fusion | flops 1048576 | bytes 1572864 | tf_op jit(solution)/shard_map/convert_element_type | solution.py:557
  82.3 16.8 %all_to_all.20.in_ref = bf16[16,128,128]{2,1,0:T(8,128)(2,1)} all-to-all(bf16[16,128,128]{2,1,0:T(8,128)(2,1)S(1)} %fusion), channel_id=1, replica_groups=mesh['chip'=16,'core'=2,'head'=4] {'chip'}, dimensions={0} | all-to-all | bytes 1048576 | tf_op jit(solution)/shard_map/all_to_all | solution.py:558
  99.1 1.9 %suffix_scan.1 = bf16[16,128,128]{2,1,0:T(8,128)(2,1)} custom-call(bf16[16,128,128]{2,1,0:T(8,128)(2,1)} %all_to_all.20.in_ref), custom_call_target="tpu_custom_call" | custom-call | bytes 2097152 | tf_op jit(solution)/shard_map/suffix_scan/pallas_call | solution.py:171
  101.0 0.0 copy-done.2
  101.0 3.6 %all-to-all-start.3 = ((bf16[16,128,128]{2,1,0:T(8,128)(2,1)}), bf16[16,128,128]{2,1,0:T(8,128)(2,1)S(1)}, u32[]{:S(2)}, u32[]{:S(2)}) async-start(bf16[16,128,128]{2,1,0:T(8,128)(2,1)} %suffix_scan.1), calls=%async_computation.3 | async-start | bytes 1048576 | tf_op jit(solution)/shard_map/all_to_all | solution.py:558
  104.6 10.0 %all-to-all-done.3.refs_3_ = bf16[16,128,128]{2,1,0:T(8,128)(2,1)S(1)} async-done(((bf16[16,128,128]{2,1,0:T(8,128)(2,1)}), bf16[16,128,128]{2,1,0:T(8,128)(2,1)S(1)}, u32[]{:S(2)}, u32[]{:S(2)}) %all-to-all-start.3) | async-done | bytes 524320 | tf_op jit(solution)/shard_map/all_to_all | solution.py:558
  114.6 0.0 copy-done.3
  114.6 0.0 copy-start
  114.6 0.2 fusion.2
  114.8 2.6 %collective-permute-start.5 = (bf16[16,128,128]{2,1,0:T(8,128)(2,1)S(1)}, bf16[16,128,128]{2,1,0:T(8,128)(2,1)S(1)}, u32[]{:S(2)}, u32[]{:S(2)}) collective-permute-start(bf16[16,128,128]{2,1,0:T(8,128)(2,1)S(1)} %fusion.2), channel_id=1, source_target_pairs={{0,4},{4,0},{1,5},{5,1},{2,6},{6,2},{3,7},{7,3},{8,12},{12,8},{9,1... | collective-permute-start | bytes 1572872 | tf_op jit(solution)/shard_map/ppermute | solution.py:561
  117.4 0.0 copy-done
  117.4 3.1 %finish_own.1 = (bf16[1024,512]{1,0:T(8,128)(2,1)}, f32[4,512,128]{2,1,0:T(8,128)}) custom-call(s32[1]{0:T(128)} %bitcast.1.refs_0_, s32[4,1024]{1,0:T(4,128)} %bitcast.10, f32[1024,512]{1,0:T(8,128)} %get-tuple-element.27.refs_2_, bf16[16,128,128]{2,1,0:T(8,128)(2,1)} %copy-done, bf16[16,128,128]{2,1,0:T(8,128)(2,1)} %copy-done.2, ...), custom_call_target="tpu_custom_call" | custom-call | flops 1073741824 | bytes 8388608 | tf_op jit(solution)/shard_map/finish_own/pallas_call | solution.py:515
  120.5 0.0 collective-permute-done.5.refs_3_
  120.5 0.0 copy-start.5
  120.5 0.8 copy-done.5
  121.3 3.0 %finish_other.1 = (bf16[1024,512]{1,0:T(8,128)(2,1)}, f32[4,512,128]{2,1,0:T(8,128)}) custom-call(s32[1]{0:T(128)} %bitcast.1.refs_0_, s32[4,1024]{1,0:T(4,128)} %bitcast.11, f32[1024,512]{1,0:T(8,128)} %get-tuple-element.27.refs_2_, bf16[16,128,128]{2,1,0:T(8,128)(2,1)} %copy-done.5, ...), custom_call_target="tpu_custom_call", output_to_operand_aliasing={{0}: (5, {}), {1}: (6, {})} | custom-call | flops 1073741824 | bytes 8388608 | tf_op jit(solution)/shard_map/finish_other/pallas_call | solution.py:515
  (2 shorter events, 0.0 us)
Async XLA Ops:
  0.6 26.0 %collective-permute-start = (bf16[1024,512]{1,0:T(8,128)(2,1)}, bf16[1024,512]{1,0:T(8,128)(2,1)S(1)}, u32[]{:S(2)}, u32[]{:S(2)}) collective-permute-start(bf16[1024,512]{1,0:T(8,128)(2,1)} %own_ref.1), channel_id=1, source_target_pairs={{0,1},{1,2},{2,3},{3,0},{4,5},{5,6},{6,7},{7,4},{8,9},{9,10},{10,1... | collective-permute-start | bytes 3145736 | tf_op jit(solution)/shard_map/ppermute | solution.py:527
  2.7 24.5 %collective-permute-start.1 = (bf16[1024,512]{1,0:T(8,128)(2,1)}, bf16[1024,512]{1,0:T(8,128)(2,1)}, u32[]{:S(2)}, u32[]{:S(2)}) collective-permute-start(bf16[1024,512]{1,0:T(8,128)(2,1)} %own_ref.1), channel_id=1, source_target_pairs={{0,3},{1,0},{2,1},{3,2},{4,7},{5,4},{6,5},{7,6},{8,11},{9,8},{10,9... | collective-permute-start | bytes 3145736 | tf_op jit(solution)/shard_map/ppermute | solution.py:528
  7.8 23.7 %all-to-all-start = ((bf16[32,96,128]{2,1,0:T(8,128)(2,1)}), bf16[32,96,128]{2,1,0:T(8,128)(2,1)S(1)}, u32[]{:S(2)}, u32[]{:S(2)}) async-start(bf16[32,96,128]{2,1,0:T(8,128)(2,1)} %get-tuple-element.19), calls=%async_computation | async-start | bytes 1572864 | tf_op jit(solution)/shard_map/all_to_all | solution.py:550
  17.3 26.8 %copy-start.4 = (bf16[4,512,128]{2,1,0:T(8,128)(2,1)S(1)}, bf16[4,512,128]{2,1,0:T(8,128)(2,1)}, u32[]{:S(2)}) copy-start(bf16[4,512,128]{2,1,0:T(8,128)(2,1)} %book_ref.1) | copy-start | bytes 1572868
  26.7 18.4 %copy-start.7 = (bf16[1024,512]{1,0:T(8,128)(2,1)}, bf16[1024,512]{1,0:T(8,128)(2,1)S(1)}, u32[]{:S(2)}) copy-start(bf16[1024,512]{1,0:T(8,128)(2,1)S(1)} %collective-permute-done.left_ref) | copy-start | bytes 3145732
  26.7 28.9 %collective-permute-start.2 = (bf16[512,512]{1,0:T(8,128)(2,1)S(1)}, bf16[512,512]{1,0:T(8,128)(2,1)}, u32[]{:S(2)}, u32[]{:S(2)}) collective-permute-start(bf16[512,512]{1,0:T(8,128)(2,1)S(1)} %slice.8), channel_id=1, source_target_pairs={{0,1},{1,2},{2,3},{3,0},{4,5},{5,6},{6,7},{7,4},{8,9},{9,10},{10,1... | collective-permute-start | bytes 1572872 | tf_op jit(solution)/shard_map/ppermute | solution.py:530
  28.3 27.3 %collective-permute-start.3 = (bf16[512,512]{1,0:T(8,128)(2,1)S(1)}, bf16[512,512]{1,0:T(8,128)(2,1)}, u32[]{:S(2)}, u32[]{:S(2)}) collective-permute-start(bf16[512,512]{1,0:T(8,128)(2,1)S(1)} %slice.9), channel_id=1, source_target_pairs={{0,3},{1,0},{2,1},{3,2},{4,7},{5,4},{6,5},{7,6},{8,11},{9,8},{10,9... | collective-permute-start | bytes 1572872 | tf_op jit(solution)/shard_map/ppermute | solution.py:530
  31.5 0.9 copy-start.1
  34.4 21.2 %all-to-all-start.1 = ((bf16[32,64,128]{2,1,0:T(8,128)(2,1)}), bf16[32,64,128]{2,1,0:T(8,128)(2,1)S(1)}, u32[]{:S(2)}, u32[]{:S(2)}) async-start(bf16[32,64,128]{2,1,0:T(8,128)(2,1)} %get-tuple-element.24), calls=%async_computation.1 | async-start | bytes 1048576 | tf_op jit(solution)/shard_map/all_to_all | solution.py:551
  55.6 0.8 copy-start.6
  78.6 2.3 %collective-permute-start.4 = (bf16[16,128,128]{2,1,0:T(8,128)(2,1)}, bf16[16,128,128]{2,1,0:T(8,128)(2,1)S(1)}, u32[]{:S(2)}, u32[]{:S(2)}) collective-permute-start(bf16[16,128,128]{2,1,0:T(8,128)(2,1)} %get-tuple-element.29), channel_id=1, source_target_pairs={{0,4},{4,0},{1,5},{5,1},{2,6},{6,2},{3,7},{7,3},{8,12},{12,8},{9,1... | collective-permute-start | bytes 1572872 | tf_op jit(solution)/shard_map/ppermute | solution.py:556
  80.9 20.2 %copy-start.2 = (bf16[16,128,128]{2,1,0:T(8,128)(2,1)}, bf16[16,128,128]{2,1,0:T(8,128)(2,1)S(1)}, u32[]{:S(2)}) copy-start(bf16[16,128,128]{2,1,0:T(8,128)(2,1)S(1)} %collective-permute-done.4.refs_4_) | copy-start | bytes 1572868
  80.9 33.7 %copy-start.3 = (bf16[16,128,128]{2,1,0:T(8,128)(2,1)S(1)}, bf16[16,128,128]{2,1,0:T(8,128)(2,1)}, u32[]{:S(2)}) copy-start(bf16[16,128,128]{2,1,0:T(8,128)(2,1)} %get-tuple-element.28) | copy-start | bytes 1572868
  101.0 13.6 %all-to-all-start.3 = ((bf16[16,128,128]{2,1,0:T(8,128)(2,1)}), bf16[16,128,128]{2,1,0:T(8,128)(2,1)S(1)}, u32[]{:S(2)}, u32[]{:S(2)}) async-start(bf16[16,128,128]{2,1,0:T(8,128)(2,1)} %suffix_scan.1), calls=%async_computation.3 | async-start | bytes 1048576 | tf_op jit(solution)/shard_map/all_to_all | solution.py:558
  114.6 2.9 %copy-start = (bf16[16,128,128]{2,1,0:T(8,128)(2,1)}, bf16[16,128,128]{2,1,0:T(8,128)(2,1)S(1)}, u32[]{:S(2)}) copy-start(bf16[16,128,128]{2,1,0:T(8,128)(2,1)S(1)} %all-to-all-done.3.refs_3_) | copy-start | bytes 1572868
  114.8 5.7 %collective-permute-start.5 = (bf16[16,128,128]{2,1,0:T(8,128)(2,1)S(1)}, bf16[16,128,128]{2,1,0:T(8,128)(2,1)S(1)}, u32[]{:S(2)}, u32[]{:S(2)}) collective-permute-start(bf16[16,128,128]{2,1,0:T(8,128)(2,1)S(1)} %fusion.2), channel_id=1, source_target_pairs={{0,4},{4,0},{1,5},{5,1},{2,6},{6,2},{3,7},{7,3},{8,12},{12,8},{9,1... | collective-permute-start | bytes 1572872 | tf_op jit(solution)/shard_map/ppermute | solution.py:561
  120.5 0.8 copy-start.5

commit v7 on v6

--- a/solution.py
+++ b/solution.py
@@ -16,7 +16,8 @@
 ROWS = 96
 F32 = jnp.float32
 BF16 = jnp.bfloat16
-VMEM_LIMIT = 60 << 20
+VMEM_LIMIT = 44 << 20
+IN_VMEM = pl.BlockSpec(memory_space=pltpu.VMEM)
 
 
 def dot(left, right):
@@ -29,7 +30,7 @@
 
 def call(kernel, name, grid, in_specs, outs, scratch=(), aliases=None, prefetch=0, flops=0, size=0,
          limit=VMEM_LIMIT):
-    return pl.pallas_call(
+    run = pl.pallas_call(
         kernel,
         grid_spec=pltpu.PrefetchScalarGridSpec(
             num_scalar_prefetch=prefetch,
@@ -38,7 +39,7 @@
             out_specs=[spec for _, _, spec in outs],
             scratch_shapes=list(scratch),
         ),
-        out_shape=[jax.ShapeDtypeStruct(shape, dtype) for shape, dtype, _ in outs],
+        out_shape=[pltpu.HBM(shape, dtype) for shape, dtype, _ in outs],
         input_output_aliases=aliases or {},
         compiler_params=pltpu.CompilerParams(
             dimension_semantics=("arbitrary",) * len(grid), vmem_limit_bytes=limit
@@ -46,6 +47,16 @@
         cost_estimate=pl.CostEstimate(flops=flops, bytes_accessed=size, transcendentals=0),
         name=name,
     )
+
+    def placed(array, spec):
+        space = pltpu.VMEM if spec.memory_space == pltpu.VMEM else pltpu.HBM
+        return pltpu.with_memory_space_constraint(array, space)
+
+    def with_places(*args):
+        arrays = [placed(a, spec) for a, spec in zip(args[prefetch:], in_specs)]
+        return run(*args[:prefetch], *arrays)
+
+    return with_places
 
 
 def onehot_rows(codes_row, entries):
@@ -145,7 +156,7 @@
     shape = (2, heads, 1, entries)
     return call(
         prefix_kernel, "prefix_scan", (1,),
-        [pl.BlockSpec(pieces.shape, whole), pl.BlockSpec(first.shape, whole)],
+        [IN_VMEM, pl.BlockSpec(first.shape, whole)],
         [
             ((count, HALF, TILE), BF16, pl.BlockSpec((count, HALF, TILE), whole)),
             (shape, F32, pl.BlockSpec(shape, lambda i, *_: (0, 0, 0, 0))),
@@ -169,7 +180,7 @@
 def suffix_scan(pieces):
     spec = pl.BlockSpec(pieces.shape, lambda i: (0, 0, 0))
     return call(
-        suffix_kernel, "suffix_scan", (1,), [spec], [(pieces.shape, BF16, spec)], size=2 << 20
+        suffix_kernel, "suffix_scan", (1,), [IN_VMEM], [(pieces.shape, BF16, spec)], size=2 << 20
     )(pieces)[0]
 
 
@@ -281,33 +292,34 @@
     )(codes, queries, book, book_t, counts)
 
 
-def backward_kernel(me_ref, own_ref, left_ref, right_ref, far0_ref, far1_ref, own_w, left_w, right_w,
-                    far_w, codes_ref, query_ref, value_ref, probs_ref, keys_ref, book_t_ref,
+def backward_kernel(me_ref, core_ref, own_hbm, left_ref, right_ref, far0_ref, far1_ref, weight_hbm,
+                    codes_ref, query_ref, value_ref, probs_ref, keys_ref, book_t_ref,
                     prefix_ref, count_ref, first_ref,
                     grad_query_ref, local_ref, part_ref, give_ref, keep_ref,
-                    dout, hot, rows_v, counts, grads, score_grad, key_grad, wide_t):
+                    dout, hot, rows_v, counts, grads, score_grad, key_grad, wide_t, own_ref,
+                    weight_ref, sems):
     width, entries = book_t_ref.shape[1:]
     entry_tiles = entries // TILE
     parts = BLOCK // PART
     blocks = probs_ref.shape[0]
     scale = width ** -0.5
     step = pl.program_id(0)
-    head = lax.rem(step + 2 - 2 * me_ref[1], 4)
+    head = lax.rem(step + 2 - 2 * core_ref[0], 4)
+
+    def chunk(offset):
+        columns = own_ref.shape[1]
+        at = lax.rem(me_ref[0] + offset, 4) * columns
+        return weight_ref[:, pl.ds(pl.multiple_of(at, columns), columns)]
+
+    moves = [
+        pltpu.make_async_copy(weight_hbm, weight_ref, sems.at[0]),
+        pltpu.make_async_copy(own_hbm, own_ref, sems.at[1]),
+    ]
 
     @pl.when(step == 0)
     def _():
-        count = own_ref.shape[0] // PART
-        for n in range(count):
-            span = slice(n * PART, (n + 1) * PART)
-            total = dot_nt(own_ref[span, :], own_w[...]) + dot_nt(left_ref[span, :], left_w[...])
-            total = total + dot_nt(right_ref[span, :], right_w[...])
-            if n < count // 2:
-                far = far0_ref[span, :]
-            else:
-                far = far1_ref[(n - count // 2) * PART : (n + 1 - count // 2) * PART, :]
-            total = total + dot_nt(far, far_w[...])
-            for h in range(dout.shape[0]):
-                dout[h, span, :] = total[:, h * width : (h + 1) * width].astype(BF16)
+        for move in moves:
+            move.start()
 
     codes_row = row_at(codes_ref, head)
 
@@ -315,7 +327,8 @@
         hot[b] = onehot_rows(codes_row[:, b * BLOCK : (b + 1) * BLOCK], entries)
         wide_t[b, :, :entries] = book_t_ref[0]
         wide_t[b, :, entries:] = keys_ref[b, 0]
-        sums = prefix_ref[...].reshape(entries, width)
+        slices = entries // HALF
+        sums = prefix_ref[pl.ds(head * slices, slices)].reshape(entries, width)
         if b > 0:
             sums = (sums.astype(F32) + first_ref[0]).astype(BF16)
         rows_v[b, :entries, :] = sums
@@ -366,6 +379,24 @@
     order = [(b, n) for b in range(blocks) for n in range(parts)]
     for b in range(blocks):
         prepare(b)
+
+    @pl.when(step == 0)
+    def _():
+        for move in moves:
+            move.wait()
+        count = own_ref.shape[0] // PART
+        for n in range(count):
+            span = slice(n * PART, (n + 1) * PART)
+            total = dot_nt(own_ref[span, :], chunk(0)) + dot_nt(left_ref[span, :], chunk(3))
+            total = total + dot_nt(right_ref[span, :], chunk(1))
+            if n < count // 2:
+                far = far0_ref[span, :]
+            else:
+                far = far1_ref[(n - count // 2) * PART : (n + 1 - count // 2) * PART, :]
+            total = total + dot_nt(far, chunk(2))
+            for h in range(dout.shape[0]):
+                dout[h, span, :] = total[:, h * width : (h + 1) * width].astype(BF16)
+
     multiply(*order[0])
     code = None
     part = None
@@ -406,29 +437,23 @@
         write(keep_ref)
 
 
-def backward(me, pieces, weight, codes, queries, values, probs, keys, book_t, prefix, counts,
+def backward(me, core, pieces, weight, codes, queries, values, probs, keys, book_t, prefix, counts,
              first):
     heads, width, entries = book_t.shape
     tokens = queries.shape[0]
     blocks = tokens // BLOCK
     both = entries + BLOCK
-    columns = weight.shape[1] // 4
     slices = entries // HALF
-    at = lambda s, me: lax.rem(s + 2 - 2 * me[1], 4)
-    by_head = lambda s, me: (at(s, me), 0, 0)
-    in_blocks = lambda s, me: (0, at(s, me), 0, 0)
-    rows_of = pl.BlockSpec((tokens, width), lambda s, me: (0, at(s, me)))
+    at = lambda s, core: lax.rem(s + 2 - 2 * core[0], 4)
+    by_head = lambda s, _, core: (at(s, core), 0, 0)
+    in_blocks = lambda s, _, core: (0, at(s, core), 0, 0)
+    rows_of = pl.BlockSpec((tokens, width), lambda s, _, core: (0, at(s, core)))
     shape = (slices, 2 * HALF, width)
     both_heads = (2 * slices, 2 * HALF, width)
     per_head = pl.BlockSpec((1, entries, width), by_head)
 
-    def chunk(offset):
-        return pl.BlockSpec(
-            (weight.shape[0], columns), lambda h, me: (0, lax.rem(me[0] + offset, 4))
-        )
-
-    in_specs = [pl.BlockSpec(piece.shape, lambda h, *_: (0, 0)) for piece in pieces]
-    in_specs += [chunk(0), chunk(3), chunk(1), chunk(2)]
+    anywhere = pl.BlockSpec(memory_space=pl.ANY)
+    in_specs = [anywhere] + [IN_VMEM] * (len(pieces) - 1) + [anywhere]
     in_specs += [
         pl.BlockSpec(codes.shape, lambda h, *_: (0, 0)),
         rows_of,
@@ -436,7 +461,7 @@
         pl.BlockSpec((blocks, 1, both, BLOCK), in_blocks),
         pl.BlockSpec((blocks, 1, width, BLOCK), in_blocks),
         pl.BlockSpec((1, width, entries), by_head),
-        pl.BlockSpec((slices, HALF, width), by_head),
+        IN_VMEM,
         pl.BlockSpec((blocks, 1, 1, entries), in_blocks),
         per_head,
     ]
@@ -458,9 +483,12 @@
             pltpu.VMEM((blocks, 2, both, PART), BF16),
             pltpu.VMEM((blocks, BLOCK, width), BF16),
             pltpu.VMEM((blocks, width, both), BF16),
+            pltpu.VMEM(pieces[0].shape, BF16),
+            pltpu.VMEM(weight.shape, BF16),
+            pltpu.SemaphoreType.DMA((2,)),
         ],
-        prefetch=1, flops=20 << 30, size=24 << 20,
-    )(me, *pieces, *[weight] * 4, codes, queries, values, probs, keys, book_t, prefix, counts,
+        prefetch=2, flops=20 << 30, size=24 << 20,
+    )(me, core, *pieces, weight, codes, queries, values, probs, keys, book_t, prefix, counts,
       first)
 
 
@@ -475,11 +503,12 @@
     step = pl.program_id(0)
     head = 2 * me_ref[0] + step if own else 2 - 2 * me_ref[0] + step
     codes_row = row_at(codes_ref, head)
-    later = later_ref[:, :HALF, :].astype(F32)
+    mine = pl.ds(step * (entries // HALF), entries // HALF)
+    later = later_ref[mine, :HALF, :].astype(F32)
     if own:
-        later = later + jnp.where(me_ref[0] == 0, kept_ref[:, :HALF, :].astype(F32), 0.0)
+        later = later + jnp.where(me_ref[0] == 0, kept_ref[mine, :HALF, :].astype(F32), 0.0)
     later = later.reshape(entries, width)
-    book_ref[0] = later_ref[:, HALF:, :].reshape(entries, width).astype(F32)
+    book_ref[0] = later_ref[mine, HALF:, :].reshape(entries, width).astype(F32)
     tokens = local_ref.shape[0]
     tables = [later.astype(BF16)] * (tokens // BLOCK)
     tables[0] = (later + part_ref[0]).astype(BF16)
@@ -503,11 +532,10 @@
     at = lambda s, core: (2 * core[0] if own else 2 - 2 * core[0]) + s
     by_head = lambda s, core: (at(s, core), 0, 0)
     rows_of = pl.BlockSpec((tokens, width), lambda s, core: (0, at(s, core)))
-    pieces = pl.BlockSpec((entries // HALF, 2 * HALF, width), lambda s, *_: (s, 0, 0))
     per_head = pl.BlockSpec((1, entries, width), by_head)
-    in_specs = [pl.BlockSpec(codes.shape, lambda s, *_: (0, 0)), rows_of, pieces]
+    in_specs = [pl.BlockSpec(codes.shape, lambda s, *_: (0, 0)), rows_of, IN_VMEM]
     if own:
-        in_specs += [pieces, per_head]
+        in_specs += [IN_VMEM, per_head]
         args = (*extra, part)
     else:
         in_specs += [per_head] + [pl.BlockSpec(memory_space=pl.ANY)] * 2
@@ -542,7 +570,8 @@
     other_core = functools.partial(lax.ppermute, axis_name="core", perm=[(0, 1), (1, 0)])
     core = lax.axis_index("core").astype(jnp.int32)
     me_seq = lax.axis_index(("chip", "core")).astype(jnp.int32).reshape(1)
-    me = jnp.stack([lax.axis_index("head").astype(jnp.int32), core])
+    me = lax.axis_index("head").astype(jnp.int32).reshape(1)
+    core_at = core.reshape(1)
     pieces = ring_pieces(grad_out)
     codes = codes.T
     book_t = jnp.swapaxes(codebook, 1, 2)
@@ -551,7 +580,7 @@
     prefix = exchange(prefix)
     probs, keys = forward(codes, queries, codebook, book_t, counts)
     grad_query, local, part, give, keep = backward(
-        me, pieces, out_weight, codes, queries, values, probs, keys, book_t, prefix, counts, first
+        me, core_at, pieces, out_weight, codes, queries, values, probs, keys, book_t, prefix, counts, first
     )
     got = other_core(give)
     chip = (keep.astype(F32) + got.astype(F32)).astype(BF16)
@@ -559,9 +588,8 @@
     is_value = lax.broadcasted_iota(jnp.int32, later.shape, 1) < HALF
     mine = jnp.where(is_value & (core == 1), keep.astype(F32), 0.0)
     theirs = other_core((later.astype(F32) + mine).astype(BF16))
-    core = core.reshape(1)
-    results = finish(True, core, codes, local, later, part, (got,))
-    grad_values, grad_book = finish(False, core, codes, local, theirs, part, results)
+    results = finish(True, core_at, codes, local, later, part, (got,))
+    grad_values, grad_book = finish(False, core_at, codes, local, theirs, part, results)
     return grad_query, grad_values, grad_book
 
 

time: 125 us -> 122 us (0.976)
    unnamed x17 -> x3, local copies, waits for them, and re-layouts: 3.52 us -> 2.06 us
  transfers between devices with their start and end apart: 9 -> 9, of which waited for: 5 -> 5; matrix products, arithmetic and copies ran while one was open for 2% -> 3% of each run, Pallas kernels for 15% -> 14%
where the time goes in v7:
time: 122 us
  Pallas kernels  44.7 us (37%)
  starting transfers between devices  32.4 us (27%)
  waiting for transfers between devices  21.8 us (18%)
  blocking collectives  17 us (14%)
  local copies, waits for them, and re-layouts  3.76 us (3%)
  other arithmetic  1.51 us (1%)
    pallas_call x7, Pallas kernels, with_places(): return run(*args[:prefetch], *arrays)  44.7 us
    all_to_all x1, blocking collectives, per_device(): later = between_chips(suffix_scan(between_chips(chip)))  17 us
    all_to_all x1, starting transfers between devices, per_device(): prefix = exchange(prefix)  10.1 us
    all_to_all x1, waiting for transfers between devices, per_device(): later = between_chips(suffix_scan(between_chips(chip)))  9.96 us
    all_to_all x1, starting transfers between devices, per_device(): prefix, counts = prefix_scan(me_seq, exchange(send), first_count)  9.45 us
    ppermute x1, waiting for transfers between devices, ring_pieces(): left = lax.ppermute(array, 'head', up)  9.38 us
    all_to_all x1, starting transfers between devices, per_device(): later = between_chips(suffix_scan(between_chips(chip)))  3.57 us
    ppermute x1, starting transfers between devices, per_device(): theirs = other_core((later.astype(F32) + mine).astype(BF16))  2.6 us
  transfers between devices with their start and end apart: 9, of which 5 were waited for; matrix products, arithmetic and copies ran while one was open for 3% of the time, Pallas kernels for 14%

profile of v7, /device:TPU:1, one launch (start us, length us, event | category | flops | bytes accessed | tf_op | source)
XLA Modules:
  0.0 121.8 jit_solution(16194956862270396914)
XLA Ops:
  0.6 2.1 %collective-permute-start = (bf16[1024,512]{1,0:T(8,128)(2,1)}, bf16[1024,512]{1,0:T(8,128)(2,1)S(1)}, u32[]{:S(2)}, u32[]{:S(2)}) collective-permute-start(bf16[1024,512]{1,0:T(8,128)(2,1)} %own_hbm.1), channel_id=1, source_target_pairs={{0,1},{1,2},{2,3},{3,0},{4,5},{5,6},{6,7},{7,4},{8,9},{9,10},{10,1... | collective-permute-start | bytes 3145736 | tf_op jit(solution)/shard_map/ppermute | solution.py:555
  2.7 1.4 %collective-permute-start.1 = (bf16[1024,512]{1,0:T(8,128)(2,1)}, bf16[1024,512]{1,0:T(8,128)(2,1)S(1)}, u32[]{:S(2)}, u32[]{:S(2)}) collective-permute-start(bf16[1024,512]{1,0:T(8,128)(2,1)} %own_hbm.1), channel_id=1, source_target_pairs={{0,3},{1,0},{2,1},{3,2},{4,7},{5,4},{6,5},{7,6},{8,11},{9,8},{10,9... | collective-permute-start | bytes 3145736 | tf_op jit(solution)/shard_map/ppermute | solution.py:556
  4.1 3.7 %own_sums.1 = (bf16[32,96,128]{2,1,0:T(8,128)(2,1)}, f32[4,512,128]{2,1,0:T(8,128)}, f32[4,1,512]{2,1,0:T(1,128)}) custom-call(s32[4,1024]{1,0:T(4,128)} %bitcast.7, bf16[1024,512]{1,0:T(8,128)(2,1)} %value_ref.3), custom_call_target="tpu_custom_call" | custom-call | tf_op jit(solution)/shard_map/own_sums/pallas_call | solution.py:57
  7.8 9.4 %all-to-all-start = ((bf16[32,96,128]{2,1,0:T(8,128)(2,1)}), bf16[32,96,128]{2,1,0:T(8,128)(2,1)S(1)}, u32[]{:S(2)}, u32[]{:S(2)}) async-start(bf16[32,96,128]{2,1,0:T(8,128)(2,1)} %get-tuple-element.19), calls=%async_computation | async-start | bytes 1572864 | tf_op jit(solution)/shard_map/all_to_all | solution.py:579
  17.3 9.4 %collective-permute-done.left_ref = bf16[1024,512]{1,0:T(8,128)(2,1)S(1)} collective-permute-done((bf16[1024,512]{1,0:T(8,128)(2,1)}, bf16[1024,512]{1,0:T(8,128)(2,1)S(1)}, u32[]{:S(2)}, u32[]{:S(2)}) %collective-permute-start) | collective-permute-done | bytes 1048608 | tf_op jit(solution)/shard_map/ppermute | solution.py:555
  26.7 0.8 slice.8
  27.5 0.3 collective-permute-start.2
  27.8 0.0 collective-permute-done.1.right_ref
  27.8 0.9 slice.9
  28.7 2.4 %collective-permute-start.3 = (bf16[512,512]{1,0:T(8,128)(2,1)}, bf16[512,512]{1,0:T(8,128)(2,1)}, u32[]{:S(2)}, u32[]{:S(2)}) collective-permute-start(bf16[512,512]{1,0:T(8,128)(2,1)} %slice.9), channel_id=1, source_target_pairs={{0,3},{1,0},{2,1},{3,2},{4,7},{5,4},{6,5},{7,6},{8,11},{9,8},{10,9... | collective-permute-start | bytes 1572872 | tf_op jit(solution)/shard_map/ppermute | solution.py:558
  31.0 0.5 all-to-all-done.in_ref
  31.5 1.6 %prefix_scan.1 = (bf16[32,64,128]{2,1,0:T(8,128)(2,1)}, f32[2,4,1,512]{3,2,1,0:T(1,128)}) custom-call(s32[1]{0:T(128)} %bitcast.4.me_ref, bf16[32,96,128]{2,1,0:T(8,128)(2,1)S(1)} %all-to-all-done.in_ref, f32[4,1,512]{2,1,0:T(1,128)} %get-tuple-element.20.first_ref), custom_call_target="tpu_custom_call" | custom-call | tf_op jit(solution)/shard_map/prefix_scan/pallas_call | solution.py:57
  33.1 10.1 %all-to-all-start.1 = ((bf16[32,64,128]{2,1,0:T(8,128)(2,1)}), bf16[32,64,128]{2,1,0:T(8,128)(2,1)S(1)}, u32[]{:S(2)}, u32[]{:S(2)}) async-start(bf16[32,64,128]{2,1,0:T(8,128)(2,1)} %get-tuple-element.24), calls=%async_computation.1 | async-start | bytes 1048576 | tf_op jit(solution)/shard_map/all_to_all | solution.py:580
  43.2 2.1 %copy.11 = bf16[4,512,128]{1,2,0:T(8,128)(2,1)} copy(bf16[4,512,128]{2,1,0:T(8,128)(2,1)} %book_ref.1) | data formatting | bytes 1048576 | tf_op args[3]
  45.3 9.2 %forward.1 = (bf16[2,4,1024,512]{3,2,1,0:T(8,128)(2,1)}, bf16[2,4,128,512]{3,2,1,0:T(8,128)(2,1)}) custom-call(s32[4,1024]{1,0:T(4,128)} %bitcast.8, bf16[1024,512]{1,0:T(8,128)(2,1)} %query_ref.3, bf16[4,512,128]{2,1,0:T(8,128)(2,1)} %book_ref.1, bf16[4,128,512]{2,1,0:T(8,128)(2,1)} %bitcast.5, f32[2,4,1,512]{3,2,1,0:T(1,128)} %get-tuple-element.21.count_ref), custom_call_target="tpu_custom_call" | custom-call | tf_op jit(solution)/shard_map/forward/pallas_call | solution.py:57
  54.5 0.2 all-to-all-done.1.prefix_ref
  54.8 0.0 collective-permute-done.2.far0_ref
  54.8 0.0 collective-permute-done.3.far1_ref
  54.8 23.4 %backward.1 = (bf16[1024,512]{1,0:T(8,128)(2,1)}, f32[1024,512]{1,0:T(8,128)}, f32[4,512,128]{2,1,0:T(8,128)}, bf16[16,128,128]{2,1,0:T(8,128)(2,1)}, bf16[16,128,128]{2,1,0:T(8,128)(2,1)}) custom-call(s32[1]{0:T(128)} %bitcast.me_ref, s32[1]{0:T(128)} %bitcast.1.core_ref.refs_0_, bf16[1024,512]{1,0:T(8,128)(2,1)} %own_hbm.1, ...), custom_call_target="tpu_custom_call" | custom-call | flops 21474836480 | bytes 25165824 | tf_op jit(solution)/shard_map/backward/pallas_call | solution.py:57
  78.1 0.5 collective-permute-start.4
  78.7 1.7 %collective-permute-done.4.refs_4_ = bf16[16,128,128]{2,1,0:T(8,128)(2,1)S(1)} collective-permute-done((bf16[16,128,128]{2,1,0:T(8,128)(2,1)}, bf16[16,128,128]{2,1,0:T(8,128)(2,1)S(1)}, u32[]{:S(2)}, u32[]{:S(2)}) %collective-permute-start.4) | collective-permute-done | bytes 524320 | tf_op jit(solution)/shard_map/ppermute | solution.py:585
  80.4 0.0 copy-start
  80.4 1.3 %fusion = bf16[16,128,128]{2,1,0:T(8,128)(2,1)S(1)} fusion(bf16[16,128,128]{2,1,0:T(8,128)(2,1)} %get-tuple-element.28, bf16[16,128,128]{2,1,0:T(8,128)(2,1)S(1)} %collective-permute-done.4.refs_4_), kind=kLoop, calls=%fused_computation.2 | loop fusion | flops 1048576 | bytes 1572864 | tf_op jit(solution)/shard_map/convert_element_type | solution.py:586
  81.7 17.0 %all_to_all.20.in_ref = bf16[16,128,128]{2,1,0:T(8,128)(2,1)S(1)} all-to-all(bf16[16,128,128]{2,1,0:T(8,128)(2,1)S(1)} %fusion), channel_id=1, replica_groups=mesh['chip'=16,'core'=2,'head'=4] {'chip'}, dimensions={0} | all-to-all | bytes 1048576 | tf_op jit(solution)/shard_map/all_to_all | solution.py:587
  98.6 0.9 suffix_scan.1
  99.5 3.6 %all-to-all-start.3 = ((bf16[16,128,128]{2,1,0:T(8,128)(2,1)}), bf16[16,128,128]{2,1,0:T(8,128)(2,1)S(1)}, u32[]{:S(2)}, u32[]{:S(2)}) async-start(bf16[16,128,128]{2,1,0:T(8,128)(2,1)} %suffix_scan.1), calls=%async_computation.3 | async-start | bytes 1048576 | tf_op jit(solution)/shard_map/all_to_all | solution.py:587
  103.1 10.0 %all-to-all-done.3.refs_3_ = bf16[16,128,128]{2,1,0:T(8,128)(2,1)S(1)} async-done(((bf16[16,128,128]{2,1,0:T(8,128)(2,1)}), bf16[16,128,128]{2,1,0:T(8,128)(2,1)S(1)}, u32[]{:S(2)}, u32[]{:S(2)}) %all-to-all-start.3) | async-done | bytes 524320 | tf_op jit(solution)/shard_map/all_to_all | solution.py:587
  113.1 0.0 copy-done
  113.1 0.2 fusion.2
  113.4 2.6 %collective-permute-start.5 = (bf16[16,128,128]{2,1,0:T(8,128)(2,1)S(1)}, bf16[16,128,128]{2,1,0:T(8,128)(2,1)S(1)}, u32[]{:S(2)}, u32[]{:S(2)}) collective-permute-start(bf16[16,128,128]{2,1,0:T(8,128)(2,1)S(1)} %fusion.2), channel_id=1, source_target_pairs={{0,4},{4,0},{1,5},{5,1},{2,6},{6,2},{3,7},{7,3},{8,12},{12,8},{9,1... | collective-permute-start | bytes 1572872 | tf_op jit(solution)/shard_map/ppermute | solution.py:590
  116.0 2.9 %finish_own.1 = (bf16[1024,512]{1,0:T(8,128)(2,1)}, f32[4,512,128]{2,1,0:T(8,128)}) custom-call(s32[1]{0:T(128)} %bitcast.1.core_ref.refs_0_, s32[4,1024]{1,0:T(4,128)} %bitcast.10, f32[1024,512]{1,0:T(8,128)} %get-tuple-element.27.refs_2_, bf16[16,128,128]{2,1,0:T(8,128)(2,1)S(1)} %all-to-all-done.3.refs_3_, ...), custom_call_target="tpu_custom_call" | custom-call | flops 1073741824 | bytes 8388608 | tf_op jit(solution)/shard_map/finish_own/pallas_call | solution.py:57
  118.8 0.0 collective-permute-done.5.refs_3_
  118.9 2.9 %finish_other.1 = (bf16[1024,512]{1,0:T(8,128)(2,1)}, f32[4,512,128]{2,1,0:T(8,128)}) custom-call(s32[1]{0:T(128)} %bitcast.1.core_ref.refs_0_, s32[4,1024]{1,0:T(4,128)} %bitcast.11, f32[1024,512]{1,0:T(8,128)} %get-tuple-element.27.refs_2_, bf16[16,128,128]{2,1,0:T(8,128)(2,1)S(1)} %collective-permute-done.5.refs_3_, ...), custom_call_target="tpu_custom_call", output_to_operand_aliasing={{0}: (5, {}), {1}: (6, {})} | custom-call | flops 1073741824 | bytes 8388608 | tf_op jit(solution)/shard_map/finish_other/pallas_call | solution.py:57
  (1 shorter events, 0.0 us)
Async XLA Ops:
  0.6 26.0 %collective-permute-start = (bf16[1024,512]{1,0:T(8,128)(2,1)}, bf16[1024,512]{1,0:T(8,128)(2,1)S(1)}, u32[]{:S(2)}, u32[]{:S(2)}) collective-permute-start(bf16[1024,512]{1,0:T(8,128)(2,1)} %own_hbm.1), channel_id=1, source_target_pairs={{0,1},{1,2},{2,3},{3,0},{4,5},{5,6},{6,7},{7,4},{8,9},{9,10},{10,1... | collective-permute-start | bytes 3145736 | tf_op jit(solution)/shard_map/ppermute | solution.py:555
  2.7 25.1 %collective-permute-start.1 = (bf16[1024,512]{1,0:T(8,128)(2,1)}, bf16[1024,512]{1,0:T(8,128)(2,1)S(1)}, u32[]{:S(2)}, u32[]{:S(2)}) collective-permute-start(bf16[1024,512]{1,0:T(8,128)(2,1)} %own_hbm.1), channel_id=1, source_target_pairs={{0,3},{1,0},{2,1},{3,2},{4,7},{5,4},{6,5},{7,6},{8,11},{9,8},{10,9... | collective-permute-start | bytes 3145736 | tf_op jit(solution)/shard_map/ppermute | solution.py:556
  7.8 23.7 %all-to-all-start = ((bf16[32,96,128]{2,1,0:T(8,128)(2,1)}), bf16[32,96,128]{2,1,0:T(8,128)(2,1)S(1)}, u32[]{:S(2)}, u32[]{:S(2)}) async-start(bf16[32,96,128]{2,1,0:T(8,128)(2,1)} %get-tuple-element.19), calls=%async_computation | async-start | bytes 1572864 | tf_op jit(solution)/shard_map/all_to_all | solution.py:579
  27.5 27.3 %collective-permute-start.2 = (bf16[512,512]{1,0:T(8,128)(2,1)}, bf16[512,512]{1,0:T(8,128)(2,1)S(1)}, u32[]{:S(2)}, u32[]{:S(2)}) collective-permute-start(bf16[512,512]{1,0:T(8,128)(2,1)} %slice.8), channel_id=1, source_target_pairs={{0,1},{1,2},{2,3},{3,0},{4,5},{5,6},{6,7},{7,4},{8,9},{9,10},{10,1... | collective-permute-start | bytes 1572872 | tf_op jit(solution)/shard_map/ppermute | solution.py:558
  28.7 26.1 %collective-permute-start.3 = (bf16[512,512]{1,0:T(8,128)(2,1)}, bf16[512,512]{1,0:T(8,128)(2,1)}, u32[]{:S(2)}, u32[]{:S(2)}) collective-permute-start(bf16[512,512]{1,0:T(8,128)(2,1)} %slice.9), channel_id=1, source_target_pairs={{0,3},{1,0},{2,1},{3,2},{4,7},{5,4},{6,5},{7,6},{8,11},{9,8},{10,9... | collective-permute-start | bytes 1572872 | tf_op jit(solution)/shard_map/ppermute | solution.py:558
  33.1 21.6 %all-to-all-start.1 = ((bf16[32,64,128]{2,1,0:T(8,128)(2,1)}), bf16[32,64,128]{2,1,0:T(8,128)(2,1)S(1)}, u32[]{:S(2)}, u32[]{:S(2)}) async-start(bf16[32,64,128]{2,1,0:T(8,128)(2,1)} %get-tuple-element.24), calls=%async_computation.1 | async-start | bytes 1048576 | tf_op jit(solution)/shard_map/all_to_all | solution.py:580
  78.1 2.3 %collective-permute-start.4 = (bf16[16,128,128]{2,1,0:T(8,128)(2,1)}, bf16[16,128,128]{2,1,0:T(8,128)(2,1)S(1)}, u32[]{:S(2)}, u32[]{:S(2)}) collective-permute-start(bf16[16,128,128]{2,1,0:T(8,128)(2,1)} %get-tuple-element.29), channel_id=1, source_target_pairs={{0,4},{4,0},{1,5},{5,1},{2,6},{6,2},{3,7},{7,3},{8,12},{12,8},{9,1... | collective-permute-start | bytes 1572872 | tf_op jit(solution)/shard_map/ppermute | solution.py:585
  80.4 32.7 %copy-start = (bf16[16,128,128]{2,1,0:T(8,128)(2,1)S(1)}, bf16[16,128,128]{2,1,0:T(8,128)(2,1)}, u32[]{:S(2)}) copy-start(bf16[16,128,128]{2,1,0:T(8,128)(2,1)} %get-tuple-element.28) | copy-start | bytes 1572868
  99.5 13.6 %all-to-all-start.3 = ((bf16[16,128,128]{2,1,0:T(8,128)(2,1)}), bf16[16,128,128]{2,1,0:T(8,128)(2,1)S(1)}, u32[]{:S(2)}, u32[]{:S(2)}) async-start(bf16[16,128,128]{2,1,0:T(8,128)(2,1)} %suffix_scan.1), calls=%async_computation.3 | async-start | bytes 1048576 | tf_op jit(solution)/shard_map/all_to_all | solution.py:587
  113.4 5.5 %collective-permute-start.5 = (bf16[16,128,128]{2,1,0:T(8,128)(2,1)S(1)}, bf16[16,128,128]{2,1,0:T(8,128)(2,1)S(1)}, u32[]{:S(2)}, u32[]{:S(2)}) collective-permute-start(bf16[16,128,128]{2,1,0:T(8,128)(2,1)S(1)} %fusion.2), channel_id=1, source_target_pairs={{0,4},{4,0},{1,5},{5,1},{2,6},{6,2},{3,7},{7,3},{8,12},{12,8},{9,1... | collective-permute-start | bytes 1572872 | tf_op jit(solution)/shard_map/ppermute | solution.py:590

commit v8 on v7

--- a/solution.py
+++ b/solution.py
@@ -192,8 +192,8 @@
     return jnp.concatenate(tiles, axis=0)
 
 
-def forward_kernel(codes_ref, query_ref, book_ref, book_t_ref, count_ref,
-                   low_ref, keys_ref, rows_k, counts, scores):
+def forward_kernel(codes_ref, query_ref, book_ref, count_ref,
+                   low_ref, keys_ref, book_t_ref, rows_k, counts, scores):
     entries, width = book_ref.shape[1:]
     head = pl.program_id(0)
     entry_tiles = entries // TILE
@@ -205,6 +205,7 @@
     blocks = low_ref.shape[0]
 
     codes_row = row_at(codes_ref, head)
+    book_t_ref[0] = book_ref[0].astype(F32).T.astype(BF16)
 
     def prepare(b):
         keys_t = dot(
@@ -263,7 +264,7 @@
         soften(*item)
 
 
-def forward(codes, queries, book, book_t, counts):
+def forward(codes, queries, book, counts):
     heads, entries, width = book.shape
     tokens = queries.shape[0]
     blocks = tokens // BLOCK
@@ -276,12 +277,12 @@
             pl.BlockSpec(codes.shape, lambda h: (0, 0)),
             pl.BlockSpec((tokens, width), lambda h: (0, h)),
             pl.BlockSpec((1, entries, width), by_head),
-            pl.BlockSpec((1, width, entries), by_head),
             pl.BlockSpec((blocks, 1, 1, entries), in_blocks),
         ],
         [
             ((blocks, heads, both, BLOCK), BF16, pl.BlockSpec((blocks, 1, both, BLOCK), in_blocks)),
             ((blocks, heads, width, BLOCK), BF16, pl.BlockSpec((blocks, 1, width, BLOCK), in_blocks)),
+            ((heads, width, entries), BF16, pl.BlockSpec((1, width, entries), by_head)),
         ],
         [
             pltpu.VMEM((blocks, both, width), BF16),
@@ -289,15 +290,14 @@
             pltpu.VMEM((blocks, 2, both, PART), F32),
         ],
 
-    )(codes, queries, book, book_t, counts)
-
-
-def backward_kernel(me_ref, core_ref, own_hbm, left_ref, right_ref, far0_ref, far1_ref, weight_hbm,
+    )(codes, queries, book, counts)
+
+
+def backward_kernel(me_ref, core_ref, own_ref, left_ref, right_ref, far0_ref, far1_ref, weight_ref,
                     codes_ref, query_ref, value_ref, probs_ref, keys_ref, book_t_ref,
                     prefix_ref, count_ref, first_ref,
                     grad_query_ref, local_ref, part_ref, give_ref, keep_ref,
-                    dout, hot, rows_v, counts, grads, score_grad, key_grad, wide_t, own_ref,
-                    weight_ref, sems):
+                    dout, hot, rows_v, counts, grads, score_grad, key_grad, wide_t):
     width, entries = book_t_ref.shape[1:]
     entry_tiles = entries // TILE
     parts = BLOCK // PART
@@ -310,16 +310,6 @@
         columns = own_ref.shape[1]
         at = lax.rem(me_ref[0] + offset, 4) * columns
         return weight_ref[:, pl.ds(pl.multiple_of(at, columns), columns)]
-
-    moves = [
-        pltpu.make_async_copy(weight_hbm, weight_ref, sems.at[0]),
-        pltpu.make_async_copy(own_hbm, own_ref, sems.at[1]),
-    ]
-
-    @pl.when(step == 0)
-    def _():
-        for move in moves:
-            move.start()
 
     codes_row = row_at(codes_ref, head)
 
@@ -382,8 +372,6 @@
 
     @pl.when(step == 0)
     def _():
-        for move in moves:
-            move.wait()
         count = own_ref.shape[0] // PART
         for n in range(count):
             span = slice(n * PART, (n + 1) * PART)
@@ -453,7 +441,9 @@
     per_head = pl.BlockSpec((1, entries, width), by_head)
 
     anywhere = pl.BlockSpec(memory_space=pl.ANY)
-    in_specs = [anywhere] + [IN_VMEM] * (len(pieces) - 1) + [anywhere]
+    whole = lambda s, *_: (0, 0)
+    in_specs = [pl.BlockSpec(pieces[0].shape, whole)] + [IN_VMEM] * (len(pieces) - 1)
+    in_specs.append(pl.BlockSpec(weight.shape, whole))
     in_specs += [
         pl.BlockSpec(codes.shape, lambda h, *_: (0, 0)),
         rows_of,
@@ -483,9 +473,6 @@
             pltpu.VMEM((blocks, 2, both, PART), BF16),
             pltpu.VMEM((blocks, BLOCK, width), BF16),
             pltpu.VMEM((blocks, width, both), BF16),
-            pltpu.VMEM(pieces[0].shape, BF16),
-            pltpu.VMEM(weight.shape, BF16),
-            pltpu.SemaphoreType.DMA((2,)),
         ],
         prefetch=2, flops=20 << 30, size=24 << 20,
     )(me, core, *pieces, weight, codes, queries, values, probs, keys, book_t, prefix, counts,
@@ -574,11 +561,10 @@
     core_at = core.reshape(1)
     pieces = ring_pieces(grad_out)
     codes = codes.T
-    book_t = jnp.swapaxes(codebook, 1, 2)
     send, first, first_count = own_sums(codes, values, heads, entries)
     prefix, counts = prefix_scan(me_seq, exchange(send), first_count)
     prefix = exchange(prefix)
-    probs, keys = forward(codes, queries, codebook, book_t, counts)
+    probs, keys, book_t = forward(codes, queries, codebook, counts)
     grad_query, local, part, give, keep = backward(
         me, core_at, pieces, out_weight, codes, queries, values, probs, keys, book_t, prefix, counts, first
     )

time: 122 us -> 120 us (0.984)
  local copies, waits for them, and re-layouts: 3.76 us -> 1.71 us
  blocking collectives: 17 us -> 15.5 us
  waiting for transfers between devices: 21.8 us -> 23.3 us
    unnamed x3 -> x2, local copies, waits for them, and re-layouts: 2.06 us -> 0.01 us
    all_to_all x1, blocking collectives: 17 us -> 15.5 us  [per_device(): later = between_chips(suffix_scan(between_chips(chip)))]
    all_to_all x1, waiting for transfers between devices: 0.24 us -> 1.73 us  [per_device(): prefix = exchange(prefix)]
  transfers between devices with their start and end apart: 9 -> 9, of which waited for: 5 -> 5; matrix products, arithmetic and copies ran while one was open for 3% -> 1% of each run, Pallas kernels for 14% -> 15%
where the time goes in v8:
time: 120 us; the launch traced here: 119 us
  Pallas kernels  44.5 us (37%)
  starting transfers between devices  32.4 us (27%)
  waiting for transfers between devices  23.3 us (19%)
  blocking collectives  15.5 us (13%)
  local copies, waits for them, and re-layouts  1.71 us (1%)
  other arithmetic  1.51 us (1%)
    pallas_call x7, Pallas kernels, with_places(): return run(*args[:prefetch], *arrays)  44.5 us
    all_to_all x1, blocking collectives, per_device(): later = between_chips(suffix_scan(between_chips(chip)))  15.5 us
    all_to_all x1, starting transfers between devices, per_device(): prefix = exchange(prefix)  10.1 us
    all_to_all x1, waiting for transfers between devices, per_device(): later = between_chips(suffix_scan(between_chips(chip)))  9.96 us
    all_to_all x1, starting transfers between devices, per_device(): prefix, counts = prefix_scan(me_seq, exchange(send), first_count)  9.45 us
    ppermute x1, waiting for transfers between devices, ring_pieces(): left = lax.ppermute(array, 'head', up)  9.38 us
    all_to_all x1, starting transfers between devices, per_device(): later = between_chips(suffix_scan(between_chips(chip)))  3.57 us
    ppermute x1, starting transfers between devices, per_device(): theirs = other_core((later.astype(F32) + mine).astype(BF16))  2.6 us
  transfers between devices with their start and end apart: 9, of which 5 were waited for; matrix products, arithmetic and copies ran while one was open for 1% of the time, Pallas kernels for 15%

profile of v8, /device:TPU:1, one launch (start us, length us, event | category | flops | bytes accessed | tf_op | source)
XLA Modules:
  0.0 119.5 jit_solution(2177560224407200151)
XLA Ops:
  0.6 2.1 %collective-permute-start = (bf16[1024,512]{1,0:T(8,128)(2,1)}, bf16[1024,512]{1,0:T(8,128)(2,1)S(1)}, u32[]{:S(2)}, u32[]{:S(2)}) collective-permute-start(bf16[1024,512]{1,0:T(8,128)(2,1)} %own_ref.1), channel_id=1, source_target_pairs={{0,1},{1,2},{2,3},{3,0},{4,5},{5,6},{6,7},{7,4},{8,9},{9,10},{10,1... | collective-permute-start | bytes 3145736 | tf_op jit(solution)/shard_map/ppermute | solution.py:542
  2.7 1.4 %collective-permute-start.1 = (bf16[1024,512]{1,0:T(8,128)(2,1)}, bf16[1024,512]{1,0:T(8,128)(2,1)S(1)}, u32[]{:S(2)}, u32[]{:S(2)}) collective-permute-start(bf16[1024,512]{1,0:T(8,128)(2,1)} %own_ref.1), channel_id=1, source_target_pairs={{0,3},{1,0},{2,1},{3,2},{4,7},{5,4},{6,5},{7,6},{8,11},{9,8},{10,9... | collective-permute-start | bytes 3145736 | tf_op jit(solution)/shard_map/ppermute | solution.py:543
  4.1 3.7 %own_sums.1 = (bf16[32,96,128]{2,1,0:T(8,128)(2,1)}, f32[4,512,128]{2,1,0:T(8,128)}, f32[4,1,512]{2,1,0:T(1,128)}) custom-call(s32[4,1024]{1,0:T(4,128)} %bitcast.4, bf16[1024,512]{1,0:T(8,128)(2,1)} %value_ref.3), custom_call_target="tpu_custom_call" | custom-call | tf_op jit(solution)/shard_map/own_sums/pallas_call | solution.py:57
  7.8 9.4 %all-to-all-start = ((bf16[32,96,128]{2,1,0:T(8,128)(2,1)}), bf16[32,96,128]{2,1,0:T(8,128)(2,1)S(1)}, u32[]{:S(2)}, u32[]{:S(2)}) async-start(bf16[32,96,128]{2,1,0:T(8,128)(2,1)} %get-tuple-element.20), calls=%async_computation | async-start | bytes 1572864 | tf_op jit(solution)/shard_map/all_to_all | solution.py:565
  17.3 9.4 %collective-permute-done.left_ref = bf16[1024,512]{1,0:T(8,128)(2,1)S(1)} collective-permute-done((bf16[1024,512]{1,0:T(8,128)(2,1)}, bf16[1024,512]{1,0:T(8,128)(2,1)S(1)}, u32[]{:S(2)}, u32[]{:S(2)}) %collective-permute-start) | collective-permute-done | bytes 1048608 | tf_op jit(solution)/shard_map/ppermute | solution.py:542
  26.7 0.8 slice.8
  27.5 0.3 collective-permute-start.2
  27.8 0.0 collective-permute-done.1.right_ref
  27.8 0.9 slice.9
  28.7 2.4 %collective-permute-start.3 = (bf16[512,512]{1,0:T(8,128)(2,1)}, bf16[512,512]{1,0:T(8,128)(2,1)}, u32[]{:S(2)}, u32[]{:S(2)}) collective-permute-start(bf16[512,512]{1,0:T(8,128)(2,1)} %slice.9), channel_id=1, source_target_pairs={{0,3},{1,0},{2,1},{3,2},{4,7},{5,4},{6,5},{7,6},{8,11},{9,8},{10,9... | collective-permute-start | bytes 1572872 | tf_op jit(solution)/shard_map/ppermute | solution.py:545
  31.0 0.5 all-to-all-done.in_ref
  31.5 1.6 %prefix_scan.1 = (bf16[32,64,128]{2,1,0:T(8,128)(2,1)}, f32[2,4,1,512]{3,2,1,0:T(1,128)}) custom-call(s32[1]{0:T(128)} %bitcast.3.me_ref, bf16[32,96,128]{2,1,0:T(8,128)(2,1)S(1)} %all-to-all-done.in_ref, f32[4,1,512]{2,1,0:T(1,128)} %get-tuple-element.21.first_ref), custom_call_target="tpu_custom_call" | custom-call | tf_op jit(solution)/shard_map/prefix_scan/pallas_call | solution.py:57
  33.1 10.1 %all-to-all-start.1 = ((bf16[32,64,128]{2,1,0:T(8,128)(2,1)}), bf16[32,64,128]{2,1,0:T(8,128)(2,1)S(1)}, u32[]{:S(2)}, u32[]{:S(2)}) async-start(bf16[32,64,128]{2,1,0:T(8,128)(2,1)} %get-tuple-element.26), calls=%async_computation.1 | async-start | bytes 1048576 | tf_op jit(solution)/shard_map/all_to_all | solution.py:566
  43.2 9.8 %forward.1 = (bf16[2,4,1024,512]{3,2,1,0:T(8,128)(2,1)}, bf16[2,4,128,512]{3,2,1,0:T(8,128)(2,1)}, bf16[4,128,512]{2,1,0:T(8,128)(2,1)}) custom-call(s32[4,1024]{1,0:T(4,128)} %bitcast.5, bf16[1024,512]{1,0:T(8,128)(2,1)} %query_ref.3, bf16[4,512,128]{2,1,0:T(8,128)(2,1)} %book_ref.1, f32[2,4,1,512]{3,2,1,0:T(1,128)} %get-tuple-element.22.count_ref), custom_call_target="tpu_custom_call" | custom-call | tf_op jit(solution)/shard_map/forward/pallas_call | solution.py:57
  53.0 1.7 %all-to-all-done.1.prefix_ref = bf16[32,64,128]{2,1,0:T(8,128)(2,1)S(1)} async-done(((bf16[32,64,128]{2,1,0:T(8,128)(2,1)}), bf16[32,64,128]{2,1,0:T(8,128)(2,1)S(1)}, u32[]{:S(2)}, u32[]{:S(2)}) %all-to-all-start.1) | async-done | bytes 524320 | tf_op jit(solution)/shard_map/all_to_all | solution.py:566
  54.8 0.0 collective-permute-done.2.far0_ref
  54.8 0.0 collective-permute-done.3.far1_ref
  54.8 22.6 %backward.1 = (bf16[1024,512]{1,0:T(8,128)(2,1)}, f32[1024,512]{1,0:T(8,128)}, f32[4,512,128]{2,1,0:T(8,128)}, bf16[16,128,128]{2,1,0:T(8,128)(2,1)}, bf16[16,128,128]{2,1,0:T(8,128)(2,1)}) custom-call(s32[1]{0:T(128)} %bitcast.me_ref, s32[1]{0:T(128)} %bitcast.1.core_ref.refs_0_, bf16[1024,512]{1,0:T(8,128)(2,1)} %own_ref.1, ...), custom_call_target="tpu_custom_call" | custom-call | flops 21474836480 | bytes 25165824 | tf_op jit(solution)/shard_map/backward/pallas_call | solution.py:57
  77.4 0.5 collective-permute-start.4
  77.9 1.7 %collective-permute-done.4.refs_4_ = bf16[16,128,128]{2,1,0:T(8,128)(2,1)S(1)} collective-permute-done((bf16[16,128,128]{2,1,0:T(8,128)(2,1)}, bf16[16,128,128]{2,1,0:T(8,128)(2,1)S(1)}, u32[]{:S(2)}, u32[]{:S(2)}) %collective-permute-start.4) | collective-permute-done | bytes 524320 | tf_op jit(solution)/shard_map/ppermute | solution.py:571
  79.6 0.0 copy-start
  79.6 1.3 %fusion = bf16[16,128,128]{2,1,0:T(8,128)(2,1)S(1)} fusion(bf16[16,128,128]{2,1,0:T(8,128)(2,1)} %get-tuple-element.30, bf16[16,128,128]{2,1,0:T(8,128)(2,1)S(1)} %collective-permute-done.4.refs_4_), kind=kLoop, calls=%fused_computation.2 | loop fusion | flops 1048576 | bytes 1572864 | tf_op jit(solution)/shard_map/convert_element_type | solution.py:572
  80.9 15.5 %all_to_all.20.in_ref = bf16[16,128,128]{2,1,0:T(8,128)(2,1)S(1)} all-to-all(bf16[16,128,128]{2,1,0:T(8,128)(2,1)S(1)} %fusion), channel_id=1, replica_groups=mesh['chip'=16,'core'=2,'head'=4] {'chip'}, dimensions={0} | all-to-all | bytes 1048576 | tf_op jit(solution)/shard_map/all_to_all | solution.py:573
  96.4 0.9 suffix_scan.1
  97.2 3.6 %all-to-all-start.3 = ((bf16[16,128,128]{2,1,0:T(8,128)(2,1)}), bf16[16,128,128]{2,1,0:T(8,128)(2,1)S(1)}, u32[]{:S(2)}, u32[]{:S(2)}) async-start(bf16[16,128,128]{2,1,0:T(8,128)(2,1)} %suffix_scan.1), calls=%async_computation.3 | async-start | bytes 1048576 | tf_op jit(solution)/shard_map/all_to_all | solution.py:573
  100.8 10.0 %all-to-all-done.3.refs_3_ = bf16[16,128,128]{2,1,0:T(8,128)(2,1)S(1)} async-done(((bf16[16,128,128]{2,1,0:T(8,128)(2,1)}), bf16[16,128,128]{2,1,0:T(8,128)(2,1)S(1)}, u32[]{:S(2)}, u32[]{:S(2)}) %all-to-all-start.3) | async-done | bytes 524320 | tf_op jit(solution)/shard_map/all_to_all | solution.py:573
  110.8 0.0 copy-done
  110.8 0.2 fusion.2
  111.1 2.6 %collective-permute-start.5 = (bf16[16,128,128]{2,1,0:T(8,128)(2,1)S(1)}, bf16[16,128,128]{2,1,0:T(8,128)(2,1)S(1)}, u32[]{:S(2)}, u32[]{:S(2)}) collective-permute-start(bf16[16,128,128]{2,1,0:T(8,128)(2,1)S(1)} %fusion.2), channel_id=1, source_target_pairs={{0,4},{4,0},{1,5},{5,1},{2,6},{6,2},{3,7},{7,3},{8,12},{12,8},{9,1... | collective-permute-start | bytes 1572872 | tf_op jit(solution)/shard_map/ppermute | solution.py:576
  113.7 2.9 %finish_own.1 = (bf16[1024,512]{1,0:T(8,128)(2,1)}, f32[4,512,128]{2,1,0:T(8,128)}) custom-call(s32[1]{0:T(128)} %bitcast.1.core_ref.refs_0_, s32[4,1024]{1,0:T(4,128)} %bitcast.7, f32[1024,512]{1,0:T(8,128)} %get-tuple-element.29.refs_2_, bf16[16,128,128]{2,1,0:T(8,128)(2,1)S(1)} %all-to-all-done.3.refs_3_, ...), custom_call_target="tpu_custom_call" | custom-call | flops 1073741824 | bytes 8388608 | tf_op jit(solution)/shard_map/finish_own/pallas_call | solution.py:57
  116.6 0.0 collective-permute-done.5.refs_3_
  116.6 2.9 %finish_other.1 = (bf16[1024,512]{1,0:T(8,128)(2,1)}, f32[4,512,128]{2,1,0:T(8,128)}) custom-call(s32[1]{0:T(128)} %bitcast.1.core_ref.refs_0_, s32[4,1024]{1,0:T(4,128)} %bitcast.8, f32[1024,512]{1,0:T(8,128)} %get-tuple-element.29.refs_2_, bf16[16,128,128]{2,1,0:T(8,128)(2,1)S(1)} %collective-permute-done.5.refs_3_, ...), custom_call_target="tpu_custom_call", output_to_operand_aliasing={{0}: (5, {}), {1}: (6, {})} | custom-call | flops 1073741824 | bytes 8388608 | tf_op jit(solution)/shard_map/finish_other/pallas_call | solution.py:57
  (1 shorter events, 0.0 us)
Async XLA Ops:
  0.6 26.0 %collective-permute-start = (bf16[1024,512]{1,0:T(8,128)(2,1)}, bf16[1024,512]{1,0:T(8,128)(2,1)S(1)}, u32[]{:S(2)}, u32[]{:S(2)}) collective-permute-start(bf16[1024,512]{1,0:T(8,128)(2,1)} %own_ref.1), channel_id=1, source_target_pairs={{0,1},{1,2},{2,3},{3,0},{4,5},{5,6},{6,7},{7,4},{8,9},{9,10},{10,1... | collective-permute-start | bytes 3145736 | tf_op jit(solution)/shard_map/ppermute | solution.py:542
  2.7 25.1 %collective-permute-start.1 = (bf16[1024,512]{1,0:T(8,128)(2,1)}, bf16[1024,512]{1,0:T(8,128)(2,1)S(1)}, u32[]{:S(2)}, u32[]{:S(2)}) collective-permute-start(bf16[1024,512]{1,0:T(8,128)(2,1)} %own_ref.1), channel_id=1, source_target_pairs={{0,3},{1,0},{2,1},{3,2},{4,7},{5,4},{6,5},{7,6},{8,11},{9,8},{10,9... | collective-permute-start | bytes 3145736 | tf_op jit(solution)/shard_map/ppermute | solution.py:543
  7.8 23.7 %all-to-all-start = ((bf16[32,96,128]{2,1,0:T(8,128)(2,1)}), bf16[32,96,128]{2,1,0:T(8,128)(2,1)S(1)}, u32[]{:S(2)}, u32[]{:S(2)}) async-start(bf16[32,96,128]{2,1,0:T(8,128)(2,1)} %get-tuple-element.20), calls=%async_computation | async-start | bytes 1572864 | tf_op jit(solution)/shard_map/all_to_all | solution.py:565
  27.5 27.3 %collective-permute-start.2 = (bf16[512,512]{1,0:T(8,128)(2,1)}, bf16[512,512]{1,0:T(8,128)(2,1)S(1)}, u32[]{:S(2)}, u32[]{:S(2)}) collective-permute-start(bf16[512,512]{1,0:T(8,128)(2,1)} %slice.8), channel_id=1, source_target_pairs={{0,1},{1,2},{2,3},{3,0},{4,5},{5,6},{6,7},{7,4},{8,9},{9,10},{10,1... | collective-permute-start | bytes 1572872 | tf_op jit(solution)/shard_map/ppermute | solution.py:545
  28.7 26.1 %collective-permute-start.3 = (bf16[512,512]{1,0:T(8,128)(2,1)}, bf16[512,512]{1,0:T(8,128)(2,1)}, u32[]{:S(2)}, u32[]{:S(2)}) collective-permute-start(bf16[512,512]{1,0:T(8,128)(2,1)} %slice.9), channel_id=1, source_target_pairs={{0,3},{1,0},{2,1},{3,2},{4,7},{5,4},{6,5},{7,6},{8,11},{9,8},{10,9... | collective-permute-start | bytes 1572872 | tf_op jit(solution)/shard_map/ppermute | solution.py:545
  33.1 21.6 %all-to-all-start.1 = ((bf16[32,64,128]{2,1,0:T(8,128)(2,1)}), bf16[32,64,128]{2,1,0:T(8,128)(2,1)S(1)}, u32[]{:S(2)}, u32[]{:S(2)}) async-start(bf16[32,64,128]{2,1,0:T(8,128)(2,1)} %get-tuple-element.26), calls=%async_computation.1 | async-start | bytes 1048576 | tf_op jit(solution)/shard_map/all_to_all | solution.py:566
  77.4 2.3 %collective-permute-start.4 = (bf16[16,128,128]{2,1,0:T(8,128)(2,1)}, bf16[16,128,128]{2,1,0:T(8,128)(2,1)S(1)}, u32[]{:S(2)}, u32[]{:S(2)}) collective-permute-start(bf16[16,128,128]{2,1,0:T(8,128)(2,1)} %get-tuple-element.31), channel_id=1, source_target_pairs={{0,4},{4,0},{1,5},{5,1},{2,6},{6,2},{3,7},{7,3},{8,12},{12,8},{9,1... | collective-permute-start | bytes 1572872 | tf_op jit(solution)/shard_map/ppermute | solution.py:571
  79.6 31.2 %copy-start = (bf16[16,128,128]{2,1,0:T(8,128)(2,1)S(1)}, bf16[16,128,128]{2,1,0:T(8,128)(2,1)}, u32[]{:S(2)}) copy-start(bf16[16,128,128]{2,1,0:T(8,128)(2,1)} %get-tuple-element.30) | copy-start | bytes 1572868
  97.2 13.6 %all-to-all-start.3 = ((bf16[16,128,128]{2,1,0:T(8,128)(2,1)}), bf16[16,128,128]{2,1,0:T(8,128)(2,1)S(1)}, u32[]{:S(2)}, u32[]{:S(2)}) async-start(bf16[16,128,128]{2,1,0:T(8,128)(2,1)} %suffix_scan.1), calls=%async_computation.3 | async-start | bytes 1048576 | tf_op jit(solution)/shard_map/all_to_all | solution.py:573
  111.1 5.5 %collective-permute-start.5 = (bf16[16,128,128]{2,1,0:T(8,128)(2,1)S(1)}, bf16[16,128,128]{2,1,0:T(8,128)(2,1)S(1)}, u32[]{:S(2)}, u32[]{:S(2)}) collective-permute-start(bf16[16,128,128]{2,1,0:T(8,128)(2,1)S(1)} %fusion.2), channel_id=1, source_target_pairs={{0,4},{4,0},{1,5},{5,1},{2,6},{6,2},{3,7},{7,3},{8,12},{12,8},{9,1... | collective-permute-start | bytes 1572872 | tf_op jit(solution)/shard_map/ppermute | solution.py:576

commit v9 on v8

--- a/solution.py
+++ b/solution.py
@@ -26,6 +26,10 @@
 
 def dot_nt(left, right):
     return lax.dot_general(left, right, (((1,), (1,)), ((), ())), preferred_element_type=F32)
+
+
+def space_of(spec):
+    return pltpu.VMEM if spec.memory_space == pltpu.VMEM else pltpu.HBM
 
 
 def call(kernel, name, grid, in_specs, outs, scratch=(), aliases=None, prefetch=0, flops=0, size=0,
@@ -39,7 +43,7 @@
             out_specs=[spec for _, _, spec in outs],
             scratch_shapes=list(scratch),
         ),
-        out_shape=[pltpu.HBM(shape, dtype) for shape, dtype, _ in outs],
+        out_shape=[space_of(spec)(shape, dtype) for shape, dtype, spec in outs],
         input_output_aliases=aliases or {},
         compiler_params=pltpu.CompilerParams(
             dimension_semantics=("arbitrary",) * len(grid), vmem_limit_bytes=limit
@@ -49,8 +53,7 @@
     )
 
     def placed(array, spec):
-        space = pltpu.VMEM if spec.memory_space == pltpu.VMEM else pltpu.HBM
-        return pltpu.with_memory_space_constraint(array, space)
+        return pltpu.with_memory_space_constraint(array, space_of(spec))
 
     def with_places(*args):
         arrays = [placed(a, spec) for a, spec in zip(args[prefetch:], in_specs)]
@@ -342,13 +345,13 @@
                 delta = delta + fold(
                     probs_ref[b, 0, rows, source].astype(F32) * grads[b, n, rows, columns]
                 )
-            delta = jnp.sum(delta, axis=0, keepdims=True) * scale
+            delta = jnp.sum(delta, axis=0, keepdims=True)
             for i in pieces:
                 rows = slice(i * TILE, (i + 1) * TILE)
                 shift = delta
                 if i < entry_tiles:
                     shift = delta * counts[b, rows, :]
-                piece = grads[b, n, rows, columns] * scale - shift
+                piece = grads[b, n, rows, columns] - shift
                 piece = probs_ref[b, 0, rows, source].astype(F32) * piece
                 score_grad[b, n, rows, columns] = piece.astype(BF16)
             if j == 0:
@@ -362,9 +365,9 @@
         at = b * BLOCK + n * PART
         span = slice(at, at + PART)
         sums_v[b][n] = dot(probs_ref[b, 0, :used, n * PART : (n + 1) * PART], dout[head, span, :])
-        sums_k[b][n] = dot(score_grad[b, n, :used, :], query_ref[span, :])
+        sums_k[b][n] = dot(score_grad[b, n, :used, :], query_ref[span, :]) * scale
         grad_t = dot(wide_t[b, :, :used], score_grad[b, n, :used, :])
-        grad_query_ref[span, :] = grad_t.T.astype(BF16)
+        grad_query_ref[span, :] = (grad_t * scale).T.astype(BF16)
 
     order = [(b, n) for b in range(blocks) for n in range(parts)]
     for b in range(blocks):
@@ -410,19 +413,20 @@
             mine = first[:entries] + last[:entries] + dot(hot[b], key_grad[b])
             code = mine if b == 0 else code + mine
 
-    def write(ref):
+    def write(ref, first):
         for k in range(entries // HALF):
             rows = slice(k * HALF, (k + 1) * HALF)
-            ref[k, :HALF, :] = part[rows].astype(BF16)
-            ref[k, HALF:, :] = code[rows].astype(BF16)
+            at = first + k
+            ref[at, :HALF, :] = part[rows].astype(BF16)
+            ref[at, HALF:, :] = code[rows].astype(BF16)
 
     @pl.when(step < 2)
     def _():
-        write(give_ref)
+        write(give_ref, lax.rem(step, 2) * (entries // HALF))
 
     @pl.when(step >= 2)
     def _():
-        write(keep_ref)
+        write(keep_ref, 0)
 
 
 def backward(me, core, pieces, weight, codes, queries, values, probs, keys, book_t, prefix, counts,
@@ -459,7 +463,7 @@
         (queries.shape, BF16, rows_of),
         (queries.shape, F32, rows_of),
         ((heads, entries, width), F32, per_head),
-        (both_heads, BF16, pl.BlockSpec(shape, lambda s, *_: (jnp.minimum(s, 1), 0, 0))),
+        (both_heads, BF16, IN_VMEM),
         (both_heads, BF16, pl.BlockSpec(shape, lambda s, *_: (jnp.maximum(s - 2, 0), 0, 0))),
     ]
     return call(

time: 120 us -> 119 us (level)
  no operation moved by 1% of the time
where the time goes in v9:
time: 119 us; the launch traced here: 118 us
  Pallas kernels  43.6 us (37%)
  starting transfers between devices  32.4 us (27%)
  waiting for transfers between devices  23.1 us (19%)
  blocking collectives  15.4 us (13%)
  local copies, waits for them, and re-layouts  1.71 us (1%)
  other arithmetic  1.51 us (1%)
    pallas_call x7, Pallas kernels, with_places(): return run(*args[:prefetch], *arrays)  43.6 us
    all_to_all x1, blocking collectives, per_device(): later = between_chips(suffix_scan(between_chips(chip)))  15.4 us
    all_to_all x1, starting transfers between devices, per_device(): prefix = exchange(prefix)  10.1 us
    all_to_all x1, waiting for transfers between devices, per_device(): later = between_chips(suffix_scan(between_chips(chip)))  9.96 us
    all_to_all x1, starting transfers between devices, per_device(): prefix, counts = prefix_scan(me_seq, exchange(send), first_count)  9.45 us
    ppermute x1, waiting for transfers between devices, ring_pieces(): left = lax.ppermute(array, 'head', up)  9.38 us
    all_to_all x1, starting transfers between devices, per_device(): later = between_chips(suffix_scan(between_chips(chip)))  3.57 us
    ppermute x1, starting transfers between devices, per_device(): theirs = other_core((later.astype(F32) + mine).astype(BF16))  2.6 us
  transfers between devices with their start and end apart: 9, of which 5 were waited for; matrix products, arithmetic and copies ran while one was open for 1% of the time, Pallas kernels for 15%

profile of v9, /device:TPU:1, one launch (start us, length us, event | category | flops | bytes accessed | tf_op | source)
XLA Modules:
  0.0 118.4 jit_solution(6360908149887961257)
XLA Ops:
  0.6 2.1 %collective-permute-start = (bf16[1024,512]{1,0:T(8,128)(2,1)}, bf16[1024,512]{1,0:T(8,128)(2,1)S(1)}, u32[]{:S(2)}, u32[]{:S(2)}) collective-permute-start(bf16[1024,512]{1,0:T(8,128)(2,1)} %own_ref.1), channel_id=1, source_target_pairs={{0,1},{1,2},{2,3},{3,0},{4,5},{5,6},{6,7},{7,4},{8,9},{9,10},{10,1... | collective-permute-start | bytes 3145736 | tf_op jit(solution)/shard_map/ppermute | solution.py:546
  2.7 1.4 %collective-permute-start.1 = (bf16[1024,512]{1,0:T(8,128)(2,1)}, bf16[1024,512]{1,0:T(8,128)(2,1)S(1)}, u32[]{:S(2)}, u32[]{:S(2)}) collective-permute-start(bf16[1024,512]{1,0:T(8,128)(2,1)} %own_ref.1), channel_id=1, source_target_pairs={{0,3},{1,0},{2,1},{3,2},{4,7},{5,4},{6,5},{7,6},{8,11},{9,8},{10,9... | collective-permute-start | bytes 3145736 | tf_op jit(solution)/shard_map/ppermute | solution.py:547
  4.1 3.7 %own_sums.1 = (bf16[32,96,128]{2,1,0:T(8,128)(2,1)}, f32[4,512,128]{2,1,0:T(8,128)}, f32[4,1,512]{2,1,0:T(1,128)}) custom-call(s32[4,1024]{1,0:T(4,128)} %bitcast.4, bf16[1024,512]{1,0:T(8,128)(2,1)} %value_ref.3), custom_call_target="tpu_custom_call" | custom-call | tf_op jit(solution)/shard_map/own_sums/pallas_call | solution.py:60
  7.8 9.4 %all-to-all-start = ((bf16[32,96,128]{2,1,0:T(8,128)(2,1)}), bf16[32,96,128]{2,1,0:T(8,128)(2,1)S(1)}, u32[]{:S(2)}, u32[]{:S(2)}) async-start(bf16[32,96,128]{2,1,0:T(8,128)(2,1)} %get-tuple-element.20), calls=%async_computation | async-start | bytes 1572864 | tf_op jit(solution)/shard_map/all_to_all | solution.py:569
  17.3 9.4 %collective-permute-done.left_ref = bf16[1024,512]{1,0:T(8,128)(2,1)S(1)} collective-permute-done((bf16[1024,512]{1,0:T(8,128)(2,1)}, bf16[1024,512]{1,0:T(8,128)(2,1)S(1)}, u32[]{:S(2)}, u32[]{:S(2)}) %collective-permute-start) | collective-permute-done | bytes 1048608 | tf_op jit(solution)/shard_map/ppermute | solution.py:546
  26.7 0.8 slice.8
  27.5 0.3 collective-permute-start.2
  27.8 0.0 collective-permute-done.1.right_ref
  27.8 0.9 slice.9
  28.7 2.4 %collective-permute-start.3 = (bf16[512,512]{1,0:T(8,128)(2,1)}, bf16[512,512]{1,0:T(8,128)(2,1)}, u32[]{:S(2)}, u32[]{:S(2)}) collective-permute-start(bf16[512,512]{1,0:T(8,128)(2,1)} %slice.9), channel_id=1, source_target_pairs={{0,3},{1,0},{2,1},{3,2},{4,7},{5,4},{6,5},{7,6},{8,11},{9,8},{10,9... | collective-permute-start | bytes 1572872 | tf_op jit(solution)/shard_map/ppermute | solution.py:549
  31.0 0.5 all-to-all-done.in_ref
  31.5 1.6 %prefix_scan.1 = (bf16[32,64,128]{2,1,0:T(8,128)(2,1)}, f32[2,4,1,512]{3,2,1,0:T(1,128)}) custom-call(s32[1]{0:T(128)} %bitcast.3.me_ref, bf16[32,96,128]{2,1,0:T(8,128)(2,1)S(1)} %all-to-all-done.in_ref, f32[4,1,512]{2,1,0:T(1,128)} %get-tuple-element.21.first_ref), custom_call_target="tpu_custom_call" | custom-call | tf_op jit(solution)/shard_map/prefix_scan/pallas_call | solution.py:60
  33.1 10.1 %all-to-all-start.1 = ((bf16[32,64,128]{2,1,0:T(8,128)(2,1)}), bf16[32,64,128]{2,1,0:T(8,128)(2,1)S(1)}, u32[]{:S(2)}, u32[]{:S(2)}) async-start(bf16[32,64,128]{2,1,0:T(8,128)(2,1)} %get-tuple-element.26), calls=%async_computation.1 | async-start | bytes 1048576 | tf_op jit(solution)/shard_map/all_to_all | solution.py:570
  43.2 9.8 %forward.1 = (bf16[2,4,1024,512]{3,2,1,0:T(8,128)(2,1)}, bf16[2,4,128,512]{3,2,1,0:T(8,128)(2,1)}, bf16[4,128,512]{2,1,0:T(8,128)(2,1)}) custom-call(s32[4,1024]{1,0:T(4,128)} %bitcast.5, bf16[1024,512]{1,0:T(8,128)(2,1)} %query_ref.3, bf16[4,512,128]{2,1,0:T(8,128)(2,1)} %book_ref.1, f32[2,4,1,512]{3,2,1,0:T(1,128)} %get-tuple-element.22.count_ref), custom_call_target="tpu_custom_call" | custom-call | tf_op jit(solution)/shard_map/forward/pallas_call | solution.py:60
  53.0 1.7 %all-to-all-done.1.prefix_ref = bf16[32,64,128]{2,1,0:T(8,128)(2,1)S(1)} async-done(((bf16[32,64,128]{2,1,0:T(8,128)(2,1)}), bf16[32,64,128]{2,1,0:T(8,128)(2,1)S(1)}, u32[]{:S(2)}, u32[]{:S(2)}) %all-to-all-start.1) | async-done | bytes 524320 | tf_op jit(solution)/shard_map/all_to_all | solution.py:570
  54.7 0.0 collective-permute-done.2.far0_ref
  54.7 0.0 collective-permute-done.3.far1_ref
  54.7 21.8 %backward.1 = (bf16[1024,512]{1,0:T(8,128)(2,1)}, f32[1024,512]{1,0:T(8,128)}, f32[4,512,128]{2,1,0:T(8,128)}, bf16[16,128,128]{2,1,0:T(8,128)(2,1)S(1)}, bf16[16,128,128]{2,1,0:T(8,128)(2,1)}) custom-call(s32[1]{0:T(128)} %bitcast.me_ref, s32[1]{0:T(128)} %bitcast.1.core_ref.refs_0_, bf16[1024,512]{1,0:T(8,128)(2,1)} %own_ref.1, ...), custom_call_target="tpu_custom_call" | custom-call | flops 21474836480 | bytes 25165824 | tf_op jit(solution)/shard_map/backward/pallas_call | solution.py:60
  76.5 0.5 collective-permute-start.4
  77.0 1.5 %collective-permute-done.4.refs_4_ = bf16[16,128,128]{2,1,0:T(8,128)(2,1)S(1)} collective-permute-done((bf16[16,128,128]{2,1,0:T(8,128)(2,1)S(1)}, bf16[16,128,128]{2,1,0:T(8,128)(2,1)S(1)}, u32[]{:S(2)}, u32[]{:S(2)}) %collective-permute-start.4) | collective-permute-done | bytes 524320 | tf_op jit(solution)/shard_map/ppermute | solution.py:575
  78.6 0.0 copy-start
  78.6 1.3 %fusion = bf16[16,128,128]{2,1,0:T(8,128)(2,1)S(1)} fusion(bf16[16,128,128]{2,1,0:T(8,128)(2,1)} %get-tuple-element.30, bf16[16,128,128]{2,1,0:T(8,128)(2,1)S(1)} %collective-permute-done.4.refs_4_), kind=kLoop, calls=%fused_computation.2 | loop fusion | flops 1048576 | bytes 1572864 | tf_op jit(solution)/shard_map/convert_element_type | solution.py:576
  79.8 15.4 %all_to_all.20.in_ref = bf16[16,128,128]{2,1,0:T(8,128)(2,1)S(1)} all-to-all(bf16[16,128,128]{2,1,0:T(8,128)(2,1)S(1)} %fusion), channel_id=1, replica_groups=mesh['chip'=16,'core'=2,'head'=4] {'chip'}, dimensions={0} | all-to-all | bytes 1048576 | tf_op jit(solution)/shard_map/all_to_all | solution.py:577
  95.3 0.9 suffix_scan.1
  96.2 3.6 %all-to-all-start.3 = ((bf16[16,128,128]{2,1,0:T(8,128)(2,1)}), bf16[16,128,128]{2,1,0:T(8,128)(2,1)S(1)}, u32[]{:S(2)}, u32[]{:S(2)}) async-start(bf16[16,128,128]{2,1,0:T(8,128)(2,1)} %suffix_scan.1), calls=%async_computation.3 | async-start | bytes 1048576 | tf_op jit(solution)/shard_map/all_to_all | solution.py:577
  99.8 10.0 %all-to-all-done.3.refs_3_ = bf16[16,128,128]{2,1,0:T(8,128)(2,1)S(1)} async-done(((bf16[16,128,128]{2,1,0:T(8,128)(2,1)}), bf16[16,128,128]{2,1,0:T(8,128)(2,1)S(1)}, u32[]{:S(2)}, u32[]{:S(2)}) %all-to-all-start.3) | async-done | bytes 524320 | tf_op jit(solution)/shard_map/all_to_all | solution.py:577
  109.7 0.0 copy-done
  109.7 0.2 fusion.2
  110.0 2.6 %collective-permute-start.5 = (bf16[16,128,128]{2,1,0:T(8,128)(2,1)S(1)}, bf16[16,128,128]{2,1,0:T(8,128)(2,1)S(1)}, u32[]{:S(2)}, u32[]{:S(2)}) collective-permute-start(bf16[16,128,128]{2,1,0:T(8,128)(2,1)S(1)} %fusion.2), channel_id=1, source_target_pairs={{0,4},{4,0},{1,5},{5,1},{2,6},{6,2},{3,7},{7,3},{8,12},{12,8},{9,1... | collective-permute-start | bytes 1572872 | tf_op jit(solution)/shard_map/ppermute | solution.py:580
  112.6 2.9 %finish_own.1 = (bf16[1024,512]{1,0:T(8,128)(2,1)}, f32[4,512,128]{2,1,0:T(8,128)}) custom-call(s32[1]{0:T(128)} %bitcast.1.core_ref.refs_0_, s32[4,1024]{1,0:T(4,128)} %bitcast.7, f32[1024,512]{1,0:T(8,128)} %get-tuple-element.29.refs_2_, bf16[16,128,128]{2,1,0:T(8,128)(2,1)S(1)} %all-to-all-done.3.refs_3_, ...), custom_call_target="tpu_custom_call" | custom-call | flops 1073741824 | bytes 8388608 | tf_op jit(solution)/shard_map/finish_own/pallas_call | solution.py:60
  115.5 0.0 collective-permute-done.5.refs_3_
  115.5 2.9 %finish_other.1 = (bf16[1024,512]{1,0:T(8,128)(2,1)}, f32[4,512,128]{2,1,0:T(8,128)}) custom-call(s32[1]{0:T(128)} %bitcast.1.core_ref.refs_0_, s32[4,1024]{1,0:T(4,128)} %bitcast.8, f32[1024,512]{1,0:T(8,128)} %get-tuple-element.29.refs_2_, bf16[16,128,128]{2,1,0:T(8,128)(2,1)S(1)} %collective-permute-done.5.refs_3_, ...), custom_call_target="tpu_custom_call", output_to_operand_aliasing={{0}: (5, {}), {1}: (6, {})} | custom-call | flops 1073741824 | bytes 8388608 | tf_op jit(solution)/shard_map/finish_other/pallas_call | solution.py:60
  (1 shorter events, 0.0 us)
Async XLA Ops:
  0.6 26.0 %collective-permute-start = (bf16[1024,512]{1,0:T(8,128)(2,1)}, bf16[1024,512]{1,0:T(8,128)(2,1)S(1)}, u32[]{:S(2)}, u32[]{:S(2)}) collective-permute-start(bf16[1024,512]{1,0:T(8,128)(2,1)} %own_ref.1), channel_id=1, source_target_pairs={{0,1},{1,2},{2,3},{3,0},{4,5},{5,6},{6,7},{7,4},{8,9},{9,10},{10,1... | collective-permute-start | bytes 3145736 | tf_op jit(solution)/shard_map/ppermute | solution.py:546
  2.7 25.1 %collective-permute-start.1 = (bf16[1024,512]{1,0:T(8,128)(2,1)}, bf16[1024,512]{1,0:T(8,128)(2,1)S(1)}, u32[]{:S(2)}, u32[]{:S(2)}) collective-permute-start(bf16[1024,512]{1,0:T(8,128)(2,1)} %own_ref.1), channel_id=1, source_target_pairs={{0,3},{1,0},{2,1},{3,2},{4,7},{5,4},{6,5},{7,6},{8,11},{9,8},{10,9... | collective-permute-start | bytes 3145736 | tf_op jit(solution)/shard_map/ppermute | solution.py:547
  7.8 23.7 %all-to-all-start = ((bf16[32,96,128]{2,1,0:T(8,128)(2,1)}), bf16[32,96,128]{2,1,0:T(8,128)(2,1)S(1)}, u32[]{:S(2)}, u32[]{:S(2)}) async-start(bf16[32,96,128]{2,1,0:T(8,128)(2,1)} %get-tuple-element.20), calls=%async_computation | async-start | bytes 1572864 | tf_op jit(solution)/shard_map/all_to_all | solution.py:569
  27.5 27.3 %collective-permute-start.2 = (bf16[512,512]{1,0:T(8,128)(2,1)}, bf16[512,512]{1,0:T(8,128)(2,1)S(1)}, u32[]{:S(2)}, u32[]{:S(2)}) collective-permute-start(bf16[512,512]{1,0:T(8,128)(2,1)} %slice.8), channel_id=1, source_target_pairs={{0,1},{1,2},{2,3},{3,0},{4,5},{5,6},{6,7},{7,4},{8,9},{9,10},{10,1... | collective-permute-start | bytes 1572872 | tf_op jit(solution)/shard_map/ppermute | solution.py:549
  28.7 26.1 %collective-permute-start.3 = (bf16[512,512]{1,0:T(8,128)(2,1)}, bf16[512,512]{1,0:T(8,128)(2,1)}, u32[]{:S(2)}, u32[]{:S(2)}) collective-permute-start(bf16[512,512]{1,0:T(8,128)(2,1)} %slice.9), channel_id=1, source_target_pairs={{0,3},{1,0},{2,1},{3,2},{4,7},{5,4},{6,5},{7,6},{8,11},{9,8},{10,9... | collective-permute-start | bytes 1572872 | tf_op jit(solution)/shard_map/ppermute | solution.py:549
  33.1 21.6 %all-to-all-start.1 = ((bf16[32,64,128]{2,1,0:T(8,128)(2,1)}), bf16[32,64,128]{2,1,0:T(8,128)(2,1)S(1)}, u32[]{:S(2)}, u32[]{:S(2)}) async-start(bf16[32,64,128]{2,1,0:T(8,128)(2,1)} %get-tuple-element.26), calls=%async_computation.1 | async-start | bytes 1048576 | tf_op jit(solution)/shard_map/all_to_all | solution.py:570
  76.5 2.1 %collective-permute-start.4 = (bf16[16,128,128]{2,1,0:T(8,128)(2,1)S(1)}, bf16[16,128,128]{2,1,0:T(8,128)(2,1)S(1)}, u32[]{:S(2)}, u32[]{:S(2)}) collective-permute-start(bf16[16,128,128]{2,1,0:T(8,128)(2,1)S(1)} %get-tuple-element.31), channel_id=1, source_target_pairs={{0,4},{4,0},{1,5},{5,1},{2,6},{6,2},{3,7},{7,3},{8,12},{12,8},{9,1... | collective-permute-start | bytes 1572872 | tf_op jit(solution)/shard_map/ppermute | solution.py:575
  78.6 31.2 %copy-start = (bf16[16,128,128]{2,1,0:T(8,128)(2,1)S(1)}, bf16[16,128,128]{2,1,0:T(8,128)(2,1)}, u32[]{:S(2)}) copy-start(bf16[16,128,128]{2,1,0:T(8,128)(2,1)} %get-tuple-element.30) | copy-start | bytes 1572868
  96.2 13.6 %all-to-all-start.3 = ((bf16[16,128,128]{2,1,0:T(8,128)(2,1)}), bf16[16,128,128]{2,1,0:T(8,128)(2,1)S(1)}, u32[]{:S(2)}, u32[]{:S(2)}) async-start(bf16[16,128,128]{2,1,0:T(8,128)(2,1)} %suffix_scan.1), calls=%async_computation.3 | async-start | bytes 1048576 | tf_op jit(solution)/shard_map/all_to_all | solution.py:577
  110.0 5.5 %collective-permute-start.5 = (bf16[16,128,128]{2,1,0:T(8,128)(2,1)S(1)}, bf16[16,128,128]{2,1,0:T(8,128)(2,1)S(1)}, u32[]{:S(2)}, u32[]{:S(2)}) collective-permute-start(bf16[16,128,128]{2,1,0:T(8,128)(2,1)S(1)} %fusion.2), channel_id=1, source_target_pairs={{0,4},{4,0},{1,5},{5,1},{2,6},{6,2},{3,7},{7,3},{8,12},{12,8},{9,1... | collective-permute-start | bytes 1572872 | tf_op jit(solution)/shard_map/ppermute | solution.py:580

commit v10 on v9

--- a/solution.py
+++ b/solution.py
@@ -185,6 +185,17 @@
     return call(
         suffix_kernel, "suffix_scan", (1,), [IN_VMEM], [(pieces.shape, BF16, spec)], size=2 << 20
     )(pieces)[0]
+
+
+def add_kernel(kept_ref, got_ref, out_ref):
+    out_ref[...] = (kept_ref[...].astype(F32) + got_ref[...].astype(F32)).astype(BF16)
+
+
+def chip_sums(kept, got):
+    spec = pl.BlockSpec(kept.shape, lambda i: (0, 0, 0))
+    return call(
+        add_kernel, "chip_sums", (1,), [spec, IN_VMEM], [(kept.shape, BF16, IN_VMEM)], size=1 << 20
+    )(kept, got)[0]
 
 
 def count_columns(number):
@@ -573,7 +584,7 @@
         me, core_at, pieces, out_weight, codes, queries, values, probs, keys, book_t, prefix, counts, first
     )
     got = other_core(give)
-    chip = (keep.astype(F32) + got.astype(F32)).astype(BF16)
+    chip = chip_sums(keep, got)
     later = between_chips(suffix_scan(between_chips(chip)))
     is_value = lax.broadcasted_iota(jnp.int32, later.shape, 1) < HALF
     mine = jnp.where(is_value & (core == 1), keep.astype(F32), 0.0)

time: 119 us -> 119 us (level)
  Pallas kernels: 43.6 us -> 44.9 us
  other arithmetic: 1.51 us -> 0.26 us
    convert_element_type x1 -> x0, other arithmetic: 1.25 us -> none  [per_device(): chip = (keep.astype(F32) + got.astype(F32)).astype(BF16)]
    pallas_call x7 -> x8, Pallas kernels: 43.6 us -> 44.9 us  [with_places(): return run(*args[:prefetch], *arrays)]
where the time goes in v10:
time: 119 us; the launch traced here: 118 us
  Pallas kernels  44.9 us (38%)
  starting transfers between devices  32.4 us (27%)
  waiting for transfers between devices  23.1 us (19%)
  blocking collectives  15.4 us (13%)
  local copies, waits for them, and re-layouts  1.71 us (1%)
    pallas_call x8, Pallas kernels, with_places(): return run(*args[:prefetch], *arrays)  44.9 us
    all_to_all x1, blocking collectives, per_device(): later = between_chips(suffix_scan(between_chips(chip)))  15.4 us
    all_to_all x1, starting transfers between devices, per_device(): prefix = exchange(prefix)  10.1 us
    all_to_all x1, waiting for transfers between devices, per_device(): later = between_chips(suffix_scan(between_chips(chip)))  9.96 us
    all_to_all x1, starting transfers between devices, per_device(): prefix, counts = prefix_scan(me_seq, exchange(send), first_count)  9.45 us
    ppermute x1, waiting for transfers between devices, ring_pieces(): left = lax.ppermute(array, 'head', up)  9.38 us
    all_to_all x1, starting transfers between devices, per_device(): later = between_chips(suffix_scan(between_chips(chip)))  3.57 us
    ppermute x1, starting transfers between devices, per_device(): theirs = other_core((later.astype(F32) + mine).astype(BF16))  2.6 us
  transfers between devices with their start and end apart: 9, of which 5 were waited for; matrix products, arithmetic and copies ran while one was open for 1% of the time, Pallas kernels for 15%

profile of v10, /device:TPU:1, one launch (start us, length us, event | category | flops | bytes accessed | tf_op | source)
XLA Modules:
  0.0 118.4 jit_solution(14148892782989610661)
XLA Ops:
  0.6 2.1 %collective-permute-start = (bf16[1024,512]{1,0:T(8,128)(2,1)}, bf16[1024,512]{1,0:T(8,128)(2,1)S(1)}, u32[]{:S(2)}, u32[]{:S(2)}) collective-permute-start(bf16[1024,512]{1,0:T(8,128)(2,1)} %own_ref.1), channel_id=1, source_target_pairs={{0,1},{1,2},{2,3},{3,0},{4,5},{5,6},{6,7},{7,4},{8,9},{9,10},{10,1... | collective-permute-start | bytes 3145736 | tf_op jit(solution)/shard_map/ppermute | solution.py:557
  2.7 1.4 %collective-permute-start.1 = (bf16[1024,512]{1,0:T(8,128)(2,1)}, bf16[1024,512]{1,0:T(8,128)(2,1)S(1)}, u32[]{:S(2)}, u32[]{:S(2)}) collective-permute-start(bf16[1024,512]{1,0:T(8,128)(2,1)} %own_ref.1), channel_id=1, source_target_pairs={{0,3},{1,0},{2,1},{3,2},{4,7},{5,4},{6,5},{7,6},{8,11},{9,8},{10,9... | collective-permute-start | bytes 3145736 | tf_op jit(solution)/shard_map/ppermute | solution.py:558
  4.1 3.7 %own_sums.1 = (bf16[32,96,128]{2,1,0:T(8,128)(2,1)}, f32[4,512,128]{2,1,0:T(8,128)}, f32[4,1,512]{2,1,0:T(1,128)}) custom-call(s32[4,1024]{1,0:T(4,128)} %bitcast.4, bf16[1024,512]{1,0:T(8,128)(2,1)} %value_ref.3), custom_call_target="tpu_custom_call" | custom-call | tf_op jit(solution)/shard_map/own_sums/pallas_call | solution.py:60
  7.8 9.4 %all-to-all-start = ((bf16[32,96,128]{2,1,0:T(8,128)(2,1)}), bf16[32,96,128]{2,1,0:T(8,128)(2,1)S(1)}, u32[]{:S(2)}, u32[]{:S(2)}) async-start(bf16[32,96,128]{2,1,0:T(8,128)(2,1)} %get-tuple-element.20), calls=%async_computation | async-start | bytes 1572864 | tf_op jit(solution)/shard_map/all_to_all | solution.py:580
  17.3 9.4 %collective-permute-done.left_ref = bf16[1024,512]{1,0:T(8,128)(2,1)S(1)} collective-permute-done((bf16[1024,512]{1,0:T(8,128)(2,1)}, bf16[1024,512]{1,0:T(8,128)(2,1)S(1)}, u32[]{:S(2)}, u32[]{:S(2)}) %collective-permute-start) | collective-permute-done | bytes 1048608 | tf_op jit(solution)/shard_map/ppermute | solution.py:557
  26.7 0.8 slice.8
  27.5 0.3 collective-permute-start.2
  27.8 0.0 collective-permute-done.1.right_ref
  27.8 0.9 slice.9
  28.7 2.4 %collective-permute-start.3 = (bf16[512,512]{1,0:T(8,128)(2,1)}, bf16[512,512]{1,0:T(8,128)(2,1)}, u32[]{:S(2)}, u32[]{:S(2)}) collective-permute-start(bf16[512,512]{1,0:T(8,128)(2,1)} %slice.9), channel_id=1, source_target_pairs={{0,3},{1,0},{2,1},{3,2},{4,7},{5,4},{6,5},{7,6},{8,11},{9,8},{10,9... | collective-permute-start | bytes 1572872 | tf_op jit(solution)/shard_map/ppermute | solution.py:560
  31.0 0.5 all-to-all-done.in_ref
  31.5 1.6 %prefix_scan.1 = (bf16[32,64,128]{2,1,0:T(8,128)(2,1)}, f32[2,4,1,512]{3,2,1,0:T(1,128)}) custom-call(s32[1]{0:T(128)} %bitcast.3.me_ref, bf16[32,96,128]{2,1,0:T(8,128)(2,1)S(1)} %all-to-all-done.in_ref, f32[4,1,512]{2,1,0:T(1,128)} %get-tuple-element.21.first_ref), custom_call_target="tpu_custom_call" | custom-call | tf_op jit(solution)/shard_map/prefix_scan/pallas_call | solution.py:60
  33.1 10.1 %all-to-all-start.1 = ((bf16[32,64,128]{2,1,0:T(8,128)(2,1)}), bf16[32,64,128]{2,1,0:T(8,128)(2,1)S(1)}, u32[]{:S(2)}, u32[]{:S(2)}) async-start(bf16[32,64,128]{2,1,0:T(8,128)(2,1)} %get-tuple-element.26), calls=%async_computation.1 | async-start | bytes 1048576 | tf_op jit(solution)/shard_map/all_to_all | solution.py:581
  43.2 9.8 %forward.1 = (bf16[2,4,1024,512]{3,2,1,0:T(8,128)(2,1)}, bf16[2,4,128,512]{3,2,1,0:T(8,128)(2,1)}, bf16[4,128,512]{2,1,0:T(8,128)(2,1)}) custom-call(s32[4,1024]{1,0:T(4,128)} %bitcast.5, bf16[1024,512]{1,0:T(8,128)(2,1)} %query_ref.3, bf16[4,512,128]{2,1,0:T(8,128)(2,1)} %book_ref.1, f32[2,4,1,512]{3,2,1,0:T(1,128)} %get-tuple-element.22.count_ref), custom_call_target="tpu_custom_call" | custom-call | tf_op jit(solution)/shard_map/forward/pallas_call | solution.py:60
  53.0 1.7 %all-to-all-done.1.prefix_ref = bf16[32,64,128]{2,1,0:T(8,128)(2,1)S(1)} async-done(((bf16[32,64,128]{2,1,0:T(8,128)(2,1)}), bf16[32,64,128]{2,1,0:T(8,128)(2,1)S(1)}, u32[]{:S(2)}, u32[]{:S(2)}) %all-to-all-start.1) | async-done | bytes 524320 | tf_op jit(solution)/shard_map/all_to_all | solution.py:581
  54.7 0.0 collective-permute-done.2.far0_ref
  54.7 0.0 collective-permute-done.3.far1_ref
  54.7 21.8 %backward.1 = (bf16[1024,512]{1,0:T(8,128)(2,1)}, f32[1024,512]{1,0:T(8,128)}, f32[4,512,128]{2,1,0:T(8,128)}, bf16[16,128,128]{2,1,0:T(8,128)(2,1)S(1)}, bf16[16,128,128]{2,1,0:T(8,128)(2,1)}) custom-call(s32[1]{0:T(128)} %bitcast.me_ref, s32[1]{0:T(128)} %bitcast.1.core_ref.refs_0_, bf16[1024,512]{1,0:T(8,128)(2,1)} %own_ref.1, ...), custom_call_target="tpu_custom_call" | custom-call | flops 21474836480 | bytes 25165824 | tf_op jit(solution)/shard_map/backward/pallas_call | solution.py:60
  76.5 0.5 collective-permute-start.4
  77.0 1.5 %collective-permute-done.4.got_ref.refs_4_ = bf16[16,128,128]{2,1,0:T(8,128)(2,1)S(1)} collective-permute-done((bf16[16,128,128]{2,1,0:T(8,128)(2,1)S(1)}, bf16[16,128,128]{2,1,0:T(8,128)(2,1)S(1)}, u32[]{:S(2)}, u32[]{:S(2)}) %collective-permute-start.4) | collective-permute-done | bytes 524320 | tf_op jit(solution)/shard_map/ppermute | solution.py:586
  78.6 0.0 copy-start
  78.6 1.2 %chip_sums.1 = bf16[16,128,128]{2,1,0:T(8,128)(2,1)S(1)} custom-call(bf16[16,128,128]{2,1,0:T(8,128)(2,1)} %get-tuple-element.30.kept_ref, bf16[16,128,128]{2,1,0:T(8,128)(2,1)S(1)} %collective-permute-done.4.got_ref.refs_4_), custom_call_target="tpu_custom_call" | custom-call | bytes 1048576 | tf_op jit(solution)/shard_map/chip_sums/pallas_call | solution.py:60
  79.8 15.4 %all_to_all.20.in_ref = bf16[16,128,128]{2,1,0:T(8,128)(2,1)S(1)} all-to-all(bf16[16,128,128]{2,1,0:T(8,128)(2,1)S(1)} %chip_sums.1), channel_id=1, replica_groups=mesh['chip'=16,'core'=2,'head'=4] {'chip'}, dimensions={0} | all-to-all | bytes 1048576 | tf_op jit(solution)/shard_map/all_to_all | solution.py:588
  95.3 0.9 suffix_scan.1
  96.1 3.6 %all-to-all-start.3 = ((bf16[16,128,128]{2,1,0:T(8,128)(2,1)}), bf16[16,128,128]{2,1,0:T(8,128)(2,1)S(1)}, u32[]{:S(2)}, u32[]{:S(2)}) async-start(bf16[16,128,128]{2,1,0:T(8,128)(2,1)} %suffix_scan.1), calls=%async_computation.3 | async-start | bytes 1048576 | tf_op jit(solution)/shard_map/all_to_all | solution.py:588
  99.7 10.0 %all-to-all-done.3.refs_3_ = bf16[16,128,128]{2,1,0:T(8,128)(2,1)S(1)} async-done(((bf16[16,128,128]{2,1,0:T(8,128)(2,1)}), bf16[16,128,128]{2,1,0:T(8,128)(2,1)S(1)}, u32[]{:S(2)}, u32[]{:S(2)}) %all-to-all-start.3) | async-done | bytes 524320 | tf_op jit(solution)/shard_map/all_to_all | solution.py:588
  109.7 0.0 copy-done
  109.7 0.2 add_convert_fusion
  110.0 2.6 %collective-permute-start.5 = (bf16[16,128,128]{2,1,0:T(8,128)(2,1)S(1)}, bf16[16,128,128]{2,1,0:T(8,128)(2,1)S(1)}, u32[]{:S(2)}, u32[]{:S(2)}) collective-permute-start(bf16[16,128,128]{2,1,0:T(8,128)(2,1)S(1)} %add_convert_fusion), channel_id=1, source_target_pairs={{0,4},{4,0},{1,5},{5,1},{2,6},{6,2},{3,7},{7,3},{8,12},{12,8},{9,1... | collective-permute-start | bytes 1572872 | tf_op jit(solution)/shard_map/ppermute | solution.py:591
  112.6 2.9 %finish_own.1 = (bf16[1024,512]{1,0:T(8,128)(2,1)}, f32[4,512,128]{2,1,0:T(8,128)}) custom-call(s32[1]{0:T(128)} %bitcast.1.core_ref.refs_0_, s32[4,1024]{1,0:T(4,128)} %bitcast.7, f32[1024,512]{1,0:T(8,128)} %get-tuple-element.29.refs_2_, bf16[16,128,128]{2,1,0:T(8,128)(2,1)S(1)} %all-to-all-done.3.refs_3_, ...), custom_call_target="tpu_custom_call" | custom-call | flops 1073741824 | bytes 8388608 | tf_op jit(solution)/shard_map/finish_own/pallas_call | solution.py:60
  115.5 0.0 collective-permute-done.5.refs_3_
  115.5 2.9 %finish_other.1 = (bf16[1024,512]{1,0:T(8,128)(2,1)}, f32[4,512,128]{2,1,0:T(8,128)}) custom-call(s32[1]{0:T(128)} %bitcast.1.core_ref.refs_0_, s32[4,1024]{1,0:T(4,128)} %bitcast.8, f32[1024,512]{1,0:T(8,128)} %get-tuple-element.29.refs_2_, bf16[16,128,128]{2,1,0:T(8,128)(2,1)S(1)} %collective-permute-done.5.refs_3_, ...), custom_call_target="tpu_custom_call", output_to_operand_aliasing={{0}: (5, {}), {1}: (6, {})} | custom-call | flops 1073741824 | bytes 8388608 | tf_op jit(solution)/shard_map/finish_other/pallas_call | solution.py:60
  (1 shorter events, 0.0 us)
Async XLA Ops:
  0.6 26.0 %collective-permute-start = (bf16[1024,512]{1,0:T(8,128)(2,1)}, bf16[1024,512]{1,0:T(8,128)(2,1)S(1)}, u32[]{:S(2)}, u32[]{:S(2)}) collective-permute-start(bf16[1024,512]{1,0:T(8,128)(2,1)} %own_ref.1), channel_id=1, source_target_pairs={{0,1},{1,2},{2,3},{3,0},{4,5},{5,6},{6,7},{7,4},{8,9},{9,10},{10,1... | collective-permute-start | bytes 3145736 | tf_op jit(solution)/shard_map/ppermute | solution.py:557
  2.7 25.1 %collective-permute-start.1 = (bf16[1024,512]{1,0:T(8,128)(2,1)}, bf16[1024,512]{1,0:T(8,128)(2,1)S(1)}, u32[]{:S(2)}, u32[]{:S(2)}) collective-permute-start(bf16[1024,512]{1,0:T(8,128)(2,1)} %own_ref.1), channel_id=1, source_target_pairs={{0,3},{1,0},{2,1},{3,2},{4,7},{5,4},{6,5},{7,6},{8,11},{9,8},{10,9... | collective-permute-start | bytes 3145736 | tf_op jit(solution)/shard_map/ppermute | solution.py:558
  7.8 23.7 %all-to-all-start = ((bf16[32,96,128]{2,1,0:T(8,128)(2,1)}), bf16[32,96,128]{2,1,0:T(8,128)(2,1)S(1)}, u32[]{:S(2)}, u32[]{:S(2)}) async-start(bf16[32,96,128]{2,1,0:T(8,128)(2,1)} %get-tuple-element.20), calls=%async_computation | async-start | bytes 1572864 | tf_op jit(solution)/shard_map/all_to_all | solution.py:580
  27.5 27.3 %collective-permute-start.2 = (bf16[512,512]{1,0:T(8,128)(2,1)}, bf16[512,512]{1,0:T(8,128)(2,1)S(1)}, u32[]{:S(2)}, u32[]{:S(2)}) collective-permute-start(bf16[512,512]{1,0:T(8,128)(2,1)} %slice.8), channel_id=1, source_target_pairs={{0,1},{1,2},{2,3},{3,0},{4,5},{5,6},{6,7},{7,4},{8,9},{9,10},{10,1... | collective-permute-start | bytes 1572872 | tf_op jit(solution)/shard_map/ppermute | solution.py:560
  28.7 26.1 %collective-permute-start.3 = (bf16[512,512]{1,0:T(8,128)(2,1)}, bf16[512,512]{1,0:T(8,128)(2,1)}, u32[]{:S(2)}, u32[]{:S(2)}) collective-permute-start(bf16[512,512]{1,0:T(8,128)(2,1)} %slice.9), channel_id=1, source_target_pairs={{0,3},{1,0},{2,1},{3,2},{4,7},{5,4},{6,5},{7,6},{8,11},{9,8},{10,9... | collective-permute-start | bytes 1572872 | tf_op jit(solution)/shard_map/ppermute | solution.py:560
  33.1 21.6 %all-to-all-start.1 = ((bf16[32,64,128]{2,1,0:T(8,128)(2,1)}), bf16[32,64,128]{2,1,0:T(8,128)(2,1)S(1)}, u32[]{:S(2)}, u32[]{:S(2)}) async-start(bf16[32,64,128]{2,1,0:T(8,128)(2,1)} %get-tuple-element.26), calls=%async_computation.1 | async-start | bytes 1048576 | tf_op jit(solution)/shard_map/all_to_all | solution.py:581
  76.5 2.1 %collective-permute-start.4 = (bf16[16,128,128]{2,1,0:T(8,128)(2,1)S(1)}, bf16[16,128,128]{2,1,0:T(8,128)(2,1)S(1)}, u32[]{:S(2)}, u32[]{:S(2)}) collective-permute-start(bf16[16,128,128]{2,1,0:T(8,128)(2,1)S(1)} %get-tuple-element.31), channel_id=1, source_target_pairs={{0,4},{4,0},{1,5},{5,1},{2,6},{6,2},{3,7},{7,3},{8,12},{12,8},{9,1... | collective-permute-start | bytes 1572872 | tf_op jit(solution)/shard_map/ppermute | solution.py:586
  78.6 31.1 %copy-start = (bf16[16,128,128]{2,1,0:T(8,128)(2,1)S(1)}, bf16[16,128,128]{2,1,0:T(8,128)(2,1)}, u32[]{:S(2)}) copy-start(bf16[16,128,128]{2,1,0:T(8,128)(2,1)} %get-tuple-element.30.kept_ref) | copy-start | bytes 1572868
  96.1 13.6 %all-to-all-start.3 = ((bf16[16,128,128]{2,1,0:T(8,128)(2,1)}), bf16[16,128,128]{2,1,0:T(8,128)(2,1)S(1)}, u32[]{:S(2)}, u32[]{:S(2)}) async-start(bf16[16,128,128]{2,1,0:T(8,128)(2,1)} %suffix_scan.1), calls=%async_computation.3 | async-start | bytes 1048576 | tf_op jit(solution)/shard_map/all_to_all | solution.py:588
  110.0 5.5 %collective-permute-start.5 = (bf16[16,128,128]{2,1,0:T(8,128)(2,1)S(1)}, bf16[16,128,128]{2,1,0:T(8,128)(2,1)S(1)}, u32[]{:S(2)}, u32[]{:S(2)}) collective-permute-start(bf16[16,128,128]{2,1,0:T(8,128)(2,1)S(1)} %add_convert_fusion), channel_id=1, source_target_pairs={{0,4},{4,0},{1,5},{5,1},{2,6},{6,2},{3,7},{7,3},{8,12},{12,8},{9,1... | collective-permute-start | bytes 1572872 | tf_op jit(solution)/shard_map/ppermute | solution.py:591

commit v11 on v9

--- a/solution.py
+++ b/solution.py
@@ -413,20 +413,20 @@
             mine = first[:entries] + last[:entries] + dot(hot[b], key_grad[b])
             code = mine if b == 0 else code + mine
 
-    def write(ref, first):
+    def write(ref):
         for k in range(entries // HALF):
             rows = slice(k * HALF, (k + 1) * HALF)
-            at = first + k
+            at = lax.rem(step, 2) * (entries // HALF) + k
             ref[at, :HALF, :] = part[rows].astype(BF16)
             ref[at, HALF:, :] = code[rows].astype(BF16)
 
     @pl.when(step < 2)
     def _():
-        write(give_ref, lax.rem(step, 2) * (entries // HALF))
+        write(give_ref)
 
     @pl.when(step >= 2)
     def _():
-        write(keep_ref, 0)
+        write(keep_ref)
 
 
 def backward(me, core, pieces, weight, codes, queries, values, probs, keys, book_t, prefix, counts,
@@ -440,13 +440,13 @@
     by_head = lambda s, _, core: (at(s, core), 0, 0)
     in_blocks = lambda s, _, core: (0, at(s, core), 0, 0)
     rows_of = pl.BlockSpec((tokens, width), lambda s, _, core: (0, at(s, core)))
-    shape = (slices, 2 * HALF, width)
     both_heads = (2 * slices, 2 * HALF, width)
     per_head = pl.BlockSpec((1, entries, width), by_head)
 
     anywhere = pl.BlockSpec(memory_space=pl.ANY)
     whole = lambda s, *_: (0, 0)
-    in_specs = [pl.BlockSpec(pieces[0].shape, whole)] + [IN_VMEM] * (len(pieces) - 1)
+    in_specs = [pl.BlockSpec(pieces[0].shape, whole), IN_VMEM, IN_VMEM]
+    in_specs += [pl.BlockSpec(piece.shape, whole) for piece in pieces[3:]]
     in_specs.append(pl.BlockSpec(weight.shape, whole))
     in_specs += [
         pl.BlockSpec(codes.shape, lambda h, *_: (0, 0)),
@@ -464,7 +464,7 @@
         (queries.shape, F32, rows_of),
         ((heads, entries, width), F32, per_head),
         (both_heads, BF16, IN_VMEM),
-        (both_heads, BF16, pl.BlockSpec(shape, lambda s, *_: (jnp.maximum(s - 2, 0), 0, 0))),
+        (both_heads, BF16, IN_VMEM),
     ]
     return call(
         backward_kernel, "backward", (heads,), in_specs, outs,

time: 119 us -> 118 us (level)
  no operation moved by 1% of the time
where the time goes in v11:
time: 118 us
  Pallas kernels  43.8 us (37%)
  starting transfers between devices  32 us (27%)
  waiting for transfers between devices  23.5 us (20%)
  blocking collectives  15.4 us (13%)
  local copies, waits for them, and re-layouts  1.92 us (2%)
    pallas_call x7, Pallas kernels, with_places(): return run(*args[:prefetch], *arrays)  43.8 us
    all_to_all x1, blocking collectives, per_device(): later = between_chips(suffix_scan(between_chips(chip)))  15.4 us
    all_to_all x1, waiting for transfers between devices, per_device(): later = between_chips(suffix_scan(between_chips(chip)))  9.97 us
    all_to_all x1, starting transfers between devices, per_device(): prefix = exchange(prefix)  9.62 us
    all_to_all x1, starting transfers between devices, per_device(): prefix, counts = prefix_scan(me_seq, exchange(send), first_count)  9.45 us
    ppermute x1, waiting for transfers between devices, ring_pieces(): left = lax.ppermute(array, 'head', up)  9.39 us
    all_to_all x1, starting transfers between devices, per_device(): later = between_chips(suffix_scan(between_chips(chip)))  3.57 us
    ppermute x1, starting transfers between devices, per_device(): theirs = other_core((later.astype(F32) + mine).astype(BF16))  2.59 us
  transfers between devices with their start and end apart: 9, of which 5 were waited for; matrix products, arithmetic and copies ran while one was open for 1% of the time, Pallas kernels for 15%

profile of v11, /device:TPU:1, one launch (start us, length us, event | category | flops | bytes accessed | tf_op | source)
XLA Modules:
  0.0 117.8 jit_solution(10899776731671546582)
XLA Ops:
  0.6 2.1 %collective-permute-start = (bf16[1024,512]{1,0:T(8,128)(2,1)}, bf16[1024,512]{1,0:T(8,128)(2,1)S(1)}, u32[]{:S(2)}, u32[]{:S(2)}) collective-permute-start(bf16[1024,512]{1,0:T(8,128)(2,1)} %own_ref.1), channel_id=1, source_target_pairs={{0,1},{1,2},{2,3},{3,0},{4,5},{5,6},{6,7},{7,4},{8,9},{9,10},{10,1... | collective-permute-start | bytes 3145736 | tf_op jit(solution)/shard_map/ppermute | solution.py:546
  2.7 1.4 %collective-permute-start.1 = (bf16[1024,512]{1,0:T(8,128)(2,1)}, bf16[1024,512]{1,0:T(8,128)(2,1)}, u32[]{:S(2)}, u32[]{:S(2)}) collective-permute-start(bf16[1024,512]{1,0:T(8,128)(2,1)} %own_ref.1), channel_id=1, source_target_pairs={{0,3},{1,0},{2,1},{3,2},{4,7},{5,4},{6,5},{7,6},{8,11},{9,8},{10,9... | collective-permute-start | bytes 3145736 | tf_op jit(solution)/shard_map/ppermute | solution.py:547
  4.1 3.7 %own_sums.1 = (bf16[32,96,128]{2,1,0:T(8,128)(2,1)}, f32[4,512,128]{2,1,0:T(8,128)}, f32[4,1,512]{2,1,0:T(1,128)}) custom-call(s32[4,1024]{1,0:T(4,128)} %bitcast.4, bf16[1024,512]{1,0:T(8,128)(2,1)} %value_ref.3), custom_call_target="tpu_custom_call" | custom-call | tf_op jit(solution)/shard_map/own_sums/pallas_call | solution.py:60
  7.8 9.4 %all-to-all-start = ((bf16[32,96,128]{2,1,0:T(8,128)(2,1)}), bf16[32,96,128]{2,1,0:T(8,128)(2,1)S(1)}, u32[]{:S(2)}, u32[]{:S(2)}) async-start(bf16[32,96,128]{2,1,0:T(8,128)(2,1)} %get-tuple-element.20), calls=%async_computation | async-start | bytes 1572864 | tf_op jit(solution)/shard_map/all_to_all | solution.py:569
  17.3 9.4 %collective-permute-done.left_ref = bf16[1024,512]{1,0:T(8,128)(2,1)S(1)} collective-permute-done((bf16[1024,512]{1,0:T(8,128)(2,1)}, bf16[1024,512]{1,0:T(8,128)(2,1)S(1)}, u32[]{:S(2)}, u32[]{:S(2)}) %collective-permute-start) | collective-permute-done | bytes 1048608 | tf_op jit(solution)/shard_map/ppermute | solution.py:546
  26.7 0.5 collective-permute-start.2
  27.2 0.0 collective-permute-done.1.right_ref
  27.2 1.1 slice.9
  28.3 2.3 %collective-permute-start.3 = (bf16[512,512]{1,0:T(8,128)(2,1)S(1)}, bf16[512,512]{1,0:T(8,128)(2,1)}, u32[]{:S(2)}, u32[]{:S(2)}) collective-permute-start(bf16[512,512]{1,0:T(8,128)(2,1)S(1)} %slice.9), channel_id=1, source_target_pairs={{0,3},{1,0},{2,1},{3,2},{4,7},{5,4},{6,5},{7,6},{8,11},{9,8},{10,9... | collective-permute-start | bytes 1572872 | tf_op jit(solution)/shard_map/ppermute | solution.py:549
  30.6 0.9 all-to-all-done.in_ref
  31.5 1.6 %prefix_scan.1 = (bf16[32,64,128]{2,1,0:T(8,128)(2,1)}, f32[2,4,1,512]{3,2,1,0:T(1,128)}) custom-call(s32[1]{0:T(128)} %bitcast.3.me_ref, bf16[32,96,128]{2,1,0:T(8,128)(2,1)S(1)} %all-to-all-done.in_ref, f32[4,1,512]{2,1,0:T(1,128)} %get-tuple-element.21.first_ref), custom_call_target="tpu_custom_call" | custom-call | tf_op jit(solution)/shard_map/prefix_scan/pallas_call | solution.py:60
  33.1 9.6 %all-to-all-start.1 = ((bf16[32,64,128]{2,1,0:T(8,128)(2,1)}), bf16[32,64,128]{2,1,0:T(8,128)(2,1)S(1)}, u32[]{:S(2)}, u32[]{:S(2)}) async-start(bf16[32,64,128]{2,1,0:T(8,128)(2,1)} %get-tuple-element.26), calls=%async_computation.1 | async-start | bytes 1048576 | tf_op jit(solution)/shard_map/all_to_all | solution.py:570
  42.7 9.8 %forward.1 = (bf16[2,4,1024,512]{3,2,1,0:T(8,128)(2,1)}, bf16[2,4,128,512]{3,2,1,0:T(8,128)(2,1)}, bf16[4,128,512]{2,1,0:T(8,128)(2,1)}) custom-call(s32[4,1024]{1,0:T(4,128)} %bitcast.5, bf16[1024,512]{1,0:T(8,128)(2,1)} %query_ref.3, bf16[4,512,128]{2,1,0:T(8,128)(2,1)} %book_ref.1, f32[2,4,1,512]{3,2,1,0:T(1,128)} %get-tuple-element.22.count_ref), custom_call_target="tpu_custom_call" | custom-call | tf_op jit(solution)/shard_map/forward/pallas_call | solution.py:60
  52.5 1.7 %all-to-all-done.1.prefix_ref = bf16[32,64,128]{2,1,0:T(8,128)(2,1)S(1)} async-done(((bf16[32,64,128]{2,1,0:T(8,128)(2,1)}), bf16[32,64,128]{2,1,0:T(8,128)(2,1)S(1)}, u32[]{:S(2)}, u32[]{:S(2)}) %all-to-all-start.1) | async-done | bytes 524320 | tf_op jit(solution)/shard_map/all_to_all | solution.py:570
  54.3 0.0 collective-permute-done.2.far0_ref
  54.3 0.0 copy-start
  54.3 0.0 collective-permute-done.3.far1_ref
  54.3 0.8 copy-done
  55.1 22.0 %backward.1 = (bf16[1024,512]{1,0:T(8,128)(2,1)}, f32[1024,512]{1,0:T(8,128)}, f32[4,512,128]{2,1,0:T(8,128)}, bf16[16,128,128]{2,1,0:T(8,128)(2,1)S(1)}, bf16[16,128,128]{2,1,0:T(8,128)(2,1)S(1)}) custom-call(s32[1]{0:T(128)} %bitcast.me_ref, s32[1]{0:T(128)} %bitcast.1.core_ref.refs_0_, bf16[1024,512]{1,0:T(8,128)(2,1)} %own_ref.1, ...), custom_call_target="tpu_custom_call" | custom-call | flops 21474836480 | bytes 25165824 | tf_op jit(solution)/shard_map/backward/pallas_call | solution.py:60
  77.1 0.5 collective-permute-start.4
  77.6 1.5 %collective-permute-done.4.refs_4_ = bf16[16,128,128]{2,1,0:T(8,128)(2,1)S(1)} collective-permute-done((bf16[16,128,128]{2,1,0:T(8,128)(2,1)S(1)}, bf16[16,128,128]{2,1,0:T(8,128)(2,1)S(1)}, u32[]{:S(2)}, u32[]{:S(2)}) %collective-permute-start.4) | collective-permute-done | bytes 524320 | tf_op jit(solution)/shard_map/ppermute | solution.py:575
  79.1 0.1 fusion
  79.3 15.4 %all_to_all.20.in_ref = bf16[16,128,128]{2,1,0:T(8,128)(2,1)S(1)} all-to-all(bf16[16,128,128]{2,1,0:T(8,128)(2,1)S(1)} %fusion), channel_id=1, replica_groups=mesh['chip'=16,'core'=2,'head'=4] {'chip'}, dimensions={0} | all-to-all | bytes 1048576 | tf_op jit(solution)/shard_map/all_to_all | solution.py:577
  94.7 0.9 suffix_scan.1
  95.6 3.6 %all-to-all-start.3 = ((bf16[16,128,128]{2,1,0:T(8,128)(2,1)}), bf16[16,128,128]{2,1,0:T(8,128)(2,1)S(1)}, u32[]{:S(2)}, u32[]{:S(2)}) async-start(bf16[16,128,128]{2,1,0:T(8,128)(2,1)} %suffix_scan.1), calls=%async_computation.3 | async-start | bytes 1048576 | tf_op jit(solution)/shard_map/all_to_all | solution.py:577
  99.2 10.0 %all-to-all-done.3.refs_3_ = bf16[16,128,128]{2,1,0:T(8,128)(2,1)S(1)} async-done(((bf16[16,128,128]{2,1,0:T(8,128)(2,1)}), bf16[16,128,128]{2,1,0:T(8,128)(2,1)S(1)}, u32[]{:S(2)}, u32[]{:S(2)}) %all-to-all-start.3) | async-done | bytes 524320 | tf_op jit(solution)/shard_map/all_to_all | solution.py:577
  109.2 0.2 fusion.2
  109.4 2.6 %collective-permute-start.5 = (bf16[16,128,128]{2,1,0:T(8,128)(2,1)S(1)}, bf16[16,128,128]{2,1,0:T(8,128)(2,1)S(1)}, u32[]{:S(2)}, u32[]{:S(2)}) collective-permute-start(bf16[16,128,128]{2,1,0:T(8,128)(2,1)S(1)} %fusion.2), channel_id=1, source_target_pairs={{0,4},{4,0},{1,5},{5,1},{2,6},{6,2},{3,7},{7,3},{8,12},{12,8},{9,1... | collective-permute-start | bytes 1572872 | tf_op jit(solution)/shard_map/ppermute | solution.py:580
  112.0 2.9 %finish_own.1 = (bf16[1024,512]{1,0:T(8,128)(2,1)}, f32[4,512,128]{2,1,0:T(8,128)}) custom-call(s32[1]{0:T(128)} %bitcast.1.core_ref.refs_0_, s32[4,1024]{1,0:T(4,128)} %bitcast.7, f32[1024,512]{1,0:T(8,128)} %get-tuple-element.29.refs_2_, bf16[16,128,128]{2,1,0:T(8,128)(2,1)S(1)} %all-to-all-done.3.refs_3_, ...), custom_call_target="tpu_custom_call" | custom-call | flops 1073741824 | bytes 8388608 | tf_op jit(solution)/shard_map/finish_own/pallas_call | solution.py:60
  114.9 0.0 collective-permute-done.5.refs_3_
  114.9 2.9 %finish_other.1 = (bf16[1024,512]{1,0:T(8,128)(2,1)}, f32[4,512,128]{2,1,0:T(8,128)}) custom-call(s32[1]{0:T(128)} %bitcast.1.core_ref.refs_0_, s32[4,1024]{1,0:T(4,128)} %bitcast.8, f32[1024,512]{1,0:T(8,128)} %get-tuple-element.29.refs_2_, bf16[16,128,128]{2,1,0:T(8,128)(2,1)S(1)} %collective-permute-done.5.refs_3_, ...), custom_call_target="tpu_custom_call", output_to_operand_aliasing={{0}: (5, {}), {1}: (6, {})} | custom-call | flops 1073741824 | bytes 8388608 | tf_op jit(solution)/shard_map/finish_other/pallas_call | solution.py:60
  (2 shorter events, 0.0 us)
Async XLA Ops:
  0.6 26.0 %collective-permute-start = (bf16[1024,512]{1,0:T(8,128)(2,1)}, bf16[1024,512]{1,0:T(8,128)(2,1)S(1)}, u32[]{:S(2)}, u32[]{:S(2)}) collective-permute-start(bf16[1024,512]{1,0:T(8,128)(2,1)} %own_ref.1), channel_id=1, source_target_pairs={{0,1},{1,2},{2,3},{3,0},{4,5},{5,6},{6,7},{7,4},{8,9},{9,10},{10,1... | collective-permute-start | bytes 3145736 | tf_op jit(solution)/shard_map/ppermute | solution.py:546
  2.7 24.5 %collective-permute-start.1 = (bf16[1024,512]{1,0:T(8,128)(2,1)}, bf16[1024,512]{1,0:T(8,128)(2,1)}, u32[]{:S(2)}, u32[]{:S(2)}) collective-permute-start(bf16[1024,512]{1,0:T(8,128)(2,1)} %own_ref.1), channel_id=1, source_target_pairs={{0,3},{1,0},{2,1},{3,2},{4,7},{5,4},{6,5},{7,6},{8,11},{9,8},{10,9... | collective-permute-start | bytes 3145736 | tf_op jit(solution)/shard_map/ppermute | solution.py:547
  7.8 23.7 %all-to-all-start = ((bf16[32,96,128]{2,1,0:T(8,128)(2,1)}), bf16[32,96,128]{2,1,0:T(8,128)(2,1)S(1)}, u32[]{:S(2)}, u32[]{:S(2)}) async-start(bf16[32,96,128]{2,1,0:T(8,128)(2,1)} %get-tuple-element.20), calls=%async_computation | async-start | bytes 1572864 | tf_op jit(solution)/shard_map/all_to_all | solution.py:569
  26.7 27.6 %collective-permute-start.2 = (bf16[512,512]{1,0:T(8,128)(2,1)S(1)}, bf16[512,512]{1,0:T(8,128)(2,1)S(1)}, u32[]{:S(2)}, u32[]{:S(2)}) collective-permute-start(bf16[512,512]{1,0:T(8,128)(2,1)S(1)} %slice.8), channel_id=1, source_target_pairs={{0,1},{1,2},{2,3},{3,0},{4,5},{5,6},{6,7},{7,4},{8,9},{9,10},{10,1... | collective-permute-start | bytes 1572872 | tf_op jit(solution)/shard_map/ppermute | solution.py:549
  28.3 26.0 %collective-permute-start.3 = (bf16[512,512]{1,0:T(8,128)(2,1)S(1)}, bf16[512,512]{1,0:T(8,128)(2,1)}, u32[]{:S(2)}, u32[]{:S(2)}) collective-permute-start(bf16[512,512]{1,0:T(8,128)(2,1)S(1)} %slice.9), channel_id=1, source_target_pairs={{0,3},{1,0},{2,1},{3,2},{4,7},{5,4},{6,5},{7,6},{8,11},{9,8},{10,9... | collective-permute-start | bytes 1572872 | tf_op jit(solution)/shard_map/ppermute | solution.py:549
  33.1 21.2 %all-to-all-start.1 = ((bf16[32,64,128]{2,1,0:T(8,128)(2,1)}), bf16[32,64,128]{2,1,0:T(8,128)(2,1)S(1)}, u32[]{:S(2)}, u32[]{:S(2)}) async-start(bf16[32,64,128]{2,1,0:T(8,128)(2,1)} %get-tuple-element.26), calls=%async_computation.1 | async-start | bytes 1048576 | tf_op jit(solution)/shard_map/all_to_all | solution.py:570
  54.3 0.8 copy-start
  77.1 2.1 %collective-permute-start.4 = (bf16[16,128,128]{2,1,0:T(8,128)(2,1)S(1)}, bf16[16,128,128]{2,1,0:T(8,128)(2,1)S(1)}, u32[]{:S(2)}, u32[]{:S(2)}) collective-permute-start(bf16[16,128,128]{2,1,0:T(8,128)(2,1)S(1)} %get-tuple-element.31), channel_id=1, source_target_pairs={{0,4},{4,0},{1,5},{5,1},{2,6},{6,2},{3,7},{7,3},{8,12},{12,8},{9,1... | collective-permute-start | bytes 1572872 | tf_op jit(solution)/shard_map/ppermute | solution.py:575
  95.6 13.6 %all-to-all-start.3 = ((bf16[16,128,128]{2,1,0:T(8,128)(2,1)}), bf16[16,128,128]{2,1,0:T(8,128)(2,1)S(1)}, u32[]{:S(2)}, u32[]{:S(2)}) async-start(bf16[16,128,128]{2,1,0:T(8,128)(2,1)} %suffix_scan.1), calls=%async_computation.3 | async-start | bytes 1048576 | tf_op jit(solution)/shard_map/all_to_all | solution.py:577
  109.4 5.5 %collective-permute-start.5 = (bf16[16,128,128]{2,1,0:T(8,128)(2,1)S(1)}, bf16[16,128,128]{2,1,0:T(8,128)(2,1)S(1)}, u32[]{:S(2)}, u32[]{:S(2)}) collective-permute-start(bf16[16,128,128]{2,1,0:T(8,128)(2,1)S(1)} %fusion.2), channel_id=1, source_target_pairs={{0,4},{4,0},{1,5},{5,1},{2,6},{6,2},{3,7},{7,3},{8,12},{12,8},{9,1... | collective-permute-start | bytes 1572872 | tf_op jit(solution)/shard_map/ppermute | solution.py:580
